TPU v7x, 128 devices: a whole 4x4x4 slice. The times are simulated.
128 devices in a mesh: ctx: 32 (over x, z, core), head: 4 (over y).
Axes of the slice: x: 4, y: 4, z: 4, core: 2. Of those that a mesh axis runs over, the one named last changes fastest.
Arguments:
- queries: bfloat16 [32768, 4, 4, 128], P('ctx', None, 'head'), may hold values from -4.5 to 4.5
- key_rows: bfloat16 [32768, 4, 128], P('ctx'), may hold values from -3 to 3
- value_rows: bfloat16 [32768, 4, 128], P('ctx'), may hold values from -6 to 6
- out_grad: bfloat16 [32768, 4, 4, 128], P('ctx', None, 'head'), may hold values from -18 to 18
- outputs: bfloat16 [32768, 4, 4, 128], P('ctx', None, 'head'), may hold values from -6 to 6
- logsumexp: float32 [4, 4, 32768], P(None, 'head', 'ctx')
- selections: int32 [256, 3], P('ctx'), may hold values from 0 to 31, as said below
Outputs:
- grad_queries: bfloat16 [32768, 4, 4, 128], P('ctx', None, 'head')
- grad_keys: bfloat16 [32768, 4, 128], P('ctx', 'head')
- grad_values: bfloat16 [32768, 4, 128], P('ctx', 'head')
Inputs may be any that keep to these rules, and one draw needn't show every extreme that they name: `selections`: column 0 of row b is the query block's own key block b // 8; columns 1 and 2 each name an earlier key block or repeat the own block, and two earlier blocks in one row differ. The query blocks of one key block never name the same earlier block twice. For every key block after the first, exactly one of its query blocks names key block 0.
All inputs are finite; a program needn't handle non-finite values.
Results may differ from a plain program's by a relative error of at most 0.005.
Values may be sent and summed in bfloat16 or wider, within the bound.
No kernel may reach another device: no remote copies, remote signals or barrier semaphores. Data moves between devices by JAX's collectives and lax.ppermute only.
A program may use at most 128 MiB of HBM per device.

v0:
```python
import jax
import jax.numpy as jnp
from jax import lax
from jax.sharding import PartitionSpec as P

QB = 128


def slot_grads(
    query_part, grad_part, lse_part, delta_part, weight, key_part, value_part, causal, scale
):
    scores = (
        jnp.einsum("srkgd,ckd->skgrc", query_part, key_part, preferred_element_type=jnp.float32)
        * scale
    )
    live = weight[:, None, None, None, None] > 0
    if causal is not None:
        live = live & causal
    prob = jnp.where(live, jnp.exp(scores - lse_part[..., None]), 0.0)
    dprob = jnp.einsum(
        "srkgd,ckd->skgrc", grad_part, value_part, preferred_element_type=jnp.float32
    )
    dscore = prob * (dprob - delta_part[..., None])
    prob_low = prob.astype(jnp.bfloat16)
    dscore_low = dscore.astype(jnp.bfloat16)
    grad_q = (
        jnp.einsum("skgrc,ckd->srkgd", dscore_low, key_part, preferred_element_type=jnp.float32)
        * scale
    )
    grad_k = (
        jnp.einsum("skgrc,srkgd->ckd", dscore_low, query_part, preferred_element_type=jnp.float32)
        * scale
    )
    grad_v = jnp.einsum("skgrc,srkgd->ckd", prob_low, grad_part, preferred_element_type=jnp.float32)
    return (grad_q, grad_k, grad_v)


def body(queries, key_rows, value_rows, out_grad, outputs, logsumexp, selections):
    row_count, kv_heads, local_heads, head_dim = queries.shape
    width = local_heads * head_dim
    block_count = row_count // QB
    peers = lax.axis_size("ctx")
    device = lax.axis_index("ctx")
    scale = head_dim ** (-0.5)
    delta_local = jnp.transpose(
        jnp.sum(out_grad.astype(jnp.float32) * outputs.astype(jnp.float32), axis=-1), (1, 2, 0)
    )
    causal = jnp.arange(row_count)[:, None] >= jnp.arange(row_count)[None, :]
    own_q, grad_k, grad_v = slot_grads(
        queries[None],
        out_grad[None],
        logsumexp[None],
        delta_local[None],
        jnp.ones((1,), jnp.float32),
        key_rows,
        value_rows,
        causal,
        scale,
    )
    grad_total = own_q.reshape(block_count, QB, kv_heads, width)
    block_ids = jnp.arange(block_count, dtype=jnp.int32)
    peer_ids = jnp.arange(peers, dtype=jnp.int32)
    remote = selections[:, 1:]
    match = jnp.any(remote[:, :, None] == peer_ids[None, None, :], axis=1) & (
        peer_ids[None, :] != device
    )
    lse_blocks = logsumexp.reshape(kv_heads, local_heads, block_count, QB)
    delta_blocks = delta_local.reshape(kv_heads, local_heads, block_count, QB)
    match_f = match.astype(jnp.float32)
    flag_send = jnp.sum(match_f, axis=0)
    source = jnp.sum(jnp.where(match, block_ids[:, None], 0), axis=0)
    send_q = jnp.take(queries.reshape(block_count, QB, kv_heads, width), source, axis=0)
    send_g = jnp.take(out_grad.reshape(block_count, QB, kv_heads, width), source, axis=0)
    send_lse = jnp.transpose(jnp.take(lse_blocks, source, axis=2), (2, 0, 1, 3))
    send_delta = jnp.transpose(jnp.take(delta_blocks, source, axis=2), (2, 0, 1, 3))
    recv_lse, recv_delta, recv_flag = (
        lax.all_to_all(send_lse, "ctx", split_axis=0, concat_axis=0, tiled=True),
        lax.all_to_all(send_delta, "ctx", split_axis=0, concat_axis=0, tiled=True),
        lax.all_to_all(flag_send, "ctx", split_axis=0, concat_axis=0, tiled=True),
    )
    recv_q, recv_g = (
        lax.all_to_all(send_q, "ctx", split_axis=0, concat_axis=0, tiled=True),
        lax.all_to_all(send_g, "ctx", split_axis=0, concat_axis=0, tiled=True),
    )
    ordering = jnp.argsort((recv_flag <= 0).astype(jnp.int32) * peers + peer_ids)
    sorted_q = jnp.take(recv_q, ordering, axis=0).reshape(
        peers, QB, kv_heads, local_heads, head_dim
    )
    sorted_g = jnp.take(recv_g, ordering, axis=0).reshape(
        peers, QB, kv_heads, local_heads, head_dim
    )
    sorted_lse = jnp.take(recv_lse, ordering, axis=0)
    sorted_delta = jnp.take(recv_delta, ordering, axis=0)
    sorted_flag = jnp.take(recv_flag, ordering, axis=0)
    group_size = 4
    empty_q = jnp.zeros((group_size, QB, kv_heads, local_heads, head_dim), jnp.float32)

    def group_step(group_turn, carry):
        dq_slots, acc_k, acc_v = carry
        start = group_turn * group_size
        part_flag = lax.dynamic_slice_in_dim(sorted_flag, start, group_size, 0)
        part_q = lax.dynamic_slice_in_dim(sorted_q, start, group_size, 0)
        part_g = lax.dynamic_slice_in_dim(sorted_g, start, group_size, 0)
        part_lse = lax.dynamic_slice_in_dim(sorted_lse, start, group_size, 0)
        part_delta = lax.dynamic_slice_in_dim(sorted_delta, start, group_size, 0)

        def active(unused):
            return slot_grads(
                part_q, part_g, part_lse, part_delta, part_flag, key_rows, value_rows, None, scale
            )

        def skipped(unused):
            return (empty_q, jnp.zeros_like(acc_k), jnp.zeros_like(acc_v))

        group_q, group_k, group_v = lax.cond(jnp.sum(part_flag) > 0, active, skipped, None)
        dq_slots = lax.dynamic_update_slice_in_dim(dq_slots, group_q, start, 0)
        return (dq_slots, acc_k + group_k, acc_v + group_v)

    dq_init = jnp.zeros((peers, QB, kv_heads, local_heads, head_dim), jnp.float32)
    dq_sorted, grad_k, grad_v = lax.fori_loop(
        0, peers // group_size, group_step, (dq_init, grad_k, grad_v)
    )
    restore = jnp.argsort(ordering)
    dq_back = jnp.take(dq_sorted, restore, axis=0).reshape(peers, QB, kv_heads, width)
    returned = lax.all_to_all(dq_back, "ctx", split_axis=0, concat_axis=0, tiled=True)
    grad_total = grad_total + jnp.einsum(
        "ip,pqke->iqke", match_f, returned, precision=lax.Precision.HIGHEST
    )
    shard_k, shard_v = (
        lax.psum_scatter(grad_k, "head", scatter_dimension=1, tiled=True),
        lax.psum_scatter(grad_v, "head", scatter_dimension=1, tiled=True),
    )
    grad_queries = grad_total.reshape(row_count, kv_heads, local_heads, head_dim).astype(
        jnp.bfloat16
    )
    return (grad_queries, shard_k.astype(jnp.bfloat16), shard_v.astype(jnp.bfloat16))


def solution(mesh):
    in_specs = (
        P("ctx", None, "head", None),
        P("ctx", None, None),
        P("ctx", None, None),
        P("ctx", None, "head", None),
        P("ctx", None, "head", None),
        P(None, "head", "ctx"),
        P("ctx", None),
    )
    out_specs = (P("ctx", None, "head", None), P("ctx", "head", None), P("ctx", "head", None))
    return jax.shard_map(body, mesh=mesh, in_specs=in_specs, out_specs=out_specs, check_vma=False)
```

profile of v0, /device:TPU:44, one launch (start us, length us, event | category | flops | bytes accessed | tf_op | source)
XLA Modules:
  0.0 551.3 jit_solution(10982267685444432818)
XLA Ops:
  8.8 8.0 %all-to-all-start = ((f32[32,1,1]{2,1,0:T(1,128)}), f32[32,1,1]{2,1,0:T(1,128)S(1)}, u32[]{:S(2)}, u32[]{:S(2)}) async-start(f32[32,1,1]{2,1,0:T(1,128)} %copy.171), calls=%async_computation | async-start | bytes 32768 | tf_op jit(solution)/shard_map/all_to_all | solution.py:79
  22.5 7.4 %all-to-all-start.4 = ((f32[32,4,1,128]{3,1,2,0:T(4,128)}), f32[32,4,1,128]{3,1,2,0:T(4,128)S(1)}, u32[]{:S(2)}, u32[]{:S(2)}) async-start(f32[32,4,1,128]{3,1,2,0:T(4,128)} %get-tuple-element.403), calls=%async_computation.4 | async-start | bytes 131072 | tf_op jit(solution)/shard_map/all_to_all | solution.py:78
  33.4 3.1 gather_fusion.2
  36.5 7.4 %all-to-all-start.2 = ((f32[32,4,1,128]{3,1,2,0:T(4,128)}), f32[32,4,1,128]{3,1,2,0:T(4,128)S(1)}, u32[]{:S(2)}, u32[]{:S(2)}) async-start(f32[32,4,1,128]{3,1,2,0:T(4,128)} %get-tuple-element.404), calls=%async_computation.2 | async-start | bytes 131072 | tf_op jit(solution)/shard_map/all_to_all | solution.py:77
  43.9 6.0 %broadcast_select_fusion.1 = (bf16[32,128,4,128]{3,1,2,0:T(8,128)(2,1)}, bf16[32,128,4,128]{3,1,2,0:T(8,128)(2,1)}) fusion(bf16[32,128,4,128]{3,1,2,0:T(8,128)(2,1)} %gather_fusion.6, pred[32]{0:T(512)(128)(4,1)S(1)} %compare_and_fusion, bf16[32,128,4,128]{3,1,2,0:T(8,128)(2,1)} %gather_fusion.2), kind=kLoop, calls=%fused_computation.71 | loop fusion | flops 4194304 | bytes 16777248 | tf_op jit(solution)/shard_map/jit(_take)/select_n | solution.py:73
  50.0 7.6 %all-to-all-start.3 = ((bf16[32,128,4,128]{3,1,2,0:T(8,128)(2,1)}), bf16[32,128,4,128]{3,1,2,0:T(8,128)(2,1)}, u32[]{:S(2)}, u32[]{:S(2)}) async-start(bf16[32,128,4,128]{3,1,2,0:T(8,128)(2,1)} %get-tuple-element.407), calls=%async_computation.3 | async-start | bytes 8388608 | tf_op jit(solution)/shard_map/all_to_all | solution.py:83
  59.1 8.1 %fusion.63 = f32[4,1024,1024]{2,1,0:T(8,128)} fusion(bf16[1024,4,128]{2,1,0:T(4,128)(2,1)S(1)} %bitcast.206, bf16[1024,4,128]{2,1,0:T(4,128)(2,1)S(1)} %copy-done.2), kind=kOutput, calls=%fused_computation.82 | convolution fusion | flops 1073741824 | bytes 18874368 | tf_op jit(solution)/shard_map/srkgd,ckd->skgrc/dot_general | solution.py:13
  67.1 40.6 %all-to-all-done.3 = bf16[32,128,4,128]{3,1,2,0:T(8,128)(2,1)} async-done(((bf16[32,128,4,128]{3,1,2,0:T(8,128)(2,1)}), bf16[32,128,4,128]{3,1,2,0:T(8,128)(2,1)}, u32[]{:S(2)}, u32[]{:S(2)}) %all-to-all-start.3) | async-done | bytes 4194336 | tf_op jit(solution)/shard_map/all_to_all | solution.py:83
  107.8 9.0 %all-to-all-start.1 = ((bf16[32,128,4,128]{3,1,2,0:T(8,128)(2,1)}), bf16[32,128,4,128]{3,1,2,0:T(8,128)(2,1)}, u32[]{:S(2)}, u32[]{:S(2)}) async-start(bf16[32,128,4,128]{3,1,2,0:T(8,128)(2,1)} %get-tuple-element.408), calls=%async_computation.1 | async-start | bytes 8388608 | tf_op jit(solution)/shard_map/all_to_all | solution.py:82
  117.3 11.8 %fusion.36 = bf16[1,4,1,1024,1024]{3,4,1,2,0:T(8,128)(2,1)} fusion(f32[4,1024,1024]{2,1,0:T(8,128)} %fusion.63, f32[4,1024]{1,0:T(4,128)S(1)} %copy.168, f32[4,1024]{1,0:T(4,128)S(1)} %bitcast.218, pred[1024,1024]{0,1:T(8,128)(4,1)} %iota_compare_fusion, bf16[1024,4,128]{2,1,0:T(4,128)(2,1)} %bitcast.208, bf16[1024,4,128]{2,1,0:T(4,128)(2,1)} %param.21), kind=kOutput, calls=%fused_computation.52 | convolution fusion | flops 1098907648 | bytes 28344320 | tf_op jit(solution)/shard_map/srkgd,ckd->skgrc/dot_general | solution.py:20
  131.4 7.1 %multiply_bitcast_fusion = f32[1024,4,128]{2,0,1:T(8,128)} fusion(bf16[1,4,1,1024,1024]{3,4,1,2,0:T(8,128)(2,1)} %fusion.36, bf16[1024,4,128]{2,1,0:T(4,128)(2,1)S(1)} %bitcast.207), kind=kOutput, calls=%fused_computation.75 | convolution fusion | flops 1074266112 | bytes 11534336 | tf_op jit(solution)/shard_map/skgrc,srkgd->ckd/dot_general | solution.py:31
  138.5 10.4 %fusion.50 = f32[1024,4,128]{2,0,1:T(8,128)} fusion(f32[4,1024,1024]{2,1,0:T(8,128)} %fusion.63, f32[4,1024]{1,0:T(4,128)S(1)} %bitcast.219, pred[1024,1024]{0,1:T(8,128)(4,1)} %iota_compare_fusion, bf16[1024,4,128]{2,1,0:T(4,128)(2,1)S(1)} %bitcast.210), kind=kOutput, calls=%fused_computation.77 | convolution fusion | flops 1090519040 | bytes 20987904 | tf_op jit(solution)/shard_map/skgrc,srkgd->ckd/dot_general | solution.py:34
  154.6 5.2 gather_fusion.7
  159.8 7.2 %all-to-all-done.1 = bf16[32,128,4,128]{3,1,2,0:T(8,128)(2,1)} async-done(((bf16[32,128,4,128]{3,1,2,0:T(8,128)(2,1)}), bf16[32,128,4,128]{3,1,2,0:T(8,128)(2,1)}, u32[]{:S(2)}, u32[]{:S(2)}) %all-to-all-start.1) | async-done | bytes 4194336 | tf_op jit(solution)/shard_map/all_to_all | solution.py:82
  167.0 5.2 gather_fusion.3
  172.2 4.1 select_bitcast_fusion
  180.8 4.3 broadcast_in_dim.117.clone
  185.1 99.7 %while.17 = (s32[]{:T(128)}, f32[32,128,4,1,128]{4,1,2,0,3:T(8,128)}, f32[1024,4,128]{2,0,1:T(8,128)}, f32[1024,4,128]{2,0,1:T(8,128)}, f32[32]{0:T(128)S(1)}, /...) while((s32[]{:T(128)}, ...), condition=%wide.region_10.15_spmd, body=%wide.region_6.14_spmd.sunk | while | flops 2707161088 | bytes 71363504 | solution.py:120
  186.4 14.1 %conditional.2 = (f32[4,128,4,1,128]{4,1,0,2,3:T(8,128)S(1)}, f32[1024,4,128]{2,0,1:T(8,128)S(1)}, f32[1024,4,128]{2,0,1:T(8,128)S(1)}) conditional(s32[]{:T(128)} %convert_element_type.83, () %tuple.72, (f32[4]{0:T(128)S(1)}, bf16[32,128,4,1,128]{4,1,0,2,3:T(8,128)(2,1)}, s32[]{:T(128)}, bf16[1024,4,128]{2,0,1:T(8,128)(2,1)}, ...), branch_computations={%region_8.12_spmd, %region_9.13_spmd} | conditional | flops 2706112512 | bytes 56682608 | solution.py:115
  189.2 3.6 fusion.8
  196.8 3.7 fusion.14
  201.6 3.1 add.140
  204.7 3.1 add.141
  209.1 14.1 %conditional.2 = (f32[4,128,4,1,128]{4,1,0,2,3:T(8,128)S(1)}, f32[1024,4,128]{2,0,1:T(8,128)S(1)}, f32[1024,4,128]{2,0,1:T(8,128)S(1)}) conditional(s32[]{:T(128)} %convert_element_type.83, () %tuple.72, (f32[4]{0:T(128)S(1)}, bf16[32,128,4,1,128]{4,1,0,2,3:T(8,128)(2,1)}, s32[]{:T(128)}, bf16[1024,4,128]{2,0,1:T(8,128)(2,1)}, ...), branch_computations={%region_8.12_spmd, %region_9.13_spmd} | conditional | flops 2706112512 | bytes 56682608 | solution.py:115
  211.9 3.6 fusion.8
  219.5 3.7 fusion.14
  224.3 3.1 add.140
  227.4 3.1 add.141
  233.3 3.1 add.140
  236.4 3.1 add.141
  242.3 3.1 add.140
  245.4 3.1 add.141
  251.3 3.1 add.140
  254.4 3.1 add.141
  260.3 3.1 add.140
  263.4 3.1 add.141
  269.4 3.1 add.140
  272.5 3.1 add.141
  278.4 3.1 add.140
  281.5 3.1 add.141
  284.8 7.7 %gather_fusion.1 = f32[32,128,4,128]{3,1,2,0:T(8,128)} fusion(f32[32,128,4,128]{3,1,2,0:T(8,128)} %bitcast.202, s32[1024]{0:T(1024)S(1)} %pad_clamp_fusion), kind=kCustom, calls=%fused_computation.9 | custom fusion | bytes 16777344 | tf_op jit(solution)/shard_map/jit(_take)/gather | solution.py:124
  292.5 8.4 %broadcast_select_fusion = f32[32,128,4,128]{3,1,2,0:T(8,128)} fusion(f32[32,128,4,128]{3,1,2,0:T(8,128)} %gather_fusion.1, pred[32]{0:T(512)(128)(4,1)S(1)} %compare_and_fusion.2), kind=kLoop, calls=%fused_computation.69 | loop fusion | flops 2097152 | bytes 16777248 | tf_op jit(solution)/shard_map/jit(_take)/select_n | solution.py:124
  300.9 13.8 %copy.190 = f32[32,128,4,128]{3,2,1,0:T(4,128)} copy(f32[32,128,4,128]{3,1,2,0:T(8,128)} %broadcast_select_fusion) | data formatting | bytes 16777216 | tf_op jit(solution)/shard_map/jit(_take)/select_n | solution.py:124
  314.7 89.6 %all-to-all-start.5 = ((f32[32,128,4,128]{3,2,1,0:T(4,128)}), f32[32,128,4,128]{3,2,1,0:T(4,128)}, u32[]{:S(2)}, u32[]{:S(2)}) async-start(f32[32,128,4,128]{3,2,1,0:T(4,128)} %copy.190), calls=%async_computation.5 | async-start | bytes 16777216 | tf_op jit(solution)/shard_map/all_to_all | solution.py:125
  405.1 6.3 %fusion.55 = f32[4,1024,128]{2,1,0:T(8,128)S(1)} fusion(bf16[1,4,1,1024,1024]{3,4,1,2,0:T(8,128)(2,1)} %fusion.36, bf16[1024,4,128]{2,1,0:T(4,128)(2,1)S(1)} %copy-done.3), kind=kOutput, calls=%fused_computation.78 | convolution fusion | flops 1074266112 | bytes 11534336 | tf_op jit(solution)/shard_map/skgrc,ckd->srkgd/dot_general | solution.py:27
  413.2 24.0 %reduce-scatter.5.cloned.1.call-done = f32[1024,1,128]{2,0,1:T(8,128)} async-done(((f32[1024,4,128]{2,0,1:T(8,128)}), f32[1024,1,128]{2,0,1:T(8,128)}) %reduce-scatter.5.cloned.1.call-update) | async-done | bytes 524304 | tf_op jit(solution)/shard_map/reduce_scatter | solution.py:131
  439.0 91.2 %all-to-all-done.5 = f32[32,128,4,128]{3,2,1,0:T(4,128)} async-done(((f32[32,128,4,128]{3,2,1,0:T(4,128)}), f32[32,128,4,128]{3,2,1,0:T(4,128)}, u32[]{:S(2)}, u32[]{:S(2)}) %all-to-all-start.5) | async-done | bytes 8388640 | tf_op jit(solution)/shard_map/all_to_all | solution.py:125
  530.2 11.6 %fusion.49 = bf16[8,128,4,128]{3,0,2,1:T(8,128)(2,1)S(1)} fusion(f32[8,128,4,128]{3,1,0,2:T(8,128)S(1)} %bitcast.212, f32[32,128,4,128]{3,2,1,0:T(4,128)} %all-to-all-done.5, pred[8,32]{1,0:T(8,128)(4,1)S(1)} %copy-done.10, pred[32]{0:T(512)(128)(4,1)S(1)} %copy-done.12), kind=kOutput, calls=%fused_computation.74 | convolution fusion | flops 202375424 | bytes 11534624 | tf_op jit(solution)/shard_map/ip,pqke->iqke/dot_general | solution.py:126
  (135 shorter events, 63.7 us)
Async XLA Ops:
  7.2 22.7 %copy-start.4 = (bf16[1024,4,1,128]{3,1,2,0:T(4,128)(2,1)S(1)}, bf16[1024,4,1,128]{3,1,2,0:T(4,128)(2,1)}, u32[]{:S(2)}) copy-start(bf16[1024,4,1,128]{3,1,2,0:T(4,128)(2,1)} %param.22) | copy-start | bytes 3145732
  8.0 14.4 %copy-start.9 = (pred[8,32]{1,0:T(8,128)(4,1)}, pred[8,32]{1,0:T(8,128)(4,1)S(1)}, u32[]{:S(2)}) copy-start(pred[8,32]{1,0:T(8,128)(4,1)S(1)} %fusion.67) | copy-start | bytes 772
  8.0 14.4 %copy-start.11 = (pred[32]{0:T(512)(128)(4,1)}, pred[32]{0:T(512)(128)(4,1)S(1)}, u32[]{:S(2)}) copy-start(pred[32]{0:T(512)(128)(4,1)S(1)} %iota_compare_fusion.2) | copy-start | bytes 100
  8.8 13.7 %all-to-all-start = ((f32[32,1,1]{2,1,0:T(1,128)}), f32[32,1,1]{2,1,0:T(1,128)S(1)}, u32[]{:S(2)}, u32[]{:S(2)}) async-start(f32[32,1,1]{2,1,0:T(1,128)} %copy.171), calls=%async_computation | async-start | bytes 32768 | tf_op jit(solution)/shard_map/all_to_all | solution.py:79
  22.5 14.1 %all-to-all-start.4 = ((f32[32,4,1,128]{3,1,2,0:T(4,128)}), f32[32,4,1,128]{3,1,2,0:T(4,128)S(1)}, u32[]{:S(2)}, u32[]{:S(2)}) async-start(f32[32,4,1,128]{3,1,2,0:T(4,128)} %get-tuple-element.403), calls=%async_computation.4 | async-start | bytes 131072 | tf_op jit(solution)/shard_map/all_to_all | solution.py:78
  30.1 3.0 copy-start.1
  36.5 13.4 %all-to-all-start.2 = ((f32[32,4,1,128]{3,1,2,0:T(4,128)}), f32[32,4,1,128]{3,1,2,0:T(4,128)S(1)}, u32[]{:S(2)}, u32[]{:S(2)}) async-start(f32[32,4,1,128]{3,1,2,0:T(4,128)} %get-tuple-element.404), calls=%async_computation.2 | async-start | bytes 131072 | tf_op jit(solution)/shard_map/all_to_all | solution.py:77
  50.0 7.6 %copy-start.8 = (f32[4,1,1024]{2,1,0:T(1,128)S(1)}, f32[4,1,1024]{2,1,0:T(1,128)}, u32[]{:S(2)}) copy-start(f32[4,1,1024]{2,1,0:T(1,128)} %param.24) | copy-start | bytes 49156
  50.0 9.1 %copy-start.2 = (bf16[1024,4,128]{2,1,0:T(4,128)(2,1)S(1)}, bf16[1024,4,128]{2,1,0:T(4,128)(2,1)}, u32[]{:S(2)}) copy-start(bf16[1024,4,128]{2,1,0:T(4,128)(2,1)} %param.20) | copy-start | bytes 3145732
  50.0 57.8 %all-to-all-start.3 = ((bf16[32,128,4,128]{3,1,2,0:T(8,128)(2,1)}), bf16[32,128,4,128]{3,1,2,0:T(8,128)(2,1)}, u32[]{:S(2)}, u32[]{:S(2)}) async-start(bf16[32,128,4,128]{3,1,2,0:T(8,128)(2,1)} %get-tuple-element.407), calls=%async_computation.3 | async-start | bytes 8388608 | tf_op jit(solution)/shard_map/all_to_all | solution.py:83
  107.8 59.2 %all-to-all-start.1 = ((bf16[32,128,4,128]{3,1,2,0:T(8,128)(2,1)}), bf16[32,128,4,128]{3,1,2,0:T(8,128)(2,1)}, u32[]{:S(2)}, u32[]{:S(2)}) async-start(bf16[32,128,4,128]{3,1,2,0:T(8,128)(2,1)} %get-tuple-element.408), calls=%async_computation.1 | async-start | bytes 8388608 | tf_op jit(solution)/shard_map/all_to_all | solution.py:82
  116.8 294.6 %reduce-scatter.3.cloned.1.call-start = ((), (), s32[]{:S(2)}) async-start(), calls=%async_computation.8 | async-start | bytes 2621440 | tf_op jit(solution)/shard_map/reduce_scatter | solution.py:130
  117.3 12.9 %copy-start.6 = (bf16[1024,4,128]{2,1,0:T(4,128)(2,1)S(1)}, bf16[1024,4,128]{2,1,0:T(4,128)(2,1)}, u32[]{:S(2)}) copy-start(bf16[1024,4,128]{2,1,0:T(4,128)(2,1)} %param.21) | copy-start | bytes 3145732
  131.4 7.1 %copy-start.5 = (bf16[1024,4,1,128]{3,1,2,0:T(4,128)(2,1)S(1)}, bf16[1024,4,1,128]{3,1,2,0:T(4,128)(2,1)}, u32[]{:S(2)}) copy-start(bf16[1024,4,1,128]{3,1,2,0:T(4,128)(2,1)} %param.22) | copy-start | bytes 3145732
  186.4 2.8 copy-start.7
  189.2 3.6 copy-start
  209.1 2.8 copy-start.7
  211.9 3.6 copy-start
  314.7 90.4 %copy-start.3 = (bf16[1024,4,128]{2,1,0:T(4,128)(2,1)S(1)}, bf16[1024,4,128]{2,1,0:T(4,128)(2,1)}, u32[]{:S(2)}) copy-start(bf16[1024,4,128]{2,1,0:T(4,128)(2,1)} %param.20) | copy-start | bytes 3145732
  314.7 215.5 %all-to-all-start.5 = ((f32[32,128,4,128]{3,2,1,0:T(4,128)}), f32[32,128,4,128]{3,2,1,0:T(4,128)}, u32[]{:S(2)}, u32[]{:S(2)}) async-start(f32[32,128,4,128]{3,2,1,0:T(4,128)} %copy.190), calls=%async_computation.5 | async-start | bytes 16777216 | tf_op jit(solution)/shard_map/all_to_all | solution.py:125
  404.3 33.0 %reduce-scatter.5.cloned.1.call-start = ((), (), s32[]{:S(2)}) async-start(), calls=%async_computation.9 | async-start | bytes 2621440 | tf_op jit(solution)/shard_map/reduce_scatter | solution.py:131
  405.0 125.2 %copy-start.10 = (pred[8,32]{1,0:T(8,128)(4,1)S(1)}, pred[8,32]{1,0:T(8,128)(4,1)}, u32[]{:S(2)}) copy-start(pred[8,32]{1,0:T(8,128)(4,1)} %copy-done.9) | copy-start | bytes 772
  405.0 125.2 %copy-start.12 = (pred[32]{0:T(512)(128)(4,1)S(1)}, pred[32]{0:T(512)(128)(4,1)}, u32[]{:S(2)}) copy-start(pred[32]{0:T(512)(128)(4,1)} %copy-done.11) | copy-start | bytes 100
Sparse Core Ops, SparseCore 0:
  284.9 108.9 reduce-scatter.2
  407.5 29.7 reduce-scatter.4
where the time goes:
time: 560 us; the launch traced here: 551 us
  waiting for transfers between devices  164 us (29%)
  starting transfers between devices  130 us (23%)
  other arithmetic  85.7 us (15%)
  matrix products  83.4 us (15%)
  local copies, waits for them, and re-layouts  68.3 us (12%)
  between operations  14.8 us (3%)
  loops' own time  5.88 us (1%)
    all_to_all x1, waiting for transfers between devices, body(): lax.all_to_all(dq_back, 'ctx', split_axis=0, concat_axis=0, tiled=True)  91.2 us
    all_to_all x1, starting transfers between devices, body(): lax.all_to_all(dq_back, 'ctx', split_axis=0, concat_axis=0, tiled=True)  89.6 us
    add x16, other arithmetic, group_step(): return (dq_slots, acc_k + group_k, acc_v + group_v)  49.7 us
    all_to_all x1, waiting for transfers between devices, body(): lax.all_to_all(send_g, 'ctx', split_axis=0, concat_axis=0, tiled=True)  40.6 us
    reduce_scatter x1, waiting for transfers between devices, body(): lax.psum_scatter(grad_v, 'head', scatter_dimension=1, tiled=True)  24 us
    dot_general x3, matrix products, slot_grads(): jnp.einsum('srkgd,ckd->skgrc', grad_part, value_part, preferred_element_t...  19 us
    dot_general x3, matrix products, slot_grads(): jnp.einsum('skgrc,srkgd->ckd', prob_low, grad_part, preferred_element_typ...  17.8 us
    select_n x1, local copies, waits for them, and re-layouts, body(): jnp.take(dq_sorted, restore, axis=0).reshape(peers, QB, kv_heads, width)  13.8 us
  transfers between devices with their start and end apart: 8, of which 4 were waited for; matrix products, arithmetic and copies ran while one was open for 20% of the time, Pallas kernels for 0%

commit v1 on v0

v1 whole, which is shorter than its diff:
```python
import functools
import math

import jax
import jax.numpy as jnp
from jax import lax
from jax.experimental import pallas as pl
from jax.experimental.pallas import tpu as pltpu
from jax.sharding import PartitionSpec as P


QB = 128
SIDE = 4
TILE = 256
OWN_TILE = 512
PIECES = 2
VMEM_LIMIT = 60 * 1024 * 1024
LOG2E = math.log2(math.e)


NT = (((1,), (1,)), ((), ()))
NN = (((1,), (0,)), ((), ()))
TN = (((0,), (0,)), ((), ()))


def dot(a, b, dims):
    return lax.dot_general(a, b, dims, preferred_element_type=jnp.float32)


def pairs(place):
    found = []
    for x in range(SIDE):
        for z in range(SIDE):
            for core in range(2):
                to_x, to_z, to_core = place(x, z, core)
                target = (to_x % SIDE * SIDE + to_z % SIDE) * 2 + to_core
                found.append(((x * SIDE + z) * 2 + core, target))
    return found


def shift(value, phase, step):
    def place(x, z, core):
        along_x = step if core == phase else 0
        return x + along_x, z + step - along_x, core

    return lax.ppermute(value, "ctx", pairs(place))


def other_core(value):
    return lax.ppermute(value, "ctx", pairs(lambda x, z, core: (x, z, 1 - core)))


def tile_grads(keys, values, q, g, lse, delta, scale2, mask=None):
    prob = jnp.exp2(dot(keys, q, NT) * scale2 - lse)
    if mask is not None:
        prob = jnp.where(mask, prob, 0.0)
    dscore = prob * (dot(values, g, NT) - delta)
    prob_low = prob.astype(jnp.bfloat16)
    dscore_low = dscore.astype(jnp.bfloat16)
    return dot(dscore_low, q, NN), dot(prob_low, g, NN), dot(dscore_low, keys, TN)


def own_kernel(scale2, q_ref, g_ref, st_ref, k_ref, v_ref, dq_ref, dk_ref, dv_ref):
    block = pl.program_id(0)

    @pl.when(block == 0)
    def _():
        dk_ref[...] = jnp.zeros_like(dk_ref)
        dv_ref[...] = jnp.zeros_like(dv_ref)

    rows = q_ref.shape[0] * QB
    q = q_ref[...].reshape(rows, -1)
    g = g_ref[...].reshape(rows, -1)
    lse = st_ref[0, 0:1, :]
    delta = st_ref[0, 1:2, :]
    ahead = lax.broadcasted_iota(jnp.int32, (OWN_TILE, rows), 0) - (
        lax.broadcasted_iota(jnp.int32, (OWN_TILE, rows), 1) & (QB - 1)
    )

    def step(tile, masked):
        where = pl.ds(tile * OWN_TILE, OWN_TILE)
        mask = ahead <= block * QB - tile * OWN_TILE if masked else None
        dk, dv, dq = tile_grads(
            k_ref[where, :], v_ref[where, :], q, g, lse, delta, scale2, mask
        )
        dk_ref[where, :] += dk
        dv_ref[where, :] += dv
        return dq

    reach = OWN_TILE // QB
    for last in range(k_ref.shape[0] // OWN_TILE):

        @pl.when(block // reach == last)
        def _():
            dq = step(last, True)
            for tile in range(last):
                dq += step(tile, False)
            dq_ref[...] = dq.reshape(dq_ref.shape)


def own_grads(packed, stats, keys, values, scale2):
    heads, _, width = packed.shape
    rows = keys.shape[0]
    blocks = rows // QB
    q_spec = pl.BlockSpec((heads, QB, width), lambda b: (0, b, 0))
    g_spec = pl.BlockSpec((heads, QB, width), lambda b: (0, b + blocks, 0))
    whole = pl.BlockSpec((rows, width), lambda b: (0, 0))
    acc = jax.ShapeDtypeStruct(keys.shape, jnp.float32)
    return pl.pallas_call(
        functools.partial(own_kernel, scale2),
        grid=(blocks,),
        in_specs=[q_spec, g_spec, pl.BlockSpec((1, 2, heads * QB), lambda b: (b, 0, 0)), whole, whole],
        out_specs=[q_spec, whole, whole],
        out_shape=[jax.ShapeDtypeStruct((heads, rows, width), jnp.float32), acc, acc],
        compiler_params=pltpu.CompilerParams(vmem_limit_bytes=VMEM_LIMIT),
        cost_estimate=pl.CostEstimate(
            flops=6 * heads * rows * rows * width, bytes_accessed=8 << 20, transcendentals=0
        ),
        name="own",
    )(packed, packed, stats, keys, values)


def remote_kernel(scale2, bases, fresh, tbl, *refs):
    sources = len(bases) * PIECES
    q0, g0, q1, g1, st0, st1, in0 = refs[:7]
    rest = refs[7:]
    if not fresh:
        in1, rest = rest[0], rest[1:]
    blocks = rest[:sources]
    dq0, dq1 = rest[sources : sources + 2]
    outs = rest[sources + 2 : -1]
    buf = rest[-1]
    at = pl.program_id(0)
    heads = q0.shape[0]
    rows = heads * QB
    span = SIDE // PIECES

    @pl.when(at == 0)
    def _():
        dq0[...] = in0[...]
        dq1[...] = jnp.zeros_like(dq1) if fresh else in1[...]

    for i, block_ref in enumerate(blocks):

        @pl.when(at // span == i)
        def _():
            buf[...] = block_ref[0]

    entry = at % SIDE + bases[0]
    for i in range(1, len(bases)):
        entry = jnp.where(at // SIDE == i, at % SIDE + bases[i], entry)
    own = tbl[entry]
    sib = tbl[SIDE * SIDE + entry]

    def load(block, q_ref, g_ref, st_ref):
        where = pl.ds(pl.multiple_of(block * QB, QB), QB)
        stats = st_ref[block]
        return (
            q_ref[:, where, :].reshape(rows, -1),
            g_ref[:, where, :].reshape(rows, -1),
            stats[0:1, :],
            stats[1:2, :],
        )

    def run(sides):
        loaded = [load(block, *side[:3]) for block, side in sides]
        total = [None] * len(sides)
        for tile in range(buf.shape[1] // TILE):
            where = pl.ds(tile * TILE, TILE)
            keys, values = buf[0, where, :], buf[1, where, :]
            dk_sum, dv_sum = None, None
            for i, (q, g, lse, delta) in enumerate(loaded):
                dk, dv, dq = tile_grads(keys, values, q, g, lse, delta, scale2)
                dk_sum = dk if dk_sum is None else dk_sum + dk
                dv_sum = dv if dv_sum is None else dv_sum + dv
                total[i] = dq if total[i] is None else total[i] + dq
            buf[0, where, :] = dk_sum.astype(jnp.bfloat16)
            buf[1, where, :] = dv_sum.astype(jnp.bfloat16)
        for (block, side), dq in zip(sides, total):
            where = pl.ds(pl.multiple_of(block * QB, QB), QB)
            side[3][:, where, :] += dq.reshape(heads, QB, -1)

    own_side = (own, (q0, g0, st0, dq0))
    sib_side = (sib, (q1, g1, st1, dq1))

    @pl.when((own >= 0) & (sib >= 0))
    def _():
        run([own_side, sib_side])

    @pl.when((own >= 0) & (sib < 0))
    def _():
        run([own_side])

    @pl.when((own < 0) & (sib >= 0))
    def _():
        run([sib_side])

    @pl.when((own < 0) & (sib < 0))
    def _():
        buf[...] = jnp.zeros_like(buf)

    for i, out_ref in enumerate(outs):

        @pl.when(at // SIDE == i)
        def _():
            out_ref[0] = buf[...]


def remote_grads(table, own, sib, stats, sources, bases, carried, scale2):
    heads, _, width = own.shape
    rows = stats[0].shape[0] * QB
    count = len(bases)
    span = SIDE // PIECES
    once = pl.Buffered(1)
    q_spec = pl.BlockSpec((heads, rows, width), lambda k, t: (0, 0, 0), pipeline_mode=once)
    g_spec = pl.BlockSpec((heads, rows, width), lambda k, t: (0, 1, 0), pipeline_mode=once)
    stat = pl.BlockSpec(stats[0].shape, lambda k, t: (0, 0, 0))
    acc_spec = pl.BlockSpec((heads, rows, width), lambda k, t: (0, 0, 0))

    def piece(size, i):
        return pl.BlockSpec(
            (1, 2, rows, width), lambda k, t: (jnp.clip(k - size * i, 0, size - 1), 0, 0, 0)
        )

    operands = [array for source in sources for array in source]
    acc = jax.ShapeDtypeStruct((heads, rows, width), jnp.float32)
    part = jax.ShapeDtypeStruct((SIDE, 2, rows, width), jnp.bfloat16)
    return pl.pallas_call(
        functools.partial(remote_kernel, scale2, bases, len(carried) == 1),
        grid_spec=pltpu.PrefetchScalarGridSpec(
            num_scalar_prefetch=1,
            grid=(SIDE * count,),
            in_specs=[q_spec, g_spec, q_spec, g_spec, stat, stat]
            + [q_spec] * len(carried)
            + [piece(span, i) for i in range(len(operands))],
            out_specs=[acc_spec, acc_spec] + [piece(SIDE, i) for i in range(count)],
            scratch_shapes=[pltpu.VMEM((2, rows, width), jnp.bfloat16)],
        ),
        out_shape=[acc, acc] + [part] * count,
        compiler_params=pltpu.CompilerParams(vmem_limit_bytes=VMEM_LIMIT),
        cost_estimate=pl.CostEstimate(
            flops=SIDE * count * 10 * heads * QB * rows * width,
            bytes_accessed=(12 + 4 * count) << 20,
            transcendentals=0,
        ),
        name="remote",
    )(table, own, own, sib, sib, *stats, *carried, *operands)


def split3(value):
    terms = []
    for _ in range(3):
        term = lax.reduce_precision(value, 8, 7)
        terms.append(term.astype(jnp.bfloat16))
        value = value - term
    return jnp.stack(terms, axis=-2)


def grads(queries, key_rows, value_rows, out_grad, outputs, logsumexp, selections):
    rows, kv_heads, _, width = queries.shape
    blocks = rows // QB
    scale = width ** (-0.5)
    scale2 = scale * LOG2E
    me = lax.axis_index("ctx")
    head = lax.axis_index("head")
    x, z, core = me // (2 * SIDE), (me // 2) % SIDE, me % 2

    keys = lax.dynamic_index_in_dim(key_rows, head, 1, keepdims=False)
    values = lax.dynamic_index_in_dim(value_rows, head, 1, keepdims=False)
    both = jnp.stack([keys, values])
    behind = shift(both, 0, 1)
    ahead = shift(both, 0, -1)
    across = shift(both, 0, 2)
    first = jnp.stack([both, behind])
    second = jnp.stack([across, ahead])
    line = (first, second)
    line_behind = (shift(first, 1, 1), shift(second, 1, 1))
    line_ahead = (shift(first, 1, -1), shift(second, 1, -1))
    line_across = (shift(line_behind[0], 1, 1), shift(line_ahead[1], 1, -1))

    def turn(value):
        return lax.all_to_all(value, "head", split_axis=0, concat_axis=0, tiled=True)

    delta = jnp.sum(out_grad.astype(jnp.float32) * outputs.astype(jnp.float32), axis=-1)
    stats = jnp.stack([logsumexp[:, 0] * LOG2E, delta[:, :, 0].T], axis=1)
    stats = split3(stats.reshape(kv_heads, 2, rows)).reshape(kv_heads, -1, width)
    own = turn(
        jnp.concatenate(
            [
                jnp.transpose(queries[:, :, 0], (1, 0, 2)),
                jnp.transpose(out_grad[:, :, 0], (1, 0, 2)),
                stats,
            ],
            axis=1,
        ),
    )
    sib = other_core(own)
    sib_selections = other_core(selections)

    def stats_of(packed):
        terms = packed[:, 2 * rows :].reshape(-1, 2, 3, blocks, QB).astype(jnp.float32)
        return (terms[:, :, 0] + terms[:, :, 1] + terms[:, :, 2]).transpose(2, 1, 0, 3).reshape(blocks, 2, -1)

    own_stats, sib_stats = stats_of(own), stats_of(sib)

    index = jnp.arange(SIDE * SIDE, dtype=jnp.int32)
    near, far = index % SIDE, index // SIDE
    back_x, back_z = jnp.where(core == 0, near, far), jnp.where(core == 0, far, near)
    source = (((x - back_x) % SIDE) * SIDE + (z - back_z) % SIDE) * 2 + core

    def listed(picks, device):
        hit = ((picks[:, 1:2] == source) | (picks[:, 2:3] == source)) & (source != device)
        return jnp.max(jnp.where(hit, jnp.arange(blocks, dtype=jnp.int32)[:, None], -1), axis=0)

    table = jnp.concatenate([listed(selections, me), listed(sib_selections, me + 1 - 2 * core)])

    def remote(sources, bases, carried):
        return remote_grads(
            table, own, sib, (own_stats, sib_stats), sources, bases, carried, scale2
        )

    own_q, own_k, own_v = own_grads(own, own_stats, keys, values, scale2)
    dq0, dq1, part_behind, part_ahead = remote(
        [line_behind, line_ahead], (SIDE, 3 * SIDE), (own_q,)
    )
    back_behind = shift(part_behind, 1, -1)
    back_ahead = shift(part_ahead, 1, 1)
    dq0, dq1, part_across, part_line = remote(
        [line_across, line], (2 * SIDE, 0), (dq0, dq1)
    )
    back_across = shift(part_across, 1, 2)

    total = [
        sum(part[i].astype(jnp.float32) for part in (part_line, back_behind, back_ahead, back_across))
        for i in range(SIDE)
    ]
    low = [part.astype(jnp.bfloat16) for part in total[1:]]
    near_sum = (
        total[0]
        + shift(low[0], 0, -1).astype(jnp.float32)
        + shift(low[2], 0, 1).astype(jnp.float32)
        + shift(low[1], 0, 2).astype(jnp.float32)
    )
    grad_k = ((near_sum[0] + own_k) * scale).astype(jnp.bfloat16)
    grad_v = (near_sum[1] + own_v).astype(jnp.bfloat16)

    dq_low = dq1.astype(jnp.bfloat16)
    returned = other_core(dq_low)
    dq = ((dq0 + returned.astype(jnp.float32)) * scale).astype(jnp.bfloat16)
    dq = jnp.transpose(turn(dq), (1, 0, 2))[:, :, None]
    return dq, grad_k[:, None], grad_v[:, None]


def solution(mesh):
    in_specs = (
        P("ctx", None, "head", None),
        P("ctx", None, None),
        P("ctx", None, None),
        P("ctx", None, "head", None),
        P("ctx", None, "head", None),
        P(None, "head", "ctx"),
        P("ctx", None),
    )
    out_specs = (P("ctx", None, "head", None), P("ctx", "head", None), P("ctx", "head", None))
    return jax.shard_map(grads, mesh=mesh, in_specs=in_specs, out_specs=out_specs, check_vma=False)
```

time: 560 us -> 210 us (0.38)
  the two profiles are of different devices: /device:TPU:44 before, /device:TPU:0 now
where the time goes in v1:
time: 210 us; the launch traced here: 209 us
  waiting for transfers between devices  70.3 us (33%)
  starting transfers between devices  67.8 us (32%)
  Pallas kernels  41 us (20%)
  other arithmetic  22.4 us (11%)
  local copies, waits for them, and re-layouts  6.99 us (3%)
    ppermute x15, starting transfers between devices, shift(): return lax.ppermute(value, 'ctx', pairs(place))  48.9 us
    ppermute x15, waiting for transfers between devices, shift(): return lax.ppermute(value, 'ctx', pairs(place))  48.5 us
    pallas_call x2, Pallas kernels, remote_grads(): pl.pallas_call(functools.partial(remote_kernel, scale2, bases, len(carrie...  25.8 us
    all_to_all x2, waiting for transfers between devices, turn(): lax.all_to_all(value, 'head', split_axis=0, concat_axis=0, tiled=True)  18.5 us
    pallas_call x1, Pallas kernels, own_grads(): pl.pallas_call(functools.partial(own_kernel, scale2), grid=(blocks,), in_...  15.1 us
    ppermute x3, starting transfers between devices, other_core(): lax.ppermute(value, 'ctx', pairs(lambda x, z, core: (x, z, 1 - core)))  10.5 us
    all_to_all x2, starting transfers between devices, turn(): lax.all_to_all(value, 'head', split_axis=0, concat_axis=0, tiled=True)  8.36 us
  transfers between devices with their start and end apart: 20, of which 8 were waited for; matrix products, arithmetic and copies ran while one was open for 10% of the time, Pallas kernels for 13%

profile of v1, /device:TPU:0, one launch (start us, length us, event | category | flops | bytes accessed | tf_op | source)
XLA Modules:
  0.0 209.4 jit_solution(4665838452832491735)
XLA Ops:
  0.6 0.0 copy-start
  0.7 0.9 fusion.16
  1.5 2.7 %multiply_reduce_fusion = f32[1024,4]{1,0:T(8,128)S(1)} fusion(bf16[1024,4,1,128]{3,1,2,0:T(4,128)(2,1)} %param.11, bf16[1024,4,1,128]{3,1,2,0:T(4,128)(2,1)} %param.10), kind=kLoop, calls=%fused_computation.2 | loop fusion | flops 2093056 | bytes 2113536 | tf_op jit(solution)/shard_map/reduce_sum | solution.py:284
  4.3 0.2 copy.62
  4.6 0.1 reshape.224
  4.6 0.3 copy_bitcast_fusion
  4.9 1.5 pad_maximum_fusion
  6.4 4.7 %all-to-all-start = ((bf16[4,2096,128]{2,1,0:T(8,128)(2,1)}), bf16[4,2096,128]{2,1,0:T(8,128)(2,1)S(1)}, u32[]{:S(2)}, u32[]{:S(2)}) async-start(bf16[4,2096,128]{2,1,0:T(8,128)(2,1)} %pad_maximum_fusion), calls=%async_computation | async-start | bytes 4292608 | tf_op jit(solution)/shard_map/all_to_all | solution.py:282
  11.2 2.3 %constant_dynamic-slice_fusion = (bf16[1024,1,128]{2,1,0:T(2,128)(2,1)S(1)}, bf16[1024,1,128]{2,1,0:T(2,128)(2,1)S(1)}) fusion(bf16[1024,4,128]{2,1,0:T(4,128)(2,1)S(1)} %copy-done.9, s32[]{:T(128)S(6)} %select_n.138, bf16[1024,4,128]{2,1,0:T(4,128)(2,1)} %param.8), kind=kLoop, calls=%fused_computation.71 | loop fusion | bytes 1048580 | tf_op jit(solution)/shard_map/jit(dynamic_index_in_dim)/dynamic_slice | solution.py:269
  13.6 0.9 fusion.23
  14.5 3.0 %collective-permute-start.4 = (bf16[2,1024,128]{2,1,0:T(8,128)(2,1)}, bf16[2,1024,128]{2,1,0:T(8,128)(2,1)}, u32[]{:S(2)}, u32[]{:S(2)}) collective-permute-start(bf16[2,1024,128]{2,1,0:T(8,128)(2,1)} %get-tuple-element.50), channel_id=1, source_target_pairs={{0,64},{4,20},{8,72},{12,28},{16,80},{20,4},{24,88},{28,12},{32,96... | collective-permute-start | bytes 1572872 | tf_op jit(solution)/shard_map/ppermute | solution.py:46
  17.5 1.1 collective-permute-start.5
  18.6 0.9 collective-permute-start.2
  19.5 18.5 %all-to-all-done.q_ref.g_ref.refs_0_.refs_1_ = bf16[4,2096,128]{2,1,0:T(8,128)(2,1)S(1)} async-done(((bf16[4,2096,128]{2,1,0:T(8,128)(2,1)}), bf16[4,2096,128]{2,1,0:T(8,128)(2,1)S(1)}, u32[]{:S(2)}, u32[]{:S(2)}) %all-to-all-start) | async-done | bytes 2146336 | tf_op jit(solution)/shard_map/all_to_all | solution.py:282
  38.0 3.1 %pad_maximum_fusion.2.refs_11_ = bf16[2,2,1024,128]{3,2,1,0:T(8,128)(2,1)} fusion(bf16[1,2,1024,128]{3,2,1,0:T(8,128)(2,1)} %bitcast.24, bf16[1,2,1024,128]{3,2,1,0:T(8,128)(2,1)} %bitcast.23), kind=kLoop, calls=%fused_computation.4 | loop fusion | flops 524288 | bytes 2097152 | tf_op jit(solution)/shard_map/stack | solution.py:275
  41.1 4.0 %collective-permute-start.8 = (bf16[2,2,1024,128]{3,2,1,0:T(8,128)(2,1)}, bf16[2,2,1024,128]{3,2,1,0:T(8,128)(2,1)}, u32[]{:S(2)}, u32[]{:S(2)}) collective-permute-start(bf16[2,2,1024,128]{3,2,1,0:T(8,128)(2,1)} %pad_maximum_fusion.2.refs_11_), channel_id=1, source_target_pairs={{0,24},{4,100},{8,0},{12,108},{16,8},{20,116},{24,16},{28,124},{32... | collective-permute-start | bytes 3145736 | tf_op jit(solution)/shard_map/ppermute | solution.py:46
  45.2 2.1 %pad_maximum_fusion.1.refs_10_ = bf16[2,2,1024,128]{3,2,1,0:T(8,128)(2,1)} fusion(bf16[1,2,1024,128]{3,2,1,0:T(8,128)(2,1)} %bitcast.22, bf16[1,2,1024,128]{3,2,1,0:T(8,128)(2,1)S(1)} %get-tuple-element.49), kind=kLoop, calls=%fused_computation.3 | loop fusion | flops 524288 | bytes 2097152 | tf_op jit(solution)/shard_map/stack | solution.py:274
  47.3 0.1 collective-permute-start
  47.5 1.1 collective-permute-done
  48.6 0.1 select_reduce_fusion.1
  48.6 0.6 pad_add_fusion.tbl
  49.2 3.2 %collective-permute-start.7 = (bf16[2,2,1024,128]{3,2,1,0:T(8,128)(2,1)}, bf16[2,2,1024,128]{3,2,1,0:T(8,128)(2,1)}, u32[]{:S(2)}, u32[]{:S(2)}) collective-permute-start(bf16[2,2,1024,128]{3,2,1,0:T(8,128)(2,1)} %pad_maximum_fusion.1.refs_10_), channel_id=1, source_target_pairs={{0,24},{4,100},{8,0},{12,108},{16,8},{20,116},{24,16},{28,124},{32... | collective-permute-start | bytes 3145736 | tf_op jit(solution)/shard_map/ppermute | solution.py:46
  52.5 5.3 %collective-permute-done.8.refs_10_ = bf16[2,2,1024,128]{3,2,1,0:T(8,128)(2,1)} collective-permute-done((bf16[2,2,1024,128]{3,2,1,0:T(8,128)(2,1)}, bf16[2,2,1024,128]{3,2,1,0:T(8,128)(2,1)}, u32[]{:S(2)}, u32[]{:S(2)}) %collective-permute-start.8) | collective-permute-done | bytes 1048608 | tf_op jit(solution)/shard_map/ppermute | solution.py:46
  57.8 3.7 %collective-permute-start.10 = (bf16[2,2,1024,128]{3,2,1,0:T(8,128)(2,1)}, bf16[2,2,1024,128]{3,2,1,0:T(8,128)(2,1)}, u32[]{:S(2)}, u32[]{:S(2)}) collective-permute-start(bf16[2,2,1024,128]{3,2,1,0:T(8,128)(2,1)} %collective-permute-done.8.refs_10_), channel_id=1, source_target_pairs={{0,24},{4,100},{8,0},{12,108},{16,8},{20,116},{24,16},{28,124},{32... | collective-permute-start | bytes 3145736 | tf_op jit(solution)/shard_map/ppermute | solution.py:46
  61.5 2.0 collective-permute-done.3.refs_7_
  63.6 0.7 reshape.225.st_ref.refs_4_
  64.3 15.1 %own.1 = (f32[4,1024,128]{2,1,0:T(8,128)}, f32[1024,128]{1,0:T(8,128)}, f32[1024,128]{1,0:T(8,128)}) custom-call(bf16[4,2096,128]{2,1,0:T(8,128)(2,1)} %copy-done.1, bf16[4,2096,128]{2,1,0:T(8,128)(2,1)} %copy-done.1, f32[8,2,512]{2,1,0:T(2,128)} %reshape.225.st_ref.refs_4_, bf16[1024,128]{1,0:T(8,128)(2,1)} %bitcast.90, bf16[1024,128]{1,0:T(8,128)(2,1)} %bitcast.88), custom_call_target="tpu_custom_call" | custom-call | flops 3221225472 | bytes 8388608 | tf_op jit(solution)/shard_map/own/pallas_call | solution.py:109
  79.5 0.8 slice.124
  80.4 0.6 reshape.226.refs_5_
  81.0 11.8 %remote.2 = (f32[4,1024,128]{2,1,0:T(8,128)}, f32[4,1024,128]{2,1,0:T(8,128)}, bf16[4,2,1024,128]{3,2,1,0:T(8,128)(2,1)}, bf16[4,2,1024,128]{3,2,1,0:T(8,128)(2,1)}) custom-call(s32[32]{0:T(128)} %pad_add_fusion.tbl, bf16[4,2096,128]{2,1,0:T(8,128)(2,1)} %copy-done.1, bf16[4,2096,128]{2,1,0:T(8,128)(2,1)} %copy-done.1, ...), custom_call_target="tpu_custom_call" | custom-call | flops 5368709120 | bytes 20971520 | tf_op jit(solution)/shard_map/remote/pallas_call | solution.py:228
  92.8 14.1 %remote.3 = (f32[4,1024,128]{2,1,0:T(8,128)}, f32[4,1024,128]{2,1,0:T(8,128)}, bf16[4,2,1024,128]{3,2,1,0:T(8,128)(2,1)}, bf16[4,2,1024,128]{3,2,1,0:T(8,128)(2,1)}) custom-call(s32[32]{0:T(128)} %pad_add_fusion.tbl, bf16[4,2096,128]{2,1,0:T(8,128)(2,1)} %copy-done.1, bf16[4,2096,128]{2,1,0:T(8,128)(2,1)} %copy-done.1, ...), custom_call_target="tpu_custom_call" | custom-call | flops 5368709120 | bytes 20971520 | tf_op jit(solution)/shard_map/remote/pallas_call | solution.py:228
  106.9 8.2 %collective-permute-start.14 = (bf16[4,2,1024,128]{3,2,1,0:T(8,128)(2,1)}, bf16[4,2,1024,128]{3,2,1,0:T(8,128)(2,1)}, u32[]{:S(2)}, u32[]{:S(2)}) collective-permute-start(bf16[4,2,1024,128]{3,2,1,0:T(8,128)(2,1)} %get-tuple-element.22), channel_id=1, source_target_pairs={{0,16},{4,68},{8,24},{12,76},{16,0},{20,84},{24,8},{28,92},{32,48}... | collective-permute-start | bytes 6291464 | tf_op jit(solution)/shard_map/ppermute | solution.py:46
  115.1 5.4 %collective-permute-start.12 = (bf16[4,2,1024,128]{3,2,1,0:T(8,128)(2,1)}, bf16[4,2,1024,128]{3,2,1,0:T(8,128)(2,1)}, u32[]{:S(2)}, u32[]{:S(2)}) collective-permute-start(bf16[4,2,1024,128]{3,2,1,0:T(8,128)(2,1)} %get-tuple-element.20), channel_id=1, source_target_pairs={{0,24},{4,100},{8,0},{12,108},{16,8},{20,116},{24,16},{28,124},{32... | collective-permute-start | bytes 6291464 | tf_op jit(solution)/shard_map/ppermute | solution.py:46
  120.5 0.8 collective-permute-start.13
  121.2 1.7 convert_element_type.148
  123.0 10.4 %collective-permute-start.11 = (bf16[4,1024,128]{2,1,0:T(8,128)(2,1)S(1)}, bf16[4,1024,128]{2,1,0:T(8,128)(2,1)S(1)}, u32[]{:S(2)}, u32[]{:S(2)}) collective-permute-start(bf16[4,1024,128]{2,1,0:T(8,128)(2,1)S(1)} %convert_element_type.148), channel_id=1, source_target_pairs={{0,4},{4,0},{8,12},{12,8},{16,20},{20,16},{24,28},{28,24},{32,36},... | collective-permute-start | bytes 3145736 | tf_op jit(solution)/shard_map/ppermute | solution.py:50
  133.4 2.3 %collective-permute-done.11 = bf16[4,1024,128]{2,1,0:T(8,128)(2,1)S(1)} collective-permute-done((bf16[4,1024,128]{2,1,0:T(8,128)(2,1)S(1)}, bf16[4,1024,128]{2,1,0:T(8,128)(2,1)S(1)}, u32[]{:S(2)}, u32[]{:S(2)}) %collective-permute-start.11) | collective-permute-done | bytes 1048608 | tf_op jit(solution)/shard_map/ppermute | solution.py:50
  135.7 1.3 multiply_convert_fusion
  137.0 3.6 %all-to-all-start.1 = ((bf16[4,1024,128]{2,1,0:T(8,128)(2,1)}), bf16[4,1024,128]{2,1,0:T(8,128)(2,1)S(1)}, u32[]{:S(2)}, u32[]{:S(2)}) async-start(bf16[4,1024,128]{2,1,0:T(8,128)(2,1)} %multiply_convert_fusion), calls=%async_computation.1 | async-start | bytes 2097152 | tf_op jit(solution)/shard_map/all_to_all | solution.py:282
  140.6 27.4 %collective-permute-done.12 = bf16[4,2,1024,128]{3,2,1,0:T(8,128)(2,1)} collective-permute-done((bf16[4,2,1024,128]{3,2,1,0:T(8,128)(2,1)}, bf16[4,2,1024,128]{3,2,1,0:T(8,128)(2,1)}, u32[]{:S(2)}, u32[]{:S(2)}) %collective-permute-start.12) | collective-permute-done | bytes 2097184 | tf_op jit(solution)/shard_map/ppermute | solution.py:46
  168.1 4.1 %fusion.2 = (bf16[2,1024,128]{2,1,0:T(8,128)(2,1)}, bf16[2,1024,128]{2,1,0:T(8,128)(2,1)}, bf16[2,1024,128]{2,1,0:T(8,128)(2,1)}) fusion(bf16[4,2,1024,128]{3,2,1,0:T(8,128)(2,1)} %collective-permute-done.14, bf16[4,2,1024,128]{3,2,1,0:T(8,128)(2,1)} %collective-permute-done.13, bf16[4,2,1024,128]{3,2,1,0:T(8,128)(2,1)} %collective-permute-done.12, ...), kind=kLoop, calls=%fused_computation.13 | loop fusion | flops 6291456 | bytes 7864320 | tf_op jit(solution)/shard_map/add | solution.py:334
  172.2 17.7 %collective-permute-start.15 = (bf16[2,1024,128]{2,1,0:T(8,128)(2,1)}, bf16[2,1024,128]{2,1,0:T(8,128)(2,1)}, u32[]{:S(2)}, u32[]{:S(2)}) collective-permute-start(bf16[2,1024,128]{2,1,0:T(8,128)(2,1)} %get-tuple-element.44), channel_id=1, source_target_pairs={{0,96},{4,28},{8,104},{12,4},{16,112},{20,12},{24,120},{28,20},{32... | collective-permute-start | bytes 1572872 | tf_op jit(solution)/shard_map/ppermute | solution.py:46
  189.9 0.9 collective-permute-start.16
  190.7 1.8 copy.72
  192.5 10.0 %collective-permute-done.15 = bf16[2,1024,128]{2,1,0:T(8,128)(2,1)} collective-permute-done((bf16[2,1024,128]{2,1,0:T(8,128)(2,1)}, bf16[2,1024,128]{2,1,0:T(8,128)(2,1)}, u32[]{:S(2)}, u32[]{:S(2)}) %collective-permute-start.15) | collective-permute-done | bytes 524320 | tf_op jit(solution)/shard_map/ppermute | solution.py:46
  202.5 3.7 %collective-permute-done.16 = bf16[2,1024,128]{2,1,0:T(8,128)(2,1)} collective-permute-done((bf16[2,1024,128]{2,1,0:T(8,128)(2,1)}, bf16[2,1024,128]{2,1,0:T(8,128)(2,1)}, u32[]{:S(2)}, u32[]{:S(2)}) %collective-permute-start.16) | collective-permute-done | bytes 524320 | tf_op jit(solution)/shard_map/ppermute | solution.py:46
  206.2 2.3 %fusion.1 = f32[2,1024,128]{2,1,0:T(8,128)S(1)} fusion(bf16[2,1024,128]{2,1,0:T(8,128)(2,1)} %collective-permute-done.17, bf16[2,1024,128]{2,1,0:T(8,128)(2,1)} %collective-permute-done.16, bf16[2,1024,128]{2,1,0:T(8,128)(2,1)} %collective-permute-done.15, bf16[4,2,1024,128]{3,2,1,0:T(8,128)(2,1)} %collective-permute-done.14, ...), kind=kLoop, calls=%fused_computation.7 | loop fusion | flops 3407872 | bytes 4718592 | tf_op jit(solution)/shard_map/add | solution.py:339
  208.5 0.9 fusion.11
  (54 shorter events, 0.4 us)
Async XLA Ops:
  0.6 4.0 %copy-start = (bf16[1024,4,1,128]{3,1,2,0:T(4,128)(2,1)S(1)}, bf16[1024,4,1,128]{3,1,2,0:T(4,128)(2,1)}, u32[]{:S(2)}) copy-start(bf16[1024,4,1,128]{3,1,2,0:T(4,128)(2,1)} %param.10) | copy-start | bytes 3145732
  0.6 4.0 %copy-start.6 = (bf16[1024,4,1,128]{3,1,2,0:T(4,128)(2,1)S(1)}, bf16[1024,4,1,128]{3,1,2,0:T(4,128)(2,1)}, u32[]{:S(2)}) copy-start(bf16[1024,4,1,128]{3,1,2,0:T(4,128)(2,1)} %param.7) | copy-start | bytes 3145732
  6.4 4.7 %copy-start.9 = (bf16[1024,4,128]{2,1,0:T(4,128)(2,1)S(1)}, bf16[1024,4,128]{2,1,0:T(4,128)(2,1)}, u32[]{:S(2)}) copy-start(bf16[1024,4,128]{2,1,0:T(4,128)(2,1)} %param.9) | copy-start | bytes 3145732
  6.4 31.6 %all-to-all-start = ((bf16[4,2096,128]{2,1,0:T(8,128)(2,1)}), bf16[4,2096,128]{2,1,0:T(8,128)(2,1)S(1)}, u32[]{:S(2)}, u32[]{:S(2)}) async-start(bf16[4,2096,128]{2,1,0:T(8,128)(2,1)} %pad_maximum_fusion), calls=%async_computation | async-start | bytes 4292608 | tf_op jit(solution)/shard_map/all_to_all | solution.py:282
  13.5 27.6 %copy-start.4 = (bf16[1024,1,128]{2,0,1:T(8,128)(2,1)}, bf16[1024,1,128]{2,0,1:T(8,128)(2,1)S(1)}, u32[]{:S(2)}) copy-start(bf16[1024,1,128]{2,0,1:T(8,128)(2,1)S(1)} %copy.104) | copy-start | bytes 786436
  13.6 33.7 %copy-start.5 = (bf16[1024,1,128]{2,0,1:T(8,128)(2,1)}, bf16[1024,1,128]{2,0,1:T(8,128)(2,1)S(1)}, u32[]{:S(2)}) copy-start(bf16[1024,1,128]{2,0,1:T(8,128)(2,1)S(1)} %copy.105) | copy-start | bytes 786436
  14.5 23.5 %collective-permute-start.4 = (bf16[2,1024,128]{2,1,0:T(8,128)(2,1)}, bf16[2,1024,128]{2,1,0:T(8,128)(2,1)}, u32[]{:S(2)}, u32[]{:S(2)}) collective-permute-start(bf16[2,1024,128]{2,1,0:T(8,128)(2,1)} %get-tuple-element.50), channel_id=1, source_target_pairs={{0,64},{4,20},{8,72},{12,28},{16,80},{20,4},{24,88},{28,12},{32,96... | collective-permute-start | bytes 1572872 | tf_op jit(solution)/shard_map/ppermute | solution.py:46
  17.5 20.5 %collective-permute-start.5 = (bf16[2,1024,128]{2,1,0:T(8,128)(2,1)}, bf16[2,1024,128]{2,1,0:T(8,128)(2,1)}, u32[]{:S(2)}, u32[]{:S(2)}) collective-permute-start(bf16[2,1024,128]{2,1,0:T(8,128)(2,1)} %get-tuple-element.50), channel_id=1, source_target_pairs={{0,96},{4,28},{8,104},{12,4},{16,112},{20,12},{24,120},{28,20},{32... | collective-permute-start | bytes 1572872 | tf_op jit(solution)/shard_map/ppermute | solution.py:46
  18.6 26.5 %collective-permute-start.2 = (bf16[2,1024,128]{2,1,0:T(8,128)(2,1)}, bf16[2,1024,128]{2,1,0:T(8,128)(2,1)}, u32[]{:S(2)}, u32[]{:S(2)}) collective-permute-start(bf16[2,1024,128]{2,1,0:T(8,128)(2,1)} %get-tuple-element.50), channel_id=1, source_target_pairs={{0,32},{4,12},{8,40},{12,20},{16,48},{20,28},{24,56},{28,4},{32,64... | collective-permute-start | bytes 1572872 | tf_op jit(solution)/shard_map/ppermute | solution.py:46
  38.0 25.5 %copy-start.1 = (bf16[4,2096,128]{2,1,0:T(8,128)(2,1)}, bf16[4,2096,128]{2,1,0:T(8,128)(2,1)S(1)}, u32[]{:S(2)}) copy-start(bf16[4,2096,128]{2,1,0:T(8,128)(2,1)S(1)} %all-to-all-done.q_ref.g_ref.refs_0_.refs_1_) | copy-start | bytes 6438916
  38.0 41.5 %collective-permute-start.1 = (bf16[4,2096,128]{2,1,0:T(8,128)(2,1)S(1)}, bf16[4,2096,128]{2,1,0:T(8,128)(2,1)}, u32[]{:S(2)}, u32[]{:S(2)}) collective-permute-start(bf16[4,2096,128]{2,1,0:T(8,128)(2,1)S(1)} %all-to-all-done.q_ref.g_ref.refs_0_.refs_1_), channel_id=1, source_target_pairs={{0,4},{4,0},{8,12},{12,8},{16,20},{20,16},{24,28},{28,24},{32,36},... | collective-permute-start | bytes 6438920 | tf_op jit(solution)/shard_map/ppermute | solution.py:50
  38.0 9.3 %copy-start.10 = (s32[8,3]{0,1:T(4,128)S(1)}, s32[8,3]{0,1:T(4,128)}, u32[]{:S(2)}) copy-start(s32[8,3]{0,1:T(4,128)} %param.13) | copy-start | bytes 292
  41.1 16.7 %collective-permute-start.8 = (bf16[2,2,1024,128]{3,2,1,0:T(8,128)(2,1)}, bf16[2,2,1024,128]{3,2,1,0:T(8,128)(2,1)}, u32[]{:S(2)}, u32[]{:S(2)}) collective-permute-start(bf16[2,2,1024,128]{3,2,1,0:T(8,128)(2,1)} %pad_maximum_fusion.2.refs_11_), channel_id=1, source_target_pairs={{0,24},{4,100},{8,0},{12,108},{16,8},{20,116},{24,16},{28,124},{32... | collective-permute-start | bytes 3145736 | tf_op jit(solution)/shard_map/ppermute | solution.py:46
  47.3 16.2 %collective-permute-start.3 = (bf16[2,2,1024,128]{3,2,1,0:T(8,128)(2,1)}, bf16[2,2,1024,128]{3,2,1,0:T(8,128)(2,1)S(1)}, u32[]{:S(2)}, u32[]{:S(2)}) collective-permute-start(bf16[2,2,1024,128]{3,2,1,0:T(8,128)(2,1)} %pad_maximum_fusion.1.refs_10_), channel_id=1, source_target_pairs={{0,8},{4,36},{8,16},{12,44},{16,24},{20,52},{24,0},{28,60},{32,40}... | collective-permute-start | bytes 3145736 | tf_op jit(solution)/shard_map/ppermute | solution.py:46
  47.3 1.2 collective-permute-start
  49.2 31.8 %collective-permute-start.6 = (bf16[2,2,1024,128]{3,2,1,0:T(8,128)(2,1)}, bf16[2,2,1024,128]{3,2,1,0:T(8,128)(2,1)}, u32[]{:S(2)}, u32[]{:S(2)}) collective-permute-start(bf16[2,2,1024,128]{3,2,1,0:T(8,128)(2,1)} %pad_maximum_fusion.2.refs_11_), channel_id=1, source_target_pairs={{0,8},{4,36},{8,16},{12,44},{16,24},{20,52},{24,0},{28,60},{32,40}... | collective-permute-start | bytes 3145736 | tf_op jit(solution)/shard_map/ppermute | solution.py:46
  49.2 31.8 %collective-permute-start.7 = (bf16[2,2,1024,128]{3,2,1,0:T(8,128)(2,1)}, bf16[2,2,1024,128]{3,2,1,0:T(8,128)(2,1)}, u32[]{:S(2)}, u32[]{:S(2)}) collective-permute-start(bf16[2,2,1024,128]{3,2,1,0:T(8,128)(2,1)} %pad_maximum_fusion.1.refs_10_), channel_id=1, source_target_pairs={{0,24},{4,100},{8,0},{12,108},{16,8},{20,116},{24,16},{28,124},{32... | collective-permute-start | bytes 3145736 | tf_op jit(solution)/shard_map/ppermute | solution.py:46
  57.8 35.0 %collective-permute-start.10 = (bf16[2,2,1024,128]{3,2,1,0:T(8,128)(2,1)}, bf16[2,2,1024,128]{3,2,1,0:T(8,128)(2,1)}, u32[]{:S(2)}, u32[]{:S(2)}) collective-permute-start(bf16[2,2,1024,128]{3,2,1,0:T(8,128)(2,1)} %collective-permute-done.8.refs_10_), channel_id=1, source_target_pairs={{0,24},{4,100},{8,0},{12,108},{16,8},{20,116},{24,16},{28,124},{32... | collective-permute-start | bytes 3145736 | tf_op jit(solution)/shard_map/ppermute | solution.py:46
  63.5 16.0 %copy-start.11 = (bf16[2,2,1024,128]{3,2,1,0:T(8,128)(2,1)}, bf16[2,2,1024,128]{3,2,1,0:T(8,128)(2,1)S(1)}, u32[]{:S(2)}) copy-start(bf16[2,2,1024,128]{3,2,1,0:T(8,128)(2,1)S(1)} %collective-permute-done.3.refs_7_) | copy-start | bytes 3145732
  63.5 29.3 %collective-permute-start.9 = (bf16[2,2,1024,128]{3,2,1,0:T(8,128)(2,1)S(1)}, bf16[2,2,1024,128]{3,2,1,0:T(8,128)(2,1)}, u32[]{:S(2)}, u32[]{:S(2)}) collective-permute-start(bf16[2,2,1024,128]{3,2,1,0:T(8,128)(2,1)S(1)} %collective-permute-done.3.refs_7_), channel_id=1, source_target_pairs={{0,8},{4,36},{8,16},{12,44},{16,24},{20,52},{24,0},{28,60},{32,40}... | collective-permute-start | bytes 3145736 | tf_op jit(solution)/shard_map/ppermute | solution.py:46
  106.8 28.8 %copy-start.2 = (f32[4,1024,128]{2,1,0:T(8,128)S(1)}, f32[4,1024,128]{2,1,0:T(8,128)}, u32[]{:S(2)}) copy-start(f32[4,1024,128]{2,1,0:T(8,128)} %get-tuple-element.17) | copy-start | bytes 6291460
  106.9 33.8 %collective-permute-start.14 = (bf16[4,2,1024,128]{3,2,1,0:T(8,128)(2,1)}, bf16[4,2,1024,128]{3,2,1,0:T(8,128)(2,1)}, u32[]{:S(2)}, u32[]{:S(2)}) collective-permute-start(bf16[4,2,1024,128]{3,2,1,0:T(8,128)(2,1)} %get-tuple-element.22), channel_id=1, source_target_pairs={{0,16},{4,68},{8,24},{12,76},{16,0},{20,84},{24,8},{28,92},{32,48}... | collective-permute-start | bytes 6291464 | tf_op jit(solution)/shard_map/ppermute | solution.py:46
  115.1 53.0 %collective-permute-start.12 = (bf16[4,2,1024,128]{3,2,1,0:T(8,128)(2,1)}, bf16[4,2,1024,128]{3,2,1,0:T(8,128)(2,1)}, u32[]{:S(2)}, u32[]{:S(2)}) collective-permute-start(bf16[4,2,1024,128]{3,2,1,0:T(8,128)(2,1)} %get-tuple-element.20), channel_id=1, source_target_pairs={{0,24},{4,100},{8,0},{12,108},{16,8},{20,116},{24,16},{28,124},{32... | collective-permute-start | bytes 6291464 | tf_op jit(solution)/shard_map/ppermute | solution.py:46
  120.5 47.6 %collective-permute-start.13 = (bf16[4,2,1024,128]{3,2,1,0:T(8,128)(2,1)}, bf16[4,2,1024,128]{3,2,1,0:T(8,128)(2,1)}, u32[]{:S(2)}, u32[]{:S(2)}) collective-permute-start(bf16[4,2,1024,128]{3,2,1,0:T(8,128)(2,1)} %get-tuple-element.21), channel_id=1, source_target_pairs={{0,8},{4,36},{8,16},{12,44},{16,24},{20,52},{24,0},{28,60},{32,40}... | collective-permute-start | bytes 6291464 | tf_op jit(solution)/shard_map/ppermute | solution.py:46
  123.0 12.7 %collective-permute-start.11 = (bf16[4,1024,128]{2,1,0:T(8,128)(2,1)S(1)}, bf16[4,1024,128]{2,1,0:T(8,128)(2,1)S(1)}, u32[]{:S(2)}, u32[]{:S(2)}) collective-permute-start(bf16[4,1024,128]{2,1,0:T(8,128)(2,1)S(1)} %convert_element_type.148), channel_id=1, source_target_pairs={{0,4},{4,0},{8,12},{12,8},{16,20},{20,16},{24,28},{28,24},{32,36},... | collective-permute-start | bytes 3145736 | tf_op jit(solution)/shard_map/ppermute | solution.py:50
  137.0 31.1 %copy-start.3 = (bf16[4,2,1024,128]{3,2,1,0:T(8,128)(2,1)S(1)}, bf16[4,2,1024,128]{3,2,1,0:T(8,128)(2,1)}, u32[]{:S(2)}) copy-start(bf16[4,2,1024,128]{3,2,1,0:T(8,128)(2,1)} %get-tuple-element.19) | copy-start | bytes 6291460
  137.0 53.7 %all-to-all-start.1 = ((bf16[4,1024,128]{2,1,0:T(8,128)(2,1)}), bf16[4,1024,128]{2,1,0:T(8,128)(2,1)S(1)}, u32[]{:S(2)}, u32[]{:S(2)}) async-start(bf16[4,1024,128]{2,1,0:T(8,128)(2,1)} %multiply_convert_fusion), calls=%async_computation.1 | async-start | bytes 2097152 | tf_op jit(solution)/shard_map/all_to_all | solution.py:282
  172.2 30.3 %collective-permute-start.15 = (bf16[2,1024,128]{2,1,0:T(8,128)(2,1)}, bf16[2,1024,128]{2,1,0:T(8,128)(2,1)}, u32[]{:S(2)}, u32[]{:S(2)}) collective-permute-start(bf16[2,1024,128]{2,1,0:T(8,128)(2,1)} %get-tuple-element.44), channel_id=1, source_target_pairs={{0,96},{4,28},{8,104},{12,4},{16,112},{20,12},{24,120},{28,20},{32... | collective-permute-start | bytes 1572872 | tf_op jit(solution)/shard_map/ppermute | solution.py:46
  189.9 12.6 %collective-permute-start.17 = (bf16[2,1024,128]{2,1,0:T(8,128)(2,1)}, bf16[2,1024,128]{2,1,0:T(8,128)(2,1)}, u32[]{:S(2)}, u32[]{:S(2)}) collective-permute-start(bf16[2,1024,128]{2,1,0:T(8,128)(2,1)} %get-tuple-element.45), channel_id=1, source_target_pairs={{0,64},{4,20},{8,72},{12,28},{16,80},{20,4},{24,88},{28,12},{32,96... | collective-permute-start | bytes 1572872 | tf_op jit(solution)/shard_map/ppermute | solution.py:46
  189.9 16.3 %collective-permute-start.16 = (bf16[2,1024,128]{2,1,0:T(8,128)(2,1)}, bf16[2,1024,128]{2,1,0:T(8,128)(2,1)}, u32[]{:S(2)}, u32[]{:S(2)}) collective-permute-start(bf16[2,1024,128]{2,1,0:T(8,128)(2,1)} %get-tuple-element.46), channel_id=1, source_target_pairs={{0,32},{4,12},{8,40},{12,20},{16,48},{20,28},{24,56},{28,4},{32,64... | collective-permute-start | bytes 1572872 | tf_op jit(solution)/shard_map/ppermute | solution.py:46
  192.5 16.0 %copy-start.7 = (f32[1024,128]{1,0:T(8,128)S(1)}, f32[1024,128]{1,0:T(8,128)}, u32[]{:S(2)}) copy-start(f32[1024,128]{1,0:T(8,128)} %get-tuple-element.23) | copy-start | bytes 1572868
  192.5 16.0 %copy-start.8 = (f32[1024,128]{1,0:T(8,128)S(1)}, f32[1024,128]{1,0:T(8,128)}, u32[]{:S(2)}) copy-start(f32[1024,128]{1,0:T(8,128)} %get-tuple-element.24) | copy-start | bytes 1572868

commit v2 on v1

--- a/solution.py
+++ b/solution.py
@@ -12,8 +12,8 @@
 QB = 128
 SIDE = 4
 TILE = 256
+UNROLL = 2
 OWN_TILE = 512
-PIECES = 2
 VMEM_LIMIT = 60 * 1024 * 1024
 LOG2E = math.log2(math.e)
 
@@ -120,29 +120,25 @@
     )(packed, packed, stats, keys, values)
 
 
-def remote_kernel(scale2, bases, fresh, tbl, *refs):
-    sources = len(bases) * PIECES
-    q0, g0, q1, g1, st0, st1, in0 = refs[:7]
-    rest = refs[7:]
-    if not fresh:
-        in1, rest = rest[0], rest[1:]
-    blocks = rest[:sources]
-    dq0, dq1 = rest[sources : sources + 2]
-    outs = rest[sources + 2 : -1]
-    buf = rest[-1]
+def remote_kernel(scale2, bases, offsets, tbl, *refs):
+    sources = len(offsets) - 1
+    q0, g0, q1, g1, st0, st1 = refs[:6]
+    blocks = refs[6 : 6 + sources]
+    out0, out1 = refs[6 + sources : 8 + sources]
+    outs = refs[8 + sources : -3]
+    buf, dq0, dq1 = refs[-3:]
     at = pl.program_id(0)
     heads = q0.shape[0]
     rows = heads * QB
-    span = SIDE // PIECES
 
     @pl.when(at == 0)
     def _():
-        dq0[...] = in0[...]
-        dq1[...] = jnp.zeros_like(dq1) if fresh else in1[...]
+        dq0[...] = jnp.zeros_like(dq0)
+        dq1[...] = jnp.zeros_like(dq1)
 
     for i, block_ref in enumerate(blocks):
 
-        @pl.when(at // span == i)
+        @pl.when((at >= offsets[i]) & (at < offsets[i + 1]))
         def _():
             buf[...] = block_ref[0]
 
@@ -164,21 +160,24 @@
 
     def run(sides):
         loaded = [load(block, *side[:3]) for block, side in sides]
-        total = [None] * len(sides)
-        for tile in range(buf.shape[1] // TILE):
-            where = pl.ds(tile * TILE, TILE)
-            keys, values = buf[0, where, :], buf[1, where, :]
-            dk_sum, dv_sum = None, None
-            for i, (q, g, lse, delta) in enumerate(loaded):
-                dk, dv, dq = tile_grads(keys, values, q, g, lse, delta, scale2)
-                dk_sum = dk if dk_sum is None else dk_sum + dk
-                dv_sum = dv if dv_sum is None else dv_sum + dv
-                total[i] = dq if total[i] is None else total[i] + dq
-            buf[0, where, :] = dk_sum.astype(jnp.bfloat16)
-            buf[1, where, :] = dv_sum.astype(jnp.bfloat16)
-        for (block, side), dq in zip(sides, total):
-            where = pl.ds(pl.multiple_of(block * QB, QB), QB)
-            side[3][:, where, :] += dq.reshape(heads, QB, -1)
+
+        @pl.loop(0, buf.shape[1] // (UNROLL * TILE))
+        def _(turn):
+            total = [None] * len(sides)
+            for tile in range(UNROLL):
+                where = pl.ds(pl.multiple_of((turn * UNROLL + tile) * TILE, TILE), TILE)
+                keys, values = buf[0, where, :], buf[1, where, :]
+                dk_sum, dv_sum = None, None
+                for i, (q, g, lse, delta) in enumerate(loaded):
+                    dk, dv, dq = tile_grads(keys, values, q, g, lse, delta, scale2)
+                    dk_sum = dk if dk_sum is None else dk_sum + dk
+                    dv_sum = dv if dv_sum is None else dv_sum + dv
+                    total[i] = dq if total[i] is None else total[i] + dq
+                buf[0, where, :] = dk_sum.astype(jnp.bfloat16)
+                buf[1, where, :] = dv_sum.astype(jnp.bfloat16)
+            for (block, side), dq in zip(sides, total):
+                where = pl.ds(pl.multiple_of(block * QB, QB), QB)
+                side[3][:, where, :] += dq.reshape(heads, QB, -1)
 
     own_side = (own, (q0, g0, st0, dq0))
     sib_side = (sib, (q1, g1, st1, dq1))
@@ -205,46 +204,56 @@
         def _():
             out_ref[0] = buf[...]
 
-
-def remote_grads(table, own, sib, stats, sources, bases, carried, scale2):
+    @pl.when(at == pl.num_programs(0) - 1)
+    def _():
+        out0[...] = dq0[...].astype(out0.dtype)
+        out1[...] = dq1[...].astype(out1.dtype)
+
+
+def remote_grads(table, own, sib, stats, groups, bases, scale2):
     heads, _, width = own.shape
     rows = stats[0].shape[0] * QB
     count = len(bases)
-    span = SIDE // PIECES
     once = pl.Buffered(1)
     q_spec = pl.BlockSpec((heads, rows, width), lambda k, t: (0, 0, 0), pipeline_mode=once)
     g_spec = pl.BlockSpec((heads, rows, width), lambda k, t: (0, 1, 0), pipeline_mode=once)
     stat = pl.BlockSpec(stats[0].shape, lambda k, t: (0, 0, 0))
     acc_spec = pl.BlockSpec((heads, rows, width), lambda k, t: (0, 0, 0))
 
-    def piece(size, i):
+    def piece(start, size):
         return pl.BlockSpec(
-            (1, 2, rows, width), lambda k, t: (jnp.clip(k - size * i, 0, size - 1), 0, 0, 0)
+            (1, 2, rows, width), lambda k, t: (jnp.clip(k - start, 0, size - 1), 0, 0, 0)
         )
 
-    operands = [array for source in sources for array in source]
-    acc = jax.ShapeDtypeStruct((heads, rows, width), jnp.float32)
+    operands = [array for group in groups for array in group]
+    offsets = [0]
+    for array in operands:
+        offsets.append(offsets[-1] + array.shape[0])
+    acc = jax.ShapeDtypeStruct((heads, rows, width), jnp.bfloat16)
     part = jax.ShapeDtypeStruct((SIDE, 2, rows, width), jnp.bfloat16)
     return pl.pallas_call(
-        functools.partial(remote_kernel, scale2, bases, len(carried) == 1),
+        functools.partial(remote_kernel, scale2, bases, offsets),
         grid_spec=pltpu.PrefetchScalarGridSpec(
             num_scalar_prefetch=1,
             grid=(SIDE * count,),
             in_specs=[q_spec, g_spec, q_spec, g_spec, stat, stat]
-            + [q_spec] * len(carried)
-            + [piece(span, i) for i in range(len(operands))],
-            out_specs=[acc_spec, acc_spec] + [piece(SIDE, i) for i in range(count)],
-            scratch_shapes=[pltpu.VMEM((2, rows, width), jnp.bfloat16)],
+            + [piece(start, array.shape[0]) for start, array in zip(offsets, operands)],
+            out_specs=[acc_spec, acc_spec] + [piece(SIDE * i, SIDE) for i in range(count)],
+            scratch_shapes=[
+                pltpu.VMEM((2, rows, width), jnp.bfloat16),
+                pltpu.VMEM((heads, rows, width), jnp.float32),
+                pltpu.VMEM((heads, rows, width), jnp.float32),
+            ],
         ),
         out_shape=[acc, acc] + [part] * count,
         compiler_params=pltpu.CompilerParams(vmem_limit_bytes=VMEM_LIMIT),
         cost_estimate=pl.CostEstimate(
             flops=SIDE * count * 10 * heads * QB * rows * width,
-            bytes_accessed=(12 + 4 * count) << 20,
+            bytes_accessed=(8 + 4 * count) << 20,
             transcendentals=0,
         ),
         name="remote",
-    )(table, own, own, sib, sib, *stats, *carried, *operands)
+    )(table, own, own, sib, sib, *stats, *operands)
 
 
 def split3(value):
@@ -271,12 +280,13 @@
     behind = shift(both, 0, 1)
     ahead = shift(both, 0, -1)
     across = shift(both, 0, 2)
-    first = jnp.stack([both, behind])
-    second = jnp.stack([across, ahead])
-    line = (first, second)
-    line_behind = (shift(first, 1, 1), shift(second, 1, 1))
-    line_ahead = (shift(first, 1, -1), shift(second, 1, -1))
-    line_across = (shift(line_behind[0], 1, 1), shift(line_ahead[1], 1, -1))
+    sides = jnp.stack([behind, ahead])
+    line = (both[None], sides, across[None])
+    line_behind = tuple(shift(piece, 1, 1) for piece in line)
+    line_ahead = tuple(shift(piece, 1, -1) for piece in line)
+    line_across = (
+        shift(line_behind[0], 1, 1), shift(line_ahead[1], 1, -1), shift(line_behind[2], 1, 1)
+    )
 
     def turn(value):
         return lax.all_to_all(value, "head", split_axis=0, concat_axis=0, tiled=True)
@@ -305,6 +315,7 @@
 
     index = jnp.arange(SIDE * SIDE, dtype=jnp.int32)
     near, far = index % SIDE, index // SIDE
+    near = jnp.where(near >= 2, 5 - near, near)
     back_x, back_z = jnp.where(core == 0, near, far), jnp.where(core == 0, far, near)
     source = (((x - back_x) % SIDE) * SIDE + (z - back_z) % SIDE) * 2 + core
 
@@ -314,39 +325,37 @@
 
     table = jnp.concatenate([listed(selections, me), listed(sib_selections, me + 1 - 2 * core)])
 
-    def remote(sources, bases, carried):
-        return remote_grads(
-            table, own, sib, (own_stats, sib_stats), sources, bases, carried, scale2
-        )
-
-    own_q, own_k, own_v = own_grads(own, own_stats, keys, values, scale2)
-    dq0, dq1, part_behind, part_ahead = remote(
-        [line_behind, line_ahead], (SIDE, 3 * SIDE), (own_q,)
-    )
+    def remote(groups, bases):
+        return remote_grads(table, own, sib, (own_stats, sib_stats), groups, bases, scale2)
+
+    level0, level1, part_line = remote([line], (0,))
+    first0, first1, part_behind, part_ahead = remote([line_behind, line_ahead], (SIDE, 3 * SIDE))
     back_behind = shift(part_behind, 1, -1)
     back_ahead = shift(part_ahead, 1, 1)
-    dq0, dq1, part_across, part_line = remote(
-        [line_across, line], (2 * SIDE, 0), (dq0, dq1)
-    )
+    second0, second1, part_across = remote([line_across], (2 * SIDE,))
     back_across = shift(part_across, 1, 2)
+    own_q, own_k, own_v = own_grads(own, own_stats, keys, values, scale2)
+
+    def summed(*parts):
+        return sum(part.astype(jnp.float32) for part in parts)
 
     total = [
-        sum(part[i].astype(jnp.float32) for part in (part_line, back_behind, back_ahead, back_across))
+        summed(part_line[i], back_behind[i], back_ahead[i], back_across[i])
         for i in range(SIDE)
     ]
     low = [part.astype(jnp.bfloat16) for part in total[1:]]
     near_sum = (
         total[0]
         + shift(low[0], 0, -1).astype(jnp.float32)
-        + shift(low[2], 0, 1).astype(jnp.float32)
-        + shift(low[1], 0, 2).astype(jnp.float32)
+        + shift(low[1], 0, 1).astype(jnp.float32)
+        + shift(low[2], 0, 2).astype(jnp.float32)
     )
     grad_k = ((near_sum[0] + own_k) * scale).astype(jnp.bfloat16)
     grad_v = (near_sum[1] + own_v).astype(jnp.bfloat16)
 
-    dq_low = dq1.astype(jnp.bfloat16)
+    dq_low = summed(level1, first1, second1).astype(jnp.bfloat16)
     returned = other_core(dq_low)
-    dq = ((dq0 + returned.astype(jnp.float32)) * scale).astype(jnp.bfloat16)
+    dq = ((own_q + summed(level0, first0, second0, returned)) * scale).astype(jnp.bfloat16)
     dq = jnp.transpose(turn(dq), (1, 0, 2))[:, :, None]
     return dq, grad_k[:, None], grad_v[:, None]
 

time: 210 us -> 213 us (1.014)
  the two profiles are of different devices: /device:TPU:0 before, /device:TPU:8 now
where the time goes in v2:
time: 213 us
  starting transfers between devices  69.3 us (33%)
  waiting for transfers between devices  68.5 us (32%)
  Pallas kernels  42.9 us (20%)
  other arithmetic  21.9 us (10%)
  local copies, waits for them, and re-layouts  9.21 us (4%)
    ppermute x18, waiting for transfers between devices, shift(): return lax.ppermute(value, 'ctx', pairs(place))  49.6 us
    ppermute x18, starting transfers between devices, shift(): return lax.ppermute(value, 'ctx', pairs(place))  47.3 us
    pallas_call x3, Pallas kernels, remote_grads(): pl.pallas_call(functools.partial(remote_kernel, scale2, bases, offsets),...  27.7 us
    all_to_all x2, waiting for transfers between devices, turn(): lax.all_to_all(value, 'head', split_axis=0, concat_axis=0, tiled=True)  18.8 us
    pallas_call x1, Pallas kernels, own_grads(): pl.pallas_call(functools.partial(own_kernel, scale2), grid=(blocks,), in_...  15.2 us
    ppermute x3, starting transfers between devices, other_core(): lax.ppermute(value, 'ctx', pairs(lambda x, z, core: (x, z, 1 - core)))  12.1 us
    all_to_all x2, starting transfers between devices, turn(): lax.all_to_all(value, 'head', split_axis=0, concat_axis=0, tiled=True)  9.9 us
  transfers between devices with their start and end apart: 23, of which 8 were waited for; matrix products, arithmetic and copies ran while one was open for 9% of the time, Pallas kernels for 20%

profile of v2, /device:TPU:8, one launch (start us, length us, event | category | flops | bytes accessed | tf_op | source)
XLA Modules:
  0.0 212.7 jit_solution(15691547130092547698)
XLA Ops:
  0.6 0.0 copy-start.1
  0.6 0.8 fusion.16
  1.5 2.7 %multiply_reduce_fusion = f32[1024,4]{1,0:T(8,128)S(1)} fusion(bf16[1024,4,1,128]{3,1,2,0:T(4,128)(2,1)} %param.11, bf16[1024,4,1,128]{3,1,2,0:T(4,128)(2,1)} %param.10), kind=kLoop, calls=%fused_computation.3 | loop fusion | flops 2093056 | bytes 2113536 | tf_op jit(solution)/shard_map/reduce_sum | solution.py:294
  4.2 0.2 copy.62
  4.5 0.1 reshape.227
  4.6 1.5 copy_bitcast_fusion
  6.1 1.5 pad_maximum_fusion
  7.6 4.9 %all-to-all-start = ((bf16[4,2096,128]{2,1,0:T(8,128)(2,1)}), bf16[4,2096,128]{2,1,0:T(8,128)(2,1)S(1)}, u32[]{:S(2)}, u32[]{:S(2)}) async-start(bf16[4,2096,128]{2,1,0:T(8,128)(2,1)} %pad_maximum_fusion), calls=%async_computation | async-start | bytes 4292608 | tf_op jit(solution)/shard_map/all_to_all | solution.py:292
  12.5 2.6 %constant_dynamic-slice_fusion = (bf16[1024,1,128]{2,1,0:T(2,128)(2,1)S(1)}, bf16[1024,1,128]{2,1,0:T(2,128)(2,1)S(1)}) fusion(bf16[1024,4,128]{2,1,0:T(4,128)(2,1)} %param.9, s32[]{:T(128)S(6)} %select_n.140, bf16[1024,4,128]{2,1,0:T(4,128)(2,1)} %param.8), kind=kLoop, calls=%fused_computation.73 | loop fusion | bytes 1048580 | tf_op jit(solution)/shard_map/jit(dynamic_index_in_dim)/dynamic_slice | solution.py:278
  15.2 1.1 pad_maximum_fusion.2
  16.3 2.8 %collective-permute-start.3 = (bf16[2,1024,128]{2,1,0:T(8,128)(2,1)}, bf16[2,1024,128]{2,1,0:T(8,128)(2,1)S(1)}, u32[]{:S(2)}, u32[]{:S(2)}) collective-permute-start(bf16[2,1024,128]{2,1,0:T(8,128)(2,1)} %get-tuple-element.53), channel_id=1, source_target_pairs={{0,96},{4,28},{8,104},{12,4},{16,112},{20,12},{24,120},{28,20},{32... | collective-permute-start | bytes 1572872 | tf_op jit(solution)/shard_map/ppermute | solution.py:46
  19.1 18.8 %all-to-all-done.q_ref.g_ref.refs_0_.refs_1_ = bf16[4,2096,128]{2,1,0:T(8,128)(2,1)S(1)} async-done(((bf16[4,2096,128]{2,1,0:T(8,128)(2,1)}), bf16[4,2096,128]{2,1,0:T(8,128)(2,1)S(1)}, u32[]{:S(2)}, u32[]{:S(2)}) %all-to-all-start) | async-done | bytes 2146336 | tf_op jit(solution)/shard_map/all_to_all | solution.py:292
  37.9 0.8 copy-done.13
  38.7 1.3 pad_maximum_fusion.1.refs_7_
  40.1 4.1 %collective-permute-start.9 = (bf16[2,2,1024,128]{3,2,1,0:T(8,128)(2,1)S(1)}, bf16[2,2,1024,128]{3,2,1,0:T(8,128)(2,1)}, u32[]{:S(2)}, u32[]{:S(2)}) collective-permute-start(bf16[2,2,1024,128]{3,2,1,0:T(8,128)(2,1)S(1)} %pad_maximum_fusion.1.refs_7_), channel_id=1, source_target_pairs={{0,24},{4,100},{8,0},{12,108},{16,8},{20,116},{24,16},{28,124},{32... | collective-permute-start | bytes 3145736 | tf_op jit(solution)/shard_map/ppermute | solution.py:46
  44.2 3.0 %collective-permute-start.4 = (bf16[2,1024,128]{2,1,0:T(8,128)(2,1)}, bf16[2,1024,128]{2,1,0:T(8,128)(2,1)}, u32[]{:S(2)}, u32[]{:S(2)}) collective-permute-start(bf16[2,1024,128]{2,1,0:T(8,128)(2,1)} %get-tuple-element.53), channel_id=1, source_target_pairs={{0,64},{4,20},{8,72},{12,28},{16,80},{20,4},{24,88},{28,12},{32,96... | collective-permute-start | bytes 1572872 | tf_op jit(solution)/shard_map/ppermute | solution.py:46
  47.2 0.5 collective-permute-start.5
  47.7 12.0 %collective-permute-done.4 = bf16[2,1024,128]{2,1,0:T(8,128)(2,1)} collective-permute-done((bf16[2,1024,128]{2,1,0:T(8,128)(2,1)}, bf16[2,1024,128]{2,1,0:T(8,128)(2,1)}, u32[]{:S(2)}, u32[]{:S(2)}) %collective-permute-start.4) | collective-permute-done | bytes 524320 | tf_op jit(solution)/shard_map/ppermute | solution.py:46
  59.8 2.4 %collective-permute-done.9.refs_10_ = bf16[2,2,1024,128]{3,2,1,0:T(8,128)(2,1)} collective-permute-done((bf16[2,2,1024,128]{3,2,1,0:T(8,128)(2,1)S(1)}, bf16[2,2,1024,128]{3,2,1,0:T(8,128)(2,1)}, u32[]{:S(2)}, u32[]{:S(2)}) %collective-permute-start.9) | collective-permute-done | bytes 1048608 | tf_op jit(solution)/shard_map/ppermute | solution.py:46
  62.1 3.8 %collective-permute-start.12 = (bf16[2,2,1024,128]{3,2,1,0:T(8,128)(2,1)}, bf16[2,2,1024,128]{3,2,1,0:T(8,128)(2,1)}, u32[]{:S(2)}, u32[]{:S(2)}) collective-permute-start(bf16[2,2,1024,128]{3,2,1,0:T(8,128)(2,1)} %collective-permute-done.9.refs_10_), channel_id=1, source_target_pairs={{0,24},{4,100},{8,0},{12,108},{16,8},{20,116},{24,16},{28,124},{32... | collective-permute-start | bytes 3145736 | tf_op jit(solution)/shard_map/ppermute | solution.py:46
  65.9 0.1 select_reduce_fusion.1
  66.0 0.1 collective-permute-start.11
  66.1 0.6 pad_add_fusion.tbl
  66.7 3.7 %collective-permute-done.7.refs_8_ = bf16[1,2,1024,128]{3,2,1,0:T(8,128)(2,1)} collective-permute-done((bf16[1,2,1024,128]{3,2,1,0:T(8,128)(2,1)}, bf16[1,2,1024,128]{3,2,1,0:T(8,128)(2,1)}, u32[]{:S(2)}, u32[]{:S(2)}) %collective-permute-start.7) | collective-permute-done | bytes 524320 | tf_op jit(solution)/shard_map/ppermute | solution.py:46
  70.5 0.6 reshape.228.st_ref.refs_4_
  71.1 3.2 %collective-permute-start.8 = (bf16[1,2,1024,128]{3,2,1,0:T(8,128)(2,1)}, bf16[1,2,1024,128]{3,2,1,0:T(8,128)(2,1)}, u32[]{:S(2)}, u32[]{:S(2)}) collective-permute-start(bf16[1,2,1024,128]{3,2,1,0:T(8,128)(2,1)} %get-tuple-element.54.refs_6_), channel_id=1, source_target_pairs={{0,24},{4,100},{8,0},{12,108},{16,8},{20,116},{24,16},{28,124},{32... | collective-permute-start | bytes 1572872 | tf_op jit(solution)/shard_map/ppermute | solution.py:46
  74.4 0.8 slice.124
  75.2 1.7 collective-permute-done.11.refs_6_
  76.9 0.6 reshape.229.refs_5_
  77.5 16.2 %collective-permute-done.13.refs_8_ = bf16[1,2,1024,128]{3,2,1,0:T(8,128)(2,1)} collective-permute-done((bf16[1,2,1024,128]{3,2,1,0:T(8,128)(2,1)}, bf16[1,2,1024,128]{3,2,1,0:T(8,128)(2,1)}, u32[]{:S(2)}, u32[]{:S(2)}) %collective-permute-start.13) | collective-permute-done | bytes 524320 | tf_op jit(solution)/shard_map/ppermute | solution.py:46
  93.7 7.5 %remote.5 = (bf16[4,1024,128]{2,1,0:T(8,128)(2,1)}, bf16[4,1024,128]{2,1,0:T(8,128)(2,1)}, bf16[4,2,1024,128]{3,2,1,0:T(8,128)(2,1)}) custom-call(s32[32]{0:T(128)} %pad_add_fusion.tbl, bf16[4,2096,128]{2,1,0:T(8,128)(2,1)} %copy-done, bf16[4,2096,128]{2,1,0:T(8,128)(2,1)} %copy-done, bf16[4,2096,128]{2,1,0:T(8,128)(2,1)} %collective-permute-done.1.refs_2_.refs_3_, ...), custom_call_target="tpu_custom_call" | custom-call | flops 2684354560 | bytes 12582912 | tf_op jit(solution)/shard_map/remote/pallas_call | solution.py:234
  101.1 2.2 %collective-permute-start.17 = (bf16[4,2,1024,128]{3,2,1,0:T(8,128)(2,1)}, bf16[4,2,1024,128]{3,2,1,0:T(8,128)(2,1)}, u32[]{:S(2)}, u32[]{:S(2)}) collective-permute-start(bf16[4,2,1024,128]{3,2,1,0:T(8,128)(2,1)} %get-tuple-element.26), channel_id=1, source_target_pairs={{0,16},{4,68},{8,24},{12,76},{16,0},{20,84},{24,8},{28,92},{32,48}... | collective-permute-start | bytes 6291464 | tf_op jit(solution)/shard_map/ppermute | solution.py:46
  103.4 10.4 %remote.4 = (bf16[4,1024,128]{2,1,0:T(8,128)(2,1)}, bf16[4,1024,128]{2,1,0:T(8,128)(2,1)}, bf16[4,2,1024,128]{3,2,1,0:T(8,128)(2,1)}, bf16[4,2,1024,128]{3,2,1,0:T(8,128)(2,1)}) custom-call(s32[32]{0:T(128)} %pad_add_fusion.tbl, bf16[4,2096,128]{2,1,0:T(8,128)(2,1)} %copy-done, bf16[4,2096,128]{2,1,0:T(8,128)(2,1)} %copy-done, ...), custom_call_target="tpu_custom_call" | custom-call | flops 5368709120 | bytes 16777216 | tf_op jit(solution)/shard_map/remote/pallas_call | solution.py:234
  113.7 10.0 %collective-permute-start.15 = (bf16[4,2,1024,128]{3,2,1,0:T(8,128)(2,1)}, bf16[4,2,1024,128]{3,2,1,0:T(8,128)(2,1)}, u32[]{:S(2)}, u32[]{:S(2)}) collective-permute-start(bf16[4,2,1024,128]{3,2,1,0:T(8,128)(2,1)} %get-tuple-element.24), channel_id=1, source_target_pairs={{0,24},{4,100},{8,0},{12,108},{16,8},{20,116},{24,16},{28,124},{32... | collective-permute-start | bytes 6291464 | tf_op jit(solution)/shard_map/ppermute | solution.py:46
  123.7 9.9 %remote.3 = (bf16[4,1024,128]{2,1,0:T(8,128)(2,1)}, bf16[4,1024,128]{2,1,0:T(8,128)(2,1)}, bf16[4,2,1024,128]{3,2,1,0:T(8,128)(2,1)}) custom-call(s32[32]{0:T(128)} %pad_add_fusion.tbl, bf16[4,2096,128]{2,1,0:T(8,128)(2,1)} %copy-done, bf16[4,2096,128]{2,1,0:T(8,128)(2,1)} %copy-done, bf16[4,2096,128]{2,1,0:T(8,128)(2,1)} %collective-permute-done.1.refs_2_.refs_3_, ...), custom_call_target="tpu_custom_call" | custom-call | flops 2684354560 | bytes 12582912 | tf_op jit(solution)/shard_map/remote/pallas_call | solution.py:234
  133.6 2.6 %add_convert_fusion = bf16[4,1024,128]{2,1,0:T(8,128)(2,1)} fusion(bf16[4,1024,128]{2,1,0:T(8,128)(2,1)S(1)} %copy-done.9, bf16[4,1024,128]{2,1,0:T(8,128)(2,1)S(1)} %copy-done.10, bf16[4,1024,128]{2,1,0:T(8,128)(2,1)} %get-tuple-element.20), kind=kLoop, calls=%fused_computation.2 | loop fusion | flops 3145728 | bytes 4194304 | tf_op jit(solution)/shard_map/convert_element_type | solution.py:356
  136.2 12.1 %collective-permute-start.14 = (bf16[4,1024,128]{2,1,0:T(8,128)(2,1)}, bf16[4,1024,128]{2,1,0:T(8,128)(2,1)}, u32[]{:S(2)}, u32[]{:S(2)}) collective-permute-start(bf16[4,1024,128]{2,1,0:T(8,128)(2,1)} %add_convert_fusion), channel_id=1, source_target_pairs={{0,4},{4,0},{8,12},{12,8},{16,20},{20,16},{24,28},{28,24},{32,36},... | collective-permute-start | bytes 3145736 | tf_op jit(solution)/shard_map/ppermute | solution.py:50
  148.3 15.2 %own.1 = (f32[4,1024,128]{2,1,0:T(8,128)}, f32[1024,128]{1,0:T(8,128)}, f32[1024,128]{1,0:T(8,128)}) custom-call(bf16[4,2096,128]{2,1,0:T(8,128)(2,1)} %copy-done, bf16[4,2096,128]{2,1,0:T(8,128)(2,1)} %copy-done, f32[8,2,512]{2,1,0:T(2,128)} %reshape.228.st_ref.refs_4_, bf16[1024,128]{1,0:T(8,128)(2,1)} %bitcast.90, bf16[1024,128]{1,0:T(8,128)(2,1)} %bitcast.88), custom_call_target="tpu_custom_call" | custom-call | flops 3221225472 | bytes 8388608 | tf_op jit(solution)/shard_map/own/pallas_call | solution.py:109
  163.6 3.5 %multiply_convert_fusion = bf16[4,1024,128]{2,1,0:T(8,128)(2,1)} fusion(f32[4,1024,128]{2,1,0:T(8,128)} %get-tuple-element.16, bf16[4,1024,128]{2,1,0:T(8,128)(2,1)} %collective-permute-done.14, bf16[4,1024,128]{2,1,0:T(8,128)(2,1)S(1)} %copy-done.4, bf16[4,1024,128]{2,1,0:T(8,128)(2,1)S(1)} %copy-done.5, bf16[4,1024,128]{2,1,0:T(8,128)(2,1)S(1)} %copy-done.6), kind=kLoop, calls=%fused_computation.1 | loop fusion | flops 5242880 | bytes 7340032 | tf_op jit(solution)/shard_map/convert_element_type | solution.py:358
  167.1 5.0 %all-to-all-start.1 = ((bf16[4,1024,128]{2,1,0:T(8,128)(2,1)}), bf16[4,1024,128]{2,1,0:T(8,128)(2,1)S(1)}, u32[]{:S(2)}, u32[]{:S(2)}) async-start(bf16[4,1024,128]{2,1,0:T(8,128)(2,1)} %multiply_convert_fusion), calls=%async_computation.1 | async-start | bytes 2097152 | tf_op jit(solution)/shard_map/all_to_all | solution.py:292
  172.1 4.2 %fusion.2 = (bf16[2,1024,128]{2,1,0:T(8,128)(2,1)}, bf16[2,1024,128]{2,1,0:T(8,128)(2,1)}, bf16[2,1024,128]{2,1,0:T(8,128)(2,1)}) fusion(bf16[4,2,1024,128]{3,2,1,0:T(8,128)(2,1)} %collective-permute-done.17, bf16[4,2,1024,128]{3,2,1,0:T(8,128)(2,1)} %collective-permute-done.16, bf16[4,2,1024,128]{3,2,1,0:T(8,128)(2,1)} %collective-permute-done.15, ...), kind=kLoop, calls=%fused_computation.13 | loop fusion | flops 6291456 | bytes 7864320 | tf_op jit(solution)/shard_map/add | solution.py:340
  176.3 16.9 %collective-permute-start.18 = (bf16[2,1024,128]{2,1,0:T(8,128)(2,1)}, bf16[2,1024,128]{2,1,0:T(8,128)(2,1)}, u32[]{:S(2)}, u32[]{:S(2)}) collective-permute-start(bf16[2,1024,128]{2,1,0:T(8,128)(2,1)} %get-tuple-element.48), channel_id=1, source_target_pairs={{0,96},{4,28},{8,104},{12,4},{16,112},{20,12},{24,120},{28,20},{32... | collective-permute-start | bytes 1572872 | tf_op jit(solution)/shard_map/ppermute | solution.py:46
  193.1 0.9 collective-permute-start.19
  194.0 1.8 copy.72
  195.8 10.0 %collective-permute-done.18 = bf16[2,1024,128]{2,1,0:T(8,128)(2,1)} collective-permute-done((bf16[2,1024,128]{2,1,0:T(8,128)(2,1)}, bf16[2,1024,128]{2,1,0:T(8,128)(2,1)}, u32[]{:S(2)}, u32[]{:S(2)}) %collective-permute-start.18) | collective-permute-done | bytes 524320 | tf_op jit(solution)/shard_map/ppermute | solution.py:46
  205.8 3.7 %collective-permute-done.19 = bf16[2,1024,128]{2,1,0:T(8,128)(2,1)} collective-permute-done((bf16[2,1024,128]{2,1,0:T(8,128)(2,1)}, bf16[2,1024,128]{2,1,0:T(8,128)(2,1)}, u32[]{:S(2)}, u32[]{:S(2)}) %collective-permute-start.19) | collective-permute-done | bytes 524320 | tf_op jit(solution)/shard_map/ppermute | solution.py:46
  209.5 2.3 %fusion.1 = f32[2,1024,128]{2,1,0:T(8,128)S(1)} fusion(bf16[2,1024,128]{2,1,0:T(8,128)(2,1)} %collective-permute-done.20, bf16[2,1024,128]{2,1,0:T(8,128)(2,1)} %collective-permute-done.19, bf16[2,1024,128]{2,1,0:T(8,128)(2,1)} %collective-permute-done.18, bf16[4,2,1024,128]{3,2,1,0:T(8,128)(2,1)} %collective-permute-done.17, ...), kind=kLoop, calls=%fused_computation.7 | loop fusion | flops 3407872 | bytes 4718592 | tf_op jit(solution)/shard_map/add | solution.py:348
  211.8 1.0 fusion.11
  (66 shorter events, 0.4 us)
Async XLA Ops:
  0.6 3.9 %copy-start.1 = (bf16[1024,4,1,128]{3,1,2,0:T(4,128)(2,1)S(1)}, bf16[1024,4,1,128]{3,1,2,0:T(4,128)(2,1)}, u32[]{:S(2)}) copy-start(bf16[1024,4,1,128]{3,1,2,0:T(4,128)(2,1)} %param.10) | copy-start | bytes 3145732
  7.6 30.3 %all-to-all-start = ((bf16[4,2096,128]{2,1,0:T(8,128)(2,1)}), bf16[4,2096,128]{2,1,0:T(8,128)(2,1)S(1)}, u32[]{:S(2)}, u32[]{:S(2)}) async-start(bf16[4,2096,128]{2,1,0:T(8,128)(2,1)} %pad_maximum_fusion), calls=%async_computation | async-start | bytes 4292608 | tf_op jit(solution)/shard_map/all_to_all | solution.py:292
  15.2 24.9 %copy-start.7 = (bf16[1024,1,128]{2,0,1:T(8,128)(2,1)}, bf16[1024,1,128]{2,0,1:T(8,128)(2,1)S(1)}, u32[]{:S(2)}) copy-start(bf16[1024,1,128]{2,0,1:T(8,128)(2,1)S(1)} %copy.104) | copy-start | bytes 786436
  15.2 32.1 %copy-start.14 = (s32[8,3]{0,1:T(4,128)S(1)}, s32[8,3]{0,1:T(4,128)}, u32[]{:S(2)}) copy-start(s32[8,3]{0,1:T(4,128)} %param.13) | copy-start | bytes 292
  15.2 22.7 %copy-start.8 = (bf16[1024,1,128]{2,0,1:T(8,128)(2,1)}, bf16[1024,1,128]{2,0,1:T(8,128)(2,1)S(1)}, u32[]{:S(2)}) copy-start(bf16[1024,1,128]{2,0,1:T(8,128)(2,1)S(1)} %copy.105) | copy-start | bytes 786436
  16.3 21.6 %collective-permute-start.3 = (bf16[2,1024,128]{2,1,0:T(8,128)(2,1)}, bf16[2,1024,128]{2,1,0:T(8,128)(2,1)S(1)}, u32[]{:S(2)}, u32[]{:S(2)}) collective-permute-start(bf16[2,1024,128]{2,1,0:T(8,128)(2,1)} %get-tuple-element.53), channel_id=1, source_target_pairs={{0,96},{4,28},{8,104},{12,4},{16,112},{20,12},{24,120},{28,20},{32... | collective-permute-start | bytes 1572872 | tf_op jit(solution)/shard_map/ppermute | solution.py:46
  19.1 18.8 %collective-permute-start.2 = (bf16[2,1024,128]{2,1,0:T(8,128)(2,1)}, bf16[2,1024,128]{2,1,0:T(8,128)(2,1)}, u32[]{:S(2)}, u32[]{:S(2)}) collective-permute-start(bf16[2,1024,128]{2,1,0:T(8,128)(2,1)} %get-tuple-element.53), channel_id=1, source_target_pairs={{0,32},{4,12},{8,40},{12,20},{16,48},{20,28},{24,56},{28,4},{32,64... | collective-permute-start | bytes 1572872 | tf_op jit(solution)/shard_map/ppermute | solution.py:46
  37.9 55.8 %copy-start = (bf16[4,2096,128]{2,1,0:T(8,128)(2,1)}, bf16[4,2096,128]{2,1,0:T(8,128)(2,1)S(1)}, u32[]{:S(2)}) copy-start(bf16[4,2096,128]{2,1,0:T(8,128)(2,1)S(1)} %all-to-all-done.q_ref.g_ref.refs_0_.refs_1_) | copy-start | bytes 6438916
  37.9 33.3 %collective-permute-start.1 = (bf16[4,2096,128]{2,1,0:T(8,128)(2,1)S(1)}, bf16[4,2096,128]{2,1,0:T(8,128)(2,1)}, u32[]{:S(2)}, u32[]{:S(2)}) collective-permute-start(bf16[4,2096,128]{2,1,0:T(8,128)(2,1)S(1)} %all-to-all-done.q_ref.g_ref.refs_0_.refs_1_), channel_id=1, source_target_pairs={{0,4},{4,0},{8,12},{12,8},{16,20},{20,16},{24,28},{28,24},{32,36},... | collective-permute-start | bytes 6438920 | tf_op jit(solution)/shard_map/ppermute | solution.py:50
  37.9 0.8 copy-start.13
  40.1 61.0 %copy-start.2 = (bf16[2,2,1024,128]{3,2,1,0:T(8,128)(2,1)}, bf16[2,2,1024,128]{3,2,1,0:T(8,128)(2,1)S(1)}, u32[]{:S(2)}) copy-start(bf16[2,2,1024,128]{3,2,1,0:T(8,128)(2,1)S(1)} %pad_maximum_fusion.1.refs_7_) | copy-start | bytes 3145732
  40.1 22.0 %collective-permute-start.9 = (bf16[2,2,1024,128]{3,2,1,0:T(8,128)(2,1)S(1)}, bf16[2,2,1024,128]{3,2,1,0:T(8,128)(2,1)}, u32[]{:S(2)}, u32[]{:S(2)}) collective-permute-start(bf16[2,2,1024,128]{3,2,1,0:T(8,128)(2,1)S(1)} %pad_maximum_fusion.1.refs_7_), channel_id=1, source_target_pairs={{0,24},{4,100},{8,0},{12,108},{16,8},{20,116},{24,16},{28,124},{32... | collective-permute-start | bytes 3145736 | tf_op jit(solution)/shard_map/ppermute | solution.py:46
  44.2 15.5 %collective-permute-start.4 = (bf16[2,1024,128]{2,1,0:T(8,128)(2,1)}, bf16[2,1024,128]{2,1,0:T(8,128)(2,1)}, u32[]{:S(2)}, u32[]{:S(2)}) collective-permute-start(bf16[2,1024,128]{2,1,0:T(8,128)(2,1)} %get-tuple-element.53), channel_id=1, source_target_pairs={{0,64},{4,20},{8,72},{12,28},{16,80},{20,4},{24,88},{28,12},{32,96... | collective-permute-start | bytes 1572872 | tf_op jit(solution)/shard_map/ppermute | solution.py:46
  47.2 12.5 %collective-permute-start = (s32[8,3]{0,1:T(4,128)S(1)}, s32[8,3]{0,1:T(4,128)S(1)}, u32[]{:S(2)}, u32[]{:S(2)}) collective-permute-start(s32[8,3]{0,1:T(4,128)S(1)} %copy-done.14), channel_id=1, source_target_pairs={{0,4},{4,0},{8,12},{12,8},{16,20},{20,16},{24,28},{28,24},{32,36},... | collective-permute-start | bytes 296 | tf_op jit(solution)/shard_map/ppermute | solution.py:50
  47.2 18.8 %collective-permute-start.5 = (bf16[1,2,1024,128]{3,2,1,0:T(8,128)(2,1)}, bf16[1,2,1024,128]{3,2,1,0:T(8,128)(2,1)}, u32[]{:S(2)}, u32[]{:S(2)}) collective-permute-start(bf16[1,2,1024,128]{3,2,1,0:T(8,128)(2,1)} %get-tuple-element.54.refs_6_), channel_id=1, source_target_pairs={{0,8},{4,36},{8,16},{12,44},{16,24},{20,52},{24,0},{28,60},{32,40}... | collective-permute-start | bytes 1572872 | tf_op jit(solution)/shard_map/ppermute | solution.py:46
  59.7 10.7 %collective-permute-start.7 = (bf16[1,2,1024,128]{3,2,1,0:T(8,128)(2,1)}, bf16[1,2,1024,128]{3,2,1,0:T(8,128)(2,1)}, u32[]{:S(2)}, u32[]{:S(2)}) collective-permute-start(bf16[1,2,1024,128]{3,2,1,0:T(8,128)(2,1)} %bitcast.24.refs_8_), channel_id=1, source_target_pairs={{0,8},{4,36},{8,16},{12,44},{16,24},{20,52},{24,0},{28,60},{32,40}... | collective-permute-start | bytes 1572872 | tf_op jit(solution)/shard_map/ppermute | solution.py:46
  62.1 31.5 %collective-permute-start.12 = (bf16[2,2,1024,128]{3,2,1,0:T(8,128)(2,1)}, bf16[2,2,1024,128]{3,2,1,0:T(8,128)(2,1)}, u32[]{:S(2)}, u32[]{:S(2)}) collective-permute-start(bf16[2,2,1024,128]{3,2,1,0:T(8,128)(2,1)} %collective-permute-done.9.refs_10_), channel_id=1, source_target_pairs={{0,24},{4,100},{8,0},{12,108},{16,8},{20,116},{24,16},{28,124},{32... | collective-permute-start | bytes 3145736 | tf_op jit(solution)/shard_map/ppermute | solution.py:46
  66.0 10.8 %collective-permute-start.11 = (bf16[1,2,1024,128]{3,2,1,0:T(8,128)(2,1)}, bf16[1,2,1024,128]{3,2,1,0:T(8,128)(2,1)}, u32[]{:S(2)}, u32[]{:S(2)}) collective-permute-start(bf16[1,2,1024,128]{3,2,1,0:T(8,128)(2,1)} %collective-permute-done.5.refs_6_), channel_id=1, source_target_pairs={{0,8},{4,36},{8,16},{12,44},{16,24},{20,52},{24,0},{28,60},{32,40}... | collective-permute-start | bytes 1572872 | tf_op jit(solution)/shard_map/ppermute | solution.py:46
  66.7 36.6 %collective-permute-start.6 = (bf16[2,2,1024,128]{3,2,1,0:T(8,128)(2,1)S(1)}, bf16[2,2,1024,128]{3,2,1,0:T(8,128)(2,1)}, u32[]{:S(2)}, u32[]{:S(2)}) collective-permute-start(bf16[2,2,1024,128]{3,2,1,0:T(8,128)(2,1)S(1)} %pad_maximum_fusion.1.refs_7_), channel_id=1, source_target_pairs={{0,8},{4,36},{8,16},{12,44},{16,24},{20,52},{24,0},{28,60},{32,40}... | collective-permute-start | bytes 3145736 | tf_op jit(solution)/shard_map/ppermute | solution.py:46
  70.4 23.2 %collective-permute-start.13 = (bf16[1,2,1024,128]{3,2,1,0:T(8,128)(2,1)}, bf16[1,2,1024,128]{3,2,1,0:T(8,128)(2,1)}, u32[]{:S(2)}, u32[]{:S(2)}) collective-permute-start(bf16[1,2,1024,128]{3,2,1,0:T(8,128)(2,1)} %collective-permute-done.7.refs_8_), channel_id=1, source_target_pairs={{0,8},{4,36},{8,16},{12,44},{16,24},{20,52},{24,0},{28,60},{32,40}... | collective-permute-start | bytes 1572872 | tf_op jit(solution)/shard_map/ppermute | solution.py:46
  71.1 32.2 %collective-permute-start.8 = (bf16[1,2,1024,128]{3,2,1,0:T(8,128)(2,1)}, bf16[1,2,1024,128]{3,2,1,0:T(8,128)(2,1)}, u32[]{:S(2)}, u32[]{:S(2)}) collective-permute-start(bf16[1,2,1024,128]{3,2,1,0:T(8,128)(2,1)} %get-tuple-element.54.refs_6_), channel_id=1, source_target_pairs={{0,24},{4,100},{8,0},{12,108},{16,8},{20,116},{24,16},{28,124},{32... | collective-permute-start | bytes 1572872 | tf_op jit(solution)/shard_map/ppermute | solution.py:46
  76.8 26.5 %collective-permute-start.10 = (bf16[1,2,1024,128]{3,2,1,0:T(8,128)(2,1)}, bf16[1,2,1024,128]{3,2,1,0:T(8,128)(2,1)}, u32[]{:S(2)}, u32[]{:S(2)}) collective-permute-start(bf16[1,2,1024,128]{3,2,1,0:T(8,128)(2,1)} %bitcast.24.refs_8_), channel_id=1, source_target_pairs={{0,24},{4,100},{8,0},{12,108},{16,8},{20,116},{24,16},{28,124},{32... | collective-permute-start | bytes 1572872 | tf_op jit(solution)/shard_map/ppermute | solution.py:46
  101.1 70.9 %collective-permute-start.17 = (bf16[4,2,1024,128]{3,2,1,0:T(8,128)(2,1)}, bf16[4,2,1024,128]{3,2,1,0:T(8,128)(2,1)}, u32[]{:S(2)}, u32[]{:S(2)}) collective-permute-start(bf16[4,2,1024,128]{3,2,1,0:T(8,128)(2,1)} %get-tuple-element.26), channel_id=1, source_target_pairs={{0,16},{4,68},{8,24},{12,76},{16,0},{20,84},{24,8},{28,92},{32,48}... | collective-permute-start | bytes 6291464 | tf_op jit(solution)/shard_map/ppermute | solution.py:46
  113.7 58.3 %collective-permute-start.15 = (bf16[4,2,1024,128]{3,2,1,0:T(8,128)(2,1)}, bf16[4,2,1024,128]{3,2,1,0:T(8,128)(2,1)}, u32[]{:S(2)}, u32[]{:S(2)}) collective-permute-start(bf16[4,2,1024,128]{3,2,1,0:T(8,128)(2,1)} %get-tuple-element.24), channel_id=1, source_target_pairs={{0,24},{4,100},{8,0},{12,108},{16,8},{20,116},{24,16},{28,124},{32... | collective-permute-start | bytes 6291464 | tf_op jit(solution)/shard_map/ppermute | solution.py:46
  123.7 9.9 %copy-start.9 = (bf16[4,1024,128]{2,1,0:T(8,128)(2,1)S(1)}, bf16[4,1024,128]{2,1,0:T(8,128)(2,1)}, u32[]{:S(2)}) copy-start(bf16[4,1024,128]{2,1,0:T(8,128)(2,1)} %get-tuple-element.22) | copy-start | bytes 3145732
  123.7 9.9 %copy-start.10 = (bf16[4,1024,128]{2,1,0:T(8,128)(2,1)S(1)}, bf16[4,1024,128]{2,1,0:T(8,128)(2,1)}, u32[]{:S(2)}) copy-start(bf16[4,1024,128]{2,1,0:T(8,128)(2,1)} %get-tuple-element.21) | copy-start | bytes 3145732
  123.7 48.4 %collective-permute-start.16 = (bf16[4,2,1024,128]{3,2,1,0:T(8,128)(2,1)}, bf16[4,2,1024,128]{3,2,1,0:T(8,128)(2,1)}, u32[]{:S(2)}, u32[]{:S(2)}) collective-permute-start(bf16[4,2,1024,128]{3,2,1,0:T(8,128)(2,1)} %get-tuple-element.25), channel_id=1, source_target_pairs={{0,8},{4,36},{8,16},{12,44},{16,24},{20,52},{24,0},{28,60},{32,40}... | collective-permute-start | bytes 6291464 | tf_op jit(solution)/shard_map/ppermute | solution.py:46
  136.2 27.3 %collective-permute-start.14 = (bf16[4,1024,128]{2,1,0:T(8,128)(2,1)}, bf16[4,1024,128]{2,1,0:T(8,128)(2,1)}, u32[]{:S(2)}, u32[]{:S(2)}) collective-permute-start(bf16[4,1024,128]{2,1,0:T(8,128)(2,1)} %add_convert_fusion), channel_id=1, source_target_pairs={{0,4},{4,0},{8,12},{12,8},{16,20},{20,16},{24,28},{28,24},{32,36},... | collective-permute-start | bytes 3145736 | tf_op jit(solution)/shard_map/ppermute | solution.py:50
  148.3 15.2 %copy-start.4 = (bf16[4,1024,128]{2,1,0:T(8,128)(2,1)S(1)}, bf16[4,1024,128]{2,1,0:T(8,128)(2,1)}, u32[]{:S(2)}) copy-start(bf16[4,1024,128]{2,1,0:T(8,128)(2,1)} %get-tuple-element.19) | copy-start | bytes 3145732
  148.3 15.3 %copy-start.5 = (bf16[4,1024,128]{2,1,0:T(8,128)(2,1)S(1)}, bf16[4,1024,128]{2,1,0:T(8,128)(2,1)}, u32[]{:S(2)}) copy-start(bf16[4,1024,128]{2,1,0:T(8,128)(2,1)} %get-tuple-element.18) | copy-start | bytes 3145732
  148.3 15.3 %copy-start.6 = (bf16[4,1024,128]{2,1,0:T(8,128)(2,1)S(1)}, bf16[4,1024,128]{2,1,0:T(8,128)(2,1)}, u32[]{:S(2)}) copy-start(bf16[4,1024,128]{2,1,0:T(8,128)(2,1)} %get-tuple-element.17) | copy-start | bytes 3145732
  167.1 5.0 %copy-start.3 = (bf16[4,2,1024,128]{3,2,1,0:T(8,128)(2,1)S(1)}, bf16[4,2,1024,128]{3,2,1,0:T(8,128)(2,1)}, u32[]{:S(2)}) copy-start(bf16[4,2,1024,128]{3,2,1,0:T(8,128)(2,1)} %get-tuple-element.23) | copy-start | bytes 6291460
  167.1 26.9 %all-to-all-start.1 = ((bf16[4,1024,128]{2,1,0:T(8,128)(2,1)}), bf16[4,1024,128]{2,1,0:T(8,128)(2,1)S(1)}, u32[]{:S(2)}, u32[]{:S(2)}) async-start(bf16[4,1024,128]{2,1,0:T(8,128)(2,1)} %multiply_convert_fusion), calls=%async_computation.1 | async-start | bytes 2097152 | tf_op jit(solution)/shard_map/all_to_all | solution.py:292
  176.3 29.5 %collective-permute-start.18 = (bf16[2,1024,128]{2,1,0:T(8,128)(2,1)}, bf16[2,1024,128]{2,1,0:T(8,128)(2,1)}, u32[]{:S(2)}, u32[]{:S(2)}) collective-permute-start(bf16[2,1024,128]{2,1,0:T(8,128)(2,1)} %get-tuple-element.48), channel_id=1, source_target_pairs={{0,96},{4,28},{8,104},{12,4},{16,112},{20,12},{24,120},{28,20},{32... | collective-permute-start | bytes 1572872 | tf_op jit(solution)/shard_map/ppermute | solution.py:46
  193.1 12.6 %collective-permute-start.20 = (bf16[2,1024,128]{2,1,0:T(8,128)(2,1)}, bf16[2,1024,128]{2,1,0:T(8,128)(2,1)}, u32[]{:S(2)}, u32[]{:S(2)}) collective-permute-start(bf16[2,1024,128]{2,1,0:T(8,128)(2,1)} %get-tuple-element.49), channel_id=1, source_target_pairs={{0,64},{4,20},{8,72},{12,28},{16,80},{20,4},{24,88},{28,12},{32,96... | collective-permute-start | bytes 1572872 | tf_op jit(solution)/shard_map/ppermute | solution.py:46
  193.1 16.3 %collective-permute-start.19 = (bf16[2,1024,128]{2,1,0:T(8,128)(2,1)}, bf16[2,1024,128]{2,1,0:T(8,128)(2,1)}, u32[]{:S(2)}, u32[]{:S(2)}) collective-permute-start(bf16[2,1024,128]{2,1,0:T(8,128)(2,1)} %get-tuple-element.50), channel_id=1, source_target_pairs={{0,32},{4,12},{8,40},{12,20},{16,48},{20,28},{24,56},{28,4},{32,64... | collective-permute-start | bytes 1572872 | tf_op jit(solution)/shard_map/ppermute | solution.py:46
  195.8 16.0 %copy-start.11 = (f32[1024,128]{1,0:T(8,128)S(1)}, f32[1024,128]{1,0:T(8,128)}, u32[]{:S(2)}) copy-start(f32[1024,128]{1,0:T(8,128)} %get-tuple-element.27) | copy-start | bytes 1572868
  195.8 16.0 %copy-start.12 = (f32[1024,128]{1,0:T(8,128)S(1)}, f32[1024,128]{1,0:T(8,128)}, u32[]{:S(2)}) copy-start(f32[1024,128]{1,0:T(8,128)} %get-tuple-element.28) | copy-start | bytes 1572868

commit v3 on v2

--- a/solution.py
+++ b/solution.py
@@ -11,8 +11,6 @@
 
 QB = 128
 SIDE = 4
-TILE = 256
-UNROLL = 2
 OWN_TILE = 512
 VMEM_LIMIT = 60 * 1024 * 1024
 LOG2E = math.log2(math.e)
@@ -125,16 +123,15 @@
     q0, g0, q1, g1, st0, st1 = refs[:6]
     blocks = refs[6 : 6 + sources]
     out0, out1 = refs[6 + sources : 8 + sources]
-    outs = refs[8 + sources : -3]
-    buf, dq0, dq1 = refs[-3:]
+    outs = refs[8 + sources : -4]
+    buf, q_buf, g_buf, dq = refs[-4:]
     at = pl.program_id(0)
     heads = q0.shape[0]
     rows = heads * QB
 
     @pl.when(at == 0)
     def _():
-        dq0[...] = jnp.zeros_like(dq0)
-        dq1[...] = jnp.zeros_like(dq1)
+        dq[...] = jnp.zeros_like(dq)
 
     for i, block_ref in enumerate(blocks):
 
@@ -148,51 +145,44 @@
     own = tbl[entry]
     sib = tbl[SIDE * SIDE + entry]
 
-    def load(block, q_ref, g_ref, st_ref):
-        where = pl.ds(pl.multiple_of(block * QB, QB), QB)
-        stats = st_ref[block]
-        return (
-            q_ref[:, where, :].reshape(rows, -1),
-            g_ref[:, where, :].reshape(rows, -1),
-            stats[0:1, :],
-            stats[1:2, :],
-        )
-
-    def run(sides):
-        loaded = [load(block, *side[:3]) for block, side in sides]
-
-        @pl.loop(0, buf.shape[1] // (UNROLL * TILE))
-        def _(turn):
-            total = [None] * len(sides)
-            for tile in range(UNROLL):
-                where = pl.ds(pl.multiple_of((turn * UNROLL + tile) * TILE, TILE), TILE)
-                keys, values = buf[0, where, :], buf[1, where, :]
-                dk_sum, dv_sum = None, None
-                for i, (q, g, lse, delta) in enumerate(loaded):
-                    dk, dv, dq = tile_grads(keys, values, q, g, lse, delta, scale2)
-                    dk_sum = dk if dk_sum is None else dk_sum + dk
-                    dv_sum = dv if dv_sum is None else dv_sum + dv
-                    total[i] = dq if total[i] is None else total[i] + dq
-                buf[0, where, :] = dk_sum.astype(jnp.bfloat16)
-                buf[1, where, :] = dv_sum.astype(jnp.bfloat16)
-            for (block, side), dq in zip(sides, total):
-                where = pl.ds(pl.multiple_of(block * QB, QB), QB)
-                side[3][:, where, :] += dq.reshape(heads, QB, -1)
-
-    own_side = (own, (q0, g0, st0, dq0))
-    sib_side = (sib, (q1, g1, st1, dq1))
+    def rows_of(block):
+        return pl.ds(pl.multiple_of(block * QB, QB), QB)
+
+    def load(block, q_ref, g_ref):
+        where = rows_of(block)
+        return q_ref[:, where, :].reshape(rows, -1), g_ref[:, where, :].reshape(rows, -1)
+
+    def run(units):
+        dk_sum, dv_sum = None, None
+        for side, block, q, g, stats in units:
+            dk, dv, dq_part = tile_grads(
+                buf[0], buf[1], q, g, stats[0:1, :], stats[1:2, :], scale2
+            )
+            dk_sum = dk if dk_sum is None else dk_sum + dk
+            dv_sum = dv if dv_sum is None else dv_sum + dv
+            dq[side, :, rows_of(block), :] += dq_part.reshape(heads, QB, -1)
+        buf[0] = dk_sum.astype(jnp.bfloat16)
+        buf[1] = dv_sum.astype(jnp.bfloat16)
 
     @pl.when((own >= 0) & (sib >= 0))
     def _():
-        run([own_side, sib_side])
-
-    @pl.when((own >= 0) & (sib < 0))
-    def _():
-        run([own_side])
-
-    @pl.when((own < 0) & (sib >= 0))
-    def _():
-        run([sib_side])
+        run([(0, own, *load(own, q0, g0), st0[own]), (1, sib, *load(sib, q1, g1), st1[sib])])
+
+    @pl.when((own >= 0) != (sib >= 0))
+    def _():
+        block = jnp.maximum(own, sib)
+        side = jnp.where(own >= 0, 0, 1)
+
+        @pl.when(side == 0)
+        def _():
+            q_buf[...], g_buf[...] = load(block, q0, g0)
+
+        @pl.when(side == 1)
+        def _():
+            q_buf[...], g_buf[...] = load(block, q1, g1)
+
+        stats = jnp.where(side == 0, st0[block], st1[block])
+        run([(side, block, q_buf[...], g_buf[...], stats)])
 
     @pl.when((own < 0) & (sib < 0))
     def _():
@@ -206,8 +196,8 @@
 
     @pl.when(at == pl.num_programs(0) - 1)
     def _():
-        out0[...] = dq0[...].astype(out0.dtype)
-        out1[...] = dq1[...].astype(out1.dtype)
+        out0[...] = dq[0].astype(out0.dtype)
+        out1[...] = dq[1].astype(out1.dtype)
 
 
 def remote_grads(table, own, sib, stats, groups, bases, scale2):
@@ -241,8 +231,9 @@
             out_specs=[acc_spec, acc_spec] + [piece(SIDE * i, SIDE) for i in range(count)],
             scratch_shapes=[
                 pltpu.VMEM((2, rows, width), jnp.bfloat16),
-                pltpu.VMEM((heads, rows, width), jnp.float32),
-                pltpu.VMEM((heads, rows, width), jnp.float32),
+                pltpu.VMEM((heads * QB, width), jnp.bfloat16),
+                pltpu.VMEM((heads * QB, width), jnp.bfloat16),
+                pltpu.VMEM((2, heads, rows, width), jnp.float32),
             ],
         ),
         out_shape=[acc, acc] + [part] * count,

time: 213 us -> 200 us (0.939)
  starting transfers between devices: 69.3 us -> 57.1 us
    ppermute x18, starting transfers between devices: 47.3 us -> 40.7 us  [shift(): return lax.ppermute(value, 'ctx', pairs(place))]
    ppermute x3, starting transfers between devices: 12.1 us -> 6.47 us  [other_core(): lax.ppermute(value, 'ctx', pairs(lambda x, z, core: (x, z, 1 - core)))]
  transfers between devices with their start and end apart: 23 -> 23, of which waited for: 8 -> 8; matrix products, arithmetic and copies ran while one was open for 9% -> 10% of each run, Pallas kernels for 20% -> 21%
where the time goes in v3:
time: 200 us
  waiting for transfers between devices  68.5 us (34%)
  starting transfers between devices  57.1 us (29%)
  Pallas kernels  42.1 us (21%)
  other arithmetic  21.9 us (11%)
  local copies, waits for them, and re-layouts  9.21 us (5%)
    ppermute x18, waiting for transfers between devices, shift(): return lax.ppermute(value, 'ctx', pairs(place))  49.6 us
    ppermute x18, starting transfers between devices, shift(): return lax.ppermute(value, 'ctx', pairs(place))  40.7 us
    pallas_call x3, Pallas kernels, remote_grads(): pl.pallas_call(functools.partial(remote_kernel, scale2, bases, offsets),...  26.9 us
    all_to_all x2, waiting for transfers between devices, turn(): lax.all_to_all(value, 'head', split_axis=0, concat_axis=0, tiled=True)  18.8 us
    pallas_call x1, Pallas kernels, own_grads(): pl.pallas_call(functools.partial(own_kernel, scale2), grid=(blocks,), in_...  15.2 us
    all_to_all x2, starting transfers between devices, turn(): lax.all_to_all(value, 'head', split_axis=0, concat_axis=0, tiled=True)  9.99 us
    ppermute x3, starting transfers between devices, other_core(): lax.ppermute(value, 'ctx', pairs(lambda x, z, core: (x, z, 1 - core)))  6.47 us
    add x1, other arithmetic, summed(): return sum((part.astype(jnp.float32) for part in parts))  4.17 us
  transfers between devices with their start and end apart: 23, of which 8 were waited for; matrix products, arithmetic and copies ran while one was open for 10% of the time, Pallas kernels for 21%

profile of v3, /device:TPU:8, one launch (start us, length us, event | category | flops | bytes accessed | tf_op | source)
XLA Modules:
  0.0 199.7 jit_solution(18231209054853240439)
XLA Ops:
  0.6 0.0 copy-start.1
  0.6 0.8 fusion.16
  1.5 2.7 %multiply_reduce_fusion = f32[1024,4]{1,0:T(8,128)S(1)} fusion(bf16[1024,4,1,128]{3,1,2,0:T(4,128)(2,1)} %param.11, bf16[1024,4,1,128]{3,1,2,0:T(4,128)(2,1)} %param.10), kind=kLoop, calls=%fused_computation.3 | loop fusion | flops 2093056 | bytes 2113536 | tf_op jit(solution)/shard_map/reduce_sum | solution.py:285
  4.2 0.2 copy.62
  4.5 0.1 reshape.227
  4.6 1.5 copy_bitcast_fusion
  6.1 1.5 pad_maximum_fusion
  7.6 4.9 %all-to-all-start = ((bf16[4,2096,128]{2,1,0:T(8,128)(2,1)}), bf16[4,2096,128]{2,1,0:T(8,128)(2,1)S(1)}, u32[]{:S(2)}, u32[]{:S(2)}) async-start(bf16[4,2096,128]{2,1,0:T(8,128)(2,1)} %pad_maximum_fusion), calls=%async_computation | async-start | bytes 4292608 | tf_op jit(solution)/shard_map/all_to_all | solution.py:283
  12.5 2.6 %constant_dynamic-slice_fusion = (bf16[1024,1,128]{2,1,0:T(2,128)(2,1)S(1)}, bf16[1024,1,128]{2,1,0:T(2,128)(2,1)S(1)}) fusion(bf16[1024,4,128]{2,1,0:T(4,128)(2,1)} %param.9, s32[]{:T(128)S(6)} %select_n.140, bf16[1024,4,128]{2,1,0:T(4,128)(2,1)} %param.8), kind=kLoop, calls=%fused_computation.73 | loop fusion | bytes 1048580 | tf_op jit(solution)/shard_map/jit(dynamic_index_in_dim)/dynamic_slice | solution.py:269
  15.2 1.1 pad_maximum_fusion.2
  16.3 2.8 %collective-permute-start.3 = (bf16[2,1024,128]{2,1,0:T(8,128)(2,1)}, bf16[2,1024,128]{2,1,0:T(8,128)(2,1)S(1)}, u32[]{:S(2)}, u32[]{:S(2)}) collective-permute-start(bf16[2,1024,128]{2,1,0:T(8,128)(2,1)} %get-tuple-element.53), channel_id=1, source_target_pairs={{0,96},{4,28},{8,104},{12,4},{16,112},{20,12},{24,120},{28,20},{32... | collective-permute-start | bytes 1572872 | tf_op jit(solution)/shard_map/ppermute | solution.py:44
  19.1 18.8 %all-to-all-done.q_ref.g_ref.refs_0_.refs_1_ = bf16[4,2096,128]{2,1,0:T(8,128)(2,1)S(1)} async-done(((bf16[4,2096,128]{2,1,0:T(8,128)(2,1)}), bf16[4,2096,128]{2,1,0:T(8,128)(2,1)S(1)}, u32[]{:S(2)}, u32[]{:S(2)}) %all-to-all-start) | async-done | bytes 2146336 | tf_op jit(solution)/shard_map/all_to_all | solution.py:283
  37.9 0.8 copy-done.13
  38.7 1.3 pad_maximum_fusion.1.refs_7_
  40.1 4.1 %collective-permute-start.9 = (bf16[2,2,1024,128]{3,2,1,0:T(8,128)(2,1)S(1)}, bf16[2,2,1024,128]{3,2,1,0:T(8,128)(2,1)}, u32[]{:S(2)}, u32[]{:S(2)}) collective-permute-start(bf16[2,2,1024,128]{3,2,1,0:T(8,128)(2,1)S(1)} %pad_maximum_fusion.1.refs_7_), channel_id=1, source_target_pairs={{0,24},{4,100},{8,0},{12,108},{16,8},{20,116},{24,16},{28,124},{32... | collective-permute-start | bytes 3145736 | tf_op jit(solution)/shard_map/ppermute | solution.py:44
  44.2 3.0 %collective-permute-start.4 = (bf16[2,1024,128]{2,1,0:T(8,128)(2,1)}, bf16[2,1024,128]{2,1,0:T(8,128)(2,1)}, u32[]{:S(2)}, u32[]{:S(2)}) collective-permute-start(bf16[2,1024,128]{2,1,0:T(8,128)(2,1)} %get-tuple-element.53), channel_id=1, source_target_pairs={{0,64},{4,20},{8,72},{12,28},{16,80},{20,4},{24,88},{28,12},{32,96... | collective-permute-start | bytes 1572872 | tf_op jit(solution)/shard_map/ppermute | solution.py:44
  47.2 0.5 collective-permute-start.5
  47.7 12.0 %collective-permute-done.4 = bf16[2,1024,128]{2,1,0:T(8,128)(2,1)} collective-permute-done((bf16[2,1024,128]{2,1,0:T(8,128)(2,1)}, bf16[2,1024,128]{2,1,0:T(8,128)(2,1)}, u32[]{:S(2)}, u32[]{:S(2)}) %collective-permute-start.4) | collective-permute-done | bytes 524320 | tf_op jit(solution)/shard_map/ppermute | solution.py:44
  59.8 2.4 %collective-permute-done.9.refs_10_ = bf16[2,2,1024,128]{3,2,1,0:T(8,128)(2,1)} collective-permute-done((bf16[2,2,1024,128]{3,2,1,0:T(8,128)(2,1)S(1)}, bf16[2,2,1024,128]{3,2,1,0:T(8,128)(2,1)}, u32[]{:S(2)}, u32[]{:S(2)}) %collective-permute-start.9) | collective-permute-done | bytes 1048608 | tf_op jit(solution)/shard_map/ppermute | solution.py:44
  62.1 3.8 %collective-permute-start.12 = (bf16[2,2,1024,128]{3,2,1,0:T(8,128)(2,1)}, bf16[2,2,1024,128]{3,2,1,0:T(8,128)(2,1)}, u32[]{:S(2)}, u32[]{:S(2)}) collective-permute-start(bf16[2,2,1024,128]{3,2,1,0:T(8,128)(2,1)} %collective-permute-done.9.refs_10_), channel_id=1, source_target_pairs={{0,24},{4,100},{8,0},{12,108},{16,8},{20,116},{24,16},{28,124},{32... | collective-permute-start | bytes 3145736 | tf_op jit(solution)/shard_map/ppermute | solution.py:44
  65.9 0.1 select_reduce_fusion.1
  66.0 0.1 collective-permute-start.11
  66.1 0.6 pad_add_fusion.tbl
  66.7 3.7 %collective-permute-done.7.refs_8_ = bf16[1,2,1024,128]{3,2,1,0:T(8,128)(2,1)} collective-permute-done((bf16[1,2,1024,128]{3,2,1,0:T(8,128)(2,1)}, bf16[1,2,1024,128]{3,2,1,0:T(8,128)(2,1)}, u32[]{:S(2)}, u32[]{:S(2)}) %collective-permute-start.7) | collective-permute-done | bytes 524320 | tf_op jit(solution)/shard_map/ppermute | solution.py:44
  70.5 0.6 reshape.228.st_ref.refs_4_
  71.1 3.2 %collective-permute-start.8 = (bf16[1,2,1024,128]{3,2,1,0:T(8,128)(2,1)}, bf16[1,2,1024,128]{3,2,1,0:T(8,128)(2,1)}, u32[]{:S(2)}, u32[]{:S(2)}) collective-permute-start(bf16[1,2,1024,128]{3,2,1,0:T(8,128)(2,1)} %get-tuple-element.54.refs_6_), channel_id=1, source_target_pairs={{0,24},{4,100},{8,0},{12,108},{16,8},{20,116},{24,16},{28,124},{32... | collective-permute-start | bytes 1572872 | tf_op jit(solution)/shard_map/ppermute | solution.py:44
  74.4 0.8 slice.124
  75.2 1.7 collective-permute-done.11.refs_6_
  76.9 0.6 reshape.229.refs_5_
  77.5 16.2 %collective-permute-done.13.refs_8_ = bf16[1,2,1024,128]{3,2,1,0:T(8,128)(2,1)} collective-permute-done((bf16[1,2,1024,128]{3,2,1,0:T(8,128)(2,1)}, bf16[1,2,1024,128]{3,2,1,0:T(8,128)(2,1)}, u32[]{:S(2)}, u32[]{:S(2)}) %collective-permute-start.13) | collective-permute-done | bytes 524320 | tf_op jit(solution)/shard_map/ppermute | solution.py:44
  93.7 7.4 %remote.5 = (bf16[4,1024,128]{2,1,0:T(8,128)(2,1)}, bf16[4,1024,128]{2,1,0:T(8,128)(2,1)}, bf16[4,2,1024,128]{3,2,1,0:T(8,128)(2,1)}) custom-call(s32[32]{0:T(128)} %pad_add_fusion.tbl, bf16[4,2096,128]{2,1,0:T(8,128)(2,1)} %copy-done, bf16[4,2096,128]{2,1,0:T(8,128)(2,1)} %copy-done, bf16[4,2096,128]{2,1,0:T(8,128)(2,1)} %collective-permute-done.1.refs_2_.refs_3_, ...), custom_call_target="tpu_custom_call" | custom-call | flops 2684354560 | bytes 12582912 | tf_op jit(solution)/shard_map/remote/pallas_call | solution.py:224
  101.1 1.0 collective-permute-start.17
  102.1 10.4 %remote.4 = (bf16[4,1024,128]{2,1,0:T(8,128)(2,1)}, bf16[4,1024,128]{2,1,0:T(8,128)(2,1)}, bf16[4,2,1024,128]{3,2,1,0:T(8,128)(2,1)}, bf16[4,2,1024,128]{3,2,1,0:T(8,128)(2,1)}) custom-call(s32[32]{0:T(128)} %pad_add_fusion.tbl, bf16[4,2096,128]{2,1,0:T(8,128)(2,1)} %copy-done, bf16[4,2096,128]{2,1,0:T(8,128)(2,1)} %copy-done, ...), custom_call_target="tpu_custom_call" | custom-call | flops 5368709120 | bytes 16777216 | tf_op jit(solution)/shard_map/remote/pallas_call | solution.py:224
  112.5 7.5 %collective-permute-start.15 = (bf16[4,2,1024,128]{3,2,1,0:T(8,128)(2,1)}, bf16[4,2,1024,128]{3,2,1,0:T(8,128)(2,1)}, u32[]{:S(2)}, u32[]{:S(2)}) collective-permute-start(bf16[4,2,1024,128]{3,2,1,0:T(8,128)(2,1)} %get-tuple-element.24), channel_id=1, source_target_pairs={{0,24},{4,100},{8,0},{12,108},{16,8},{20,116},{24,16},{28,124},{32... | collective-permute-start | bytes 6291464 | tf_op jit(solution)/shard_map/ppermute | solution.py:44
  120.0 9.1 %remote.3 = (bf16[4,1024,128]{2,1,0:T(8,128)(2,1)}, bf16[4,1024,128]{2,1,0:T(8,128)(2,1)}, bf16[4,2,1024,128]{3,2,1,0:T(8,128)(2,1)}) custom-call(s32[32]{0:T(128)} %pad_add_fusion.tbl, bf16[4,2096,128]{2,1,0:T(8,128)(2,1)} %copy-done, bf16[4,2096,128]{2,1,0:T(8,128)(2,1)} %copy-done, bf16[4,2096,128]{2,1,0:T(8,128)(2,1)} %collective-permute-done.1.refs_2_.refs_3_, ...), custom_call_target="tpu_custom_call" | custom-call | flops 2684354560 | bytes 12582912 | tf_op jit(solution)/shard_map/remote/pallas_call | solution.py:224
  129.1 2.6 %add_convert_fusion = bf16[4,1024,128]{2,1,0:T(8,128)(2,1)} fusion(bf16[4,1024,128]{2,1,0:T(8,128)(2,1)S(1)} %copy-done.9, bf16[4,1024,128]{2,1,0:T(8,128)(2,1)S(1)} %copy-done.10, bf16[4,1024,128]{2,1,0:T(8,128)(2,1)} %get-tuple-element.20), kind=kLoop, calls=%fused_computation.2 | loop fusion | flops 3145728 | bytes 4194304 | tf_op jit(solution)/shard_map/convert_element_type | solution.py:347
  131.8 6.5 %collective-permute-start.14 = (bf16[4,1024,128]{2,1,0:T(8,128)(2,1)}, bf16[4,1024,128]{2,1,0:T(8,128)(2,1)}, u32[]{:S(2)}, u32[]{:S(2)}) collective-permute-start(bf16[4,1024,128]{2,1,0:T(8,128)(2,1)} %add_convert_fusion), channel_id=1, source_target_pairs={{0,4},{4,0},{8,12},{12,8},{16,20},{20,16},{24,28},{28,24},{32,36},... | collective-permute-start | bytes 3145736 | tf_op jit(solution)/shard_map/ppermute | solution.py:48
  138.2 15.2 %own.1 = (f32[4,1024,128]{2,1,0:T(8,128)}, f32[1024,128]{1,0:T(8,128)}, f32[1024,128]{1,0:T(8,128)}) custom-call(bf16[4,2096,128]{2,1,0:T(8,128)(2,1)} %copy-done, bf16[4,2096,128]{2,1,0:T(8,128)(2,1)} %copy-done, f32[8,2,512]{2,1,0:T(2,128)} %reshape.228.st_ref.refs_4_, bf16[1024,128]{1,0:T(8,128)(2,1)} %bitcast.90, bf16[1024,128]{1,0:T(8,128)(2,1)} %bitcast.88), custom_call_target="tpu_custom_call" | custom-call | flops 3221225472 | bytes 8388608 | tf_op jit(solution)/shard_map/own/pallas_call | solution.py:107
  153.5 3.5 %multiply_convert_fusion = bf16[4,1024,128]{2,1,0:T(8,128)(2,1)} fusion(f32[4,1024,128]{2,1,0:T(8,128)} %get-tuple-element.16, bf16[4,1024,128]{2,1,0:T(8,128)(2,1)} %collective-permute-done.14, bf16[4,1024,128]{2,1,0:T(8,128)(2,1)S(1)} %copy-done.4, bf16[4,1024,128]{2,1,0:T(8,128)(2,1)S(1)} %copy-done.5, bf16[4,1024,128]{2,1,0:T(8,128)(2,1)S(1)} %copy-done.6), kind=kLoop, calls=%fused_computation.1 | loop fusion | flops 5242880 | bytes 7340032 | tf_op jit(solution)/shard_map/convert_element_type | solution.py:349
  157.0 5.1 %all-to-all-start.1 = ((bf16[4,1024,128]{2,1,0:T(8,128)(2,1)}), bf16[4,1024,128]{2,1,0:T(8,128)(2,1)S(1)}, u32[]{:S(2)}, u32[]{:S(2)}) async-start(bf16[4,1024,128]{2,1,0:T(8,128)(2,1)} %multiply_convert_fusion), calls=%async_computation.1 | async-start | bytes 2097152 | tf_op jit(solution)/shard_map/all_to_all | solution.py:283
  162.1 4.2 %fusion.2 = (bf16[2,1024,128]{2,1,0:T(8,128)(2,1)}, bf16[2,1024,128]{2,1,0:T(8,128)(2,1)}, bf16[2,1024,128]{2,1,0:T(8,128)(2,1)}) fusion(bf16[4,2,1024,128]{3,2,1,0:T(8,128)(2,1)} %collective-permute-done.17, bf16[4,2,1024,128]{3,2,1,0:T(8,128)(2,1)} %collective-permute-done.16, bf16[4,2,1024,128]{3,2,1,0:T(8,128)(2,1)} %collective-permute-done.15, ...), kind=kLoop, calls=%fused_computation.13 | loop fusion | flops 6291456 | bytes 7864320 | tf_op jit(solution)/shard_map/add | solution.py:331
  166.3 13.8 %collective-permute-start.18 = (bf16[2,1024,128]{2,1,0:T(8,128)(2,1)}, bf16[2,1024,128]{2,1,0:T(8,128)(2,1)}, u32[]{:S(2)}, u32[]{:S(2)}) collective-permute-start(bf16[2,1024,128]{2,1,0:T(8,128)(2,1)} %get-tuple-element.48), channel_id=1, source_target_pairs={{0,96},{4,28},{8,104},{12,4},{16,112},{20,12},{24,120},{28,20},{32... | collective-permute-start | bytes 1572872 | tf_op jit(solution)/shard_map/ppermute | solution.py:44
  180.1 0.9 collective-permute-start.19
  181.0 1.8 copy.72
  182.8 10.0 %collective-permute-done.18 = bf16[2,1024,128]{2,1,0:T(8,128)(2,1)} collective-permute-done((bf16[2,1024,128]{2,1,0:T(8,128)(2,1)}, bf16[2,1024,128]{2,1,0:T(8,128)(2,1)}, u32[]{:S(2)}, u32[]{:S(2)}) %collective-permute-start.18) | collective-permute-done | bytes 524320 | tf_op jit(solution)/shard_map/ppermute | solution.py:44
  192.8 3.7 %collective-permute-done.19 = bf16[2,1024,128]{2,1,0:T(8,128)(2,1)} collective-permute-done((bf16[2,1024,128]{2,1,0:T(8,128)(2,1)}, bf16[2,1024,128]{2,1,0:T(8,128)(2,1)}, u32[]{:S(2)}, u32[]{:S(2)}) %collective-permute-start.19) | collective-permute-done | bytes 524320 | tf_op jit(solution)/shard_map/ppermute | solution.py:44
  196.4 2.3 %fusion.1 = f32[2,1024,128]{2,1,0:T(8,128)S(1)} fusion(bf16[2,1024,128]{2,1,0:T(8,128)(2,1)} %collective-permute-done.20, bf16[2,1024,128]{2,1,0:T(8,128)(2,1)} %collective-permute-done.19, bf16[2,1024,128]{2,1,0:T(8,128)(2,1)} %collective-permute-done.18, bf16[4,2,1024,128]{3,2,1,0:T(8,128)(2,1)} %collective-permute-done.17, ...), kind=kLoop, calls=%fused_computation.7 | loop fusion | flops 3407872 | bytes 4718592 | tf_op jit(solution)/shard_map/add | solution.py:339
  198.7 1.0 fusion.11
  (66 shorter events, 0.4 us)
Async XLA Ops:
  0.6 3.9 %copy-start.1 = (bf16[1024,4,1,128]{3,1,2,0:T(4,128)(2,1)S(1)}, bf16[1024,4,1,128]{3,1,2,0:T(4,128)(2,1)}, u32[]{:S(2)}) copy-start(bf16[1024,4,1,128]{3,1,2,0:T(4,128)(2,1)} %param.10) | copy-start | bytes 3145732
  7.6 30.3 %all-to-all-start = ((bf16[4,2096,128]{2,1,0:T(8,128)(2,1)}), bf16[4,2096,128]{2,1,0:T(8,128)(2,1)S(1)}, u32[]{:S(2)}, u32[]{:S(2)}) async-start(bf16[4,2096,128]{2,1,0:T(8,128)(2,1)} %pad_maximum_fusion), calls=%async_computation | async-start | bytes 4292608 | tf_op jit(solution)/shard_map/all_to_all | solution.py:283
  15.2 24.9 %copy-start.7 = (bf16[1024,1,128]{2,0,1:T(8,128)(2,1)}, bf16[1024,1,128]{2,0,1:T(8,128)(2,1)S(1)}, u32[]{:S(2)}) copy-start(bf16[1024,1,128]{2,0,1:T(8,128)(2,1)S(1)} %copy.104) | copy-start | bytes 786436
  15.2 32.1 %copy-start.14 = (s32[8,3]{0,1:T(4,128)S(1)}, s32[8,3]{0,1:T(4,128)}, u32[]{:S(2)}) copy-start(s32[8,3]{0,1:T(4,128)} %param.13) | copy-start | bytes 292
  15.2 22.7 %copy-start.8 = (bf16[1024,1,128]{2,0,1:T(8,128)(2,1)}, bf16[1024,1,128]{2,0,1:T(8,128)(2,1)S(1)}, u32[]{:S(2)}) copy-start(bf16[1024,1,128]{2,0,1:T(8,128)(2,1)S(1)} %copy.105) | copy-start | bytes 786436
  16.3 21.6 %collective-permute-start.3 = (bf16[2,1024,128]{2,1,0:T(8,128)(2,1)}, bf16[2,1024,128]{2,1,0:T(8,128)(2,1)S(1)}, u32[]{:S(2)}, u32[]{:S(2)}) collective-permute-start(bf16[2,1024,128]{2,1,0:T(8,128)(2,1)} %get-tuple-element.53), channel_id=1, source_target_pairs={{0,96},{4,28},{8,104},{12,4},{16,112},{20,12},{24,120},{28,20},{32... | collective-permute-start | bytes 1572872 | tf_op jit(solution)/shard_map/ppermute | solution.py:44
  19.1 18.8 %collective-permute-start.2 = (bf16[2,1024,128]{2,1,0:T(8,128)(2,1)}, bf16[2,1024,128]{2,1,0:T(8,128)(2,1)}, u32[]{:S(2)}, u32[]{:S(2)}) collective-permute-start(bf16[2,1024,128]{2,1,0:T(8,128)(2,1)} %get-tuple-element.53), channel_id=1, source_target_pairs={{0,32},{4,12},{8,40},{12,20},{16,48},{20,28},{24,56},{28,4},{32,64... | collective-permute-start | bytes 1572872 | tf_op jit(solution)/shard_map/ppermute | solution.py:44
  37.9 55.8 %copy-start = (bf16[4,2096,128]{2,1,0:T(8,128)(2,1)}, bf16[4,2096,128]{2,1,0:T(8,128)(2,1)S(1)}, u32[]{:S(2)}) copy-start(bf16[4,2096,128]{2,1,0:T(8,128)(2,1)S(1)} %all-to-all-done.q_ref.g_ref.refs_0_.refs_1_) | copy-start | bytes 6438916
  37.9 33.3 %collective-permute-start.1 = (bf16[4,2096,128]{2,1,0:T(8,128)(2,1)S(1)}, bf16[4,2096,128]{2,1,0:T(8,128)(2,1)}, u32[]{:S(2)}, u32[]{:S(2)}) collective-permute-start(bf16[4,2096,128]{2,1,0:T(8,128)(2,1)S(1)} %all-to-all-done.q_ref.g_ref.refs_0_.refs_1_), channel_id=1, source_target_pairs={{0,4},{4,0},{8,12},{12,8},{16,20},{20,16},{24,28},{28,24},{32,36},... | collective-permute-start | bytes 6438920 | tf_op jit(solution)/shard_map/ppermute | solution.py:48
  37.9 0.8 copy-start.13
  40.1 61.0 %copy-start.2 = (bf16[2,2,1024,128]{3,2,1,0:T(8,128)(2,1)}, bf16[2,2,1024,128]{3,2,1,0:T(8,128)(2,1)S(1)}, u32[]{:S(2)}) copy-start(bf16[2,2,1024,128]{3,2,1,0:T(8,128)(2,1)S(1)} %pad_maximum_fusion.1.refs_7_) | copy-start | bytes 3145732
  40.1 22.0 %collective-permute-start.9 = (bf16[2,2,1024,128]{3,2,1,0:T(8,128)(2,1)S(1)}, bf16[2,2,1024,128]{3,2,1,0:T(8,128)(2,1)}, u32[]{:S(2)}, u32[]{:S(2)}) collective-permute-start(bf16[2,2,1024,128]{3,2,1,0:T(8,128)(2,1)S(1)} %pad_maximum_fusion.1.refs_7_), channel_id=1, source_target_pairs={{0,24},{4,100},{8,0},{12,108},{16,8},{20,116},{24,16},{28,124},{32... | collective-permute-start | bytes 3145736 | tf_op jit(solution)/shard_map/ppermute | solution.py:44
  44.2 15.5 %collective-permute-start.4 = (bf16[2,1024,128]{2,1,0:T(8,128)(2,1)}, bf16[2,1024,128]{2,1,0:T(8,128)(2,1)}, u32[]{:S(2)}, u32[]{:S(2)}) collective-permute-start(bf16[2,1024,128]{2,1,0:T(8,128)(2,1)} %get-tuple-element.53), channel_id=1, source_target_pairs={{0,64},{4,20},{8,72},{12,28},{16,80},{20,4},{24,88},{28,12},{32,96... | collective-permute-start | bytes 1572872 | tf_op jit(solution)/shard_map/ppermute | solution.py:44
  47.2 12.5 %collective-permute-start = (s32[8,3]{0,1:T(4,128)S(1)}, s32[8,3]{0,1:T(4,128)S(1)}, u32[]{:S(2)}, u32[]{:S(2)}) collective-permute-start(s32[8,3]{0,1:T(4,128)S(1)} %copy-done.14), channel_id=1, source_target_pairs={{0,4},{4,0},{8,12},{12,8},{16,20},{20,16},{24,28},{28,24},{32,36},... | collective-permute-start | bytes 296 | tf_op jit(solution)/shard_map/ppermute | solution.py:48
  47.2 18.8 %collective-permute-start.5 = (bf16[1,2,1024,128]{3,2,1,0:T(8,128)(2,1)}, bf16[1,2,1024,128]{3,2,1,0:T(8,128)(2,1)}, u32[]{:S(2)}, u32[]{:S(2)}) collective-permute-start(bf16[1,2,1024,128]{3,2,1,0:T(8,128)(2,1)} %get-tuple-element.54.refs_6_), channel_id=1, source_target_pairs={{0,8},{4,36},{8,16},{12,44},{16,24},{20,52},{24,0},{28,60},{32,40}... | collective-permute-start | bytes 1572872 | tf_op jit(solution)/shard_map/ppermute | solution.py:44
  59.7 10.7 %collective-permute-start.7 = (bf16[1,2,1024,128]{3,2,1,0:T(8,128)(2,1)}, bf16[1,2,1024,128]{3,2,1,0:T(8,128)(2,1)}, u32[]{:S(2)}, u32[]{:S(2)}) collective-permute-start(bf16[1,2,1024,128]{3,2,1,0:T(8,128)(2,1)} %bitcast.24.refs_8_), channel_id=1, source_target_pairs={{0,8},{4,36},{8,16},{12,44},{16,24},{20,52},{24,0},{28,60},{32,40}... | collective-permute-start | bytes 1572872 | tf_op jit(solution)/shard_map/ppermute | solution.py:44
  62.1 31.5 %collective-permute-start.12 = (bf16[2,2,1024,128]{3,2,1,0:T(8,128)(2,1)}, bf16[2,2,1024,128]{3,2,1,0:T(8,128)(2,1)}, u32[]{:S(2)}, u32[]{:S(2)}) collective-permute-start(bf16[2,2,1024,128]{3,2,1,0:T(8,128)(2,1)} %collective-permute-done.9.refs_10_), channel_id=1, source_target_pairs={{0,24},{4,100},{8,0},{12,108},{16,8},{20,116},{24,16},{28,124},{32... | collective-permute-start | bytes 3145736 | tf_op jit(solution)/shard_map/ppermute | solution.py:44
  66.0 10.8 %collective-permute-start.11 = (bf16[1,2,1024,128]{3,2,1,0:T(8,128)(2,1)}, bf16[1,2,1024,128]{3,2,1,0:T(8,128)(2,1)}, u32[]{:S(2)}, u32[]{:S(2)}) collective-permute-start(bf16[1,2,1024,128]{3,2,1,0:T(8,128)(2,1)} %collective-permute-done.5.refs_6_), channel_id=1, source_target_pairs={{0,8},{4,36},{8,16},{12,44},{16,24},{20,52},{24,0},{28,60},{32,40}... | collective-permute-start | bytes 1572872 | tf_op jit(solution)/shard_map/ppermute | solution.py:44
  66.7 35.4 %collective-permute-start.6 = (bf16[2,2,1024,128]{3,2,1,0:T(8,128)(2,1)S(1)}, bf16[2,2,1024,128]{3,2,1,0:T(8,128)(2,1)}, u32[]{:S(2)}, u32[]{:S(2)}) collective-permute-start(bf16[2,2,1024,128]{3,2,1,0:T(8,128)(2,1)S(1)} %pad_maximum_fusion.1.refs_7_), channel_id=1, source_target_pairs={{0,8},{4,36},{8,16},{12,44},{16,24},{20,52},{24,0},{28,60},{32,40}... | collective-permute-start | bytes 3145736 | tf_op jit(solution)/shard_map/ppermute | solution.py:44
  70.4 23.2 %collective-permute-start.13 = (bf16[1,2,1024,128]{3,2,1,0:T(8,128)(2,1)}, bf16[1,2,1024,128]{3,2,1,0:T(8,128)(2,1)}, u32[]{:S(2)}, u32[]{:S(2)}) collective-permute-start(bf16[1,2,1024,128]{3,2,1,0:T(8,128)(2,1)} %collective-permute-done.7.refs_8_), channel_id=1, source_target_pairs={{0,8},{4,36},{8,16},{12,44},{16,24},{20,52},{24,0},{28,60},{32,40}... | collective-permute-start | bytes 1572872 | tf_op jit(solution)/shard_map/ppermute | solution.py:44
  71.1 31.0 %collective-permute-start.8 = (bf16[1,2,1024,128]{3,2,1,0:T(8,128)(2,1)}, bf16[1,2,1024,128]{3,2,1,0:T(8,128)(2,1)}, u32[]{:S(2)}, u32[]{:S(2)}) collective-permute-start(bf16[1,2,1024,128]{3,2,1,0:T(8,128)(2,1)} %get-tuple-element.54.refs_6_), channel_id=1, source_target_pairs={{0,24},{4,100},{8,0},{12,108},{16,8},{20,116},{24,16},{28,124},{32... | collective-permute-start | bytes 1572872 | tf_op jit(solution)/shard_map/ppermute | solution.py:44
  76.8 25.3 %collective-permute-start.10 = (bf16[1,2,1024,128]{3,2,1,0:T(8,128)(2,1)}, bf16[1,2,1024,128]{3,2,1,0:T(8,128)(2,1)}, u32[]{:S(2)}, u32[]{:S(2)}) collective-permute-start(bf16[1,2,1024,128]{3,2,1,0:T(8,128)(2,1)} %bitcast.24.refs_8_), channel_id=1, source_target_pairs={{0,24},{4,100},{8,0},{12,108},{16,8},{20,116},{24,16},{28,124},{32... | collective-permute-start | bytes 1572872 | tf_op jit(solution)/shard_map/ppermute | solution.py:44
  101.1 61.0 %collective-permute-start.17 = (bf16[4,2,1024,128]{3,2,1,0:T(8,128)(2,1)}, bf16[4,2,1024,128]{3,2,1,0:T(8,128)(2,1)}, u32[]{:S(2)}, u32[]{:S(2)}) collective-permute-start(bf16[4,2,1024,128]{3,2,1,0:T(8,128)(2,1)} %get-tuple-element.26), channel_id=1, source_target_pairs={{0,16},{4,68},{8,24},{12,76},{16,0},{20,84},{24,8},{28,92},{32,48}... | collective-permute-start | bytes 6291464 | tf_op jit(solution)/shard_map/ppermute | solution.py:44
  112.5 49.6 %collective-permute-start.15 = (bf16[4,2,1024,128]{3,2,1,0:T(8,128)(2,1)}, bf16[4,2,1024,128]{3,2,1,0:T(8,128)(2,1)}, u32[]{:S(2)}, u32[]{:S(2)}) collective-permute-start(bf16[4,2,1024,128]{3,2,1,0:T(8,128)(2,1)} %get-tuple-element.24), channel_id=1, source_target_pairs={{0,24},{4,100},{8,0},{12,108},{16,8},{20,116},{24,16},{28,124},{32... | collective-permute-start | bytes 6291464 | tf_op jit(solution)/shard_map/ppermute | solution.py:44
  120.0 9.1 %copy-start.9 = (bf16[4,1024,128]{2,1,0:T(8,128)(2,1)S(1)}, bf16[4,1024,128]{2,1,0:T(8,128)(2,1)}, u32[]{:S(2)}) copy-start(bf16[4,1024,128]{2,1,0:T(8,128)(2,1)} %get-tuple-element.22) | copy-start | bytes 3145732
  120.0 9.1 %copy-start.10 = (bf16[4,1024,128]{2,1,0:T(8,128)(2,1)S(1)}, bf16[4,1024,128]{2,1,0:T(8,128)(2,1)}, u32[]{:S(2)}) copy-start(bf16[4,1024,128]{2,1,0:T(8,128)(2,1)} %get-tuple-element.21) | copy-start | bytes 3145732
  120.0 42.1 %collective-permute-start.16 = (bf16[4,2,1024,128]{3,2,1,0:T(8,128)(2,1)}, bf16[4,2,1024,128]{3,2,1,0:T(8,128)(2,1)}, u32[]{:S(2)}, u32[]{:S(2)}) collective-permute-start(bf16[4,2,1024,128]{3,2,1,0:T(8,128)(2,1)} %get-tuple-element.25), channel_id=1, source_target_pairs={{0,8},{4,36},{8,16},{12,44},{16,24},{20,52},{24,0},{28,60},{32,40}... | collective-permute-start | bytes 6291464 | tf_op jit(solution)/shard_map/ppermute | solution.py:44
  131.8 21.7 %collective-permute-start.14 = (bf16[4,1024,128]{2,1,0:T(8,128)(2,1)}, bf16[4,1024,128]{2,1,0:T(8,128)(2,1)}, u32[]{:S(2)}, u32[]{:S(2)}) collective-permute-start(bf16[4,1024,128]{2,1,0:T(8,128)(2,1)} %add_convert_fusion), channel_id=1, source_target_pairs={{0,4},{4,0},{8,12},{12,8},{16,20},{20,16},{24,28},{28,24},{32,36},... | collective-permute-start | bytes 3145736 | tf_op jit(solution)/shard_map/ppermute | solution.py:48
  138.2 15.2 %copy-start.4 = (bf16[4,1024,128]{2,1,0:T(8,128)(2,1)S(1)}, bf16[4,1024,128]{2,1,0:T(8,128)(2,1)}, u32[]{:S(2)}) copy-start(bf16[4,1024,128]{2,1,0:T(8,128)(2,1)} %get-tuple-element.19) | copy-start | bytes 3145732
  138.2 15.2 %copy-start.5 = (bf16[4,1024,128]{2,1,0:T(8,128)(2,1)S(1)}, bf16[4,1024,128]{2,1,0:T(8,128)(2,1)}, u32[]{:S(2)}) copy-start(bf16[4,1024,128]{2,1,0:T(8,128)(2,1)} %get-tuple-element.18) | copy-start | bytes 3145732
  138.2 15.3 %copy-start.6 = (bf16[4,1024,128]{2,1,0:T(8,128)(2,1)S(1)}, bf16[4,1024,128]{2,1,0:T(8,128)(2,1)}, u32[]{:S(2)}) copy-start(bf16[4,1024,128]{2,1,0:T(8,128)(2,1)} %get-tuple-element.17) | copy-start | bytes 3145732
  157.0 5.1 %copy-start.3 = (bf16[4,2,1024,128]{3,2,1,0:T(8,128)(2,1)S(1)}, bf16[4,2,1024,128]{3,2,1,0:T(8,128)(2,1)}, u32[]{:S(2)}) copy-start(bf16[4,2,1024,128]{3,2,1,0:T(8,128)(2,1)} %get-tuple-element.23) | copy-start | bytes 6291460
  157.0 24.0 %all-to-all-start.1 = ((bf16[4,1024,128]{2,1,0:T(8,128)(2,1)}), bf16[4,1024,128]{2,1,0:T(8,128)(2,1)S(1)}, u32[]{:S(2)}, u32[]{:S(2)}) async-start(bf16[4,1024,128]{2,1,0:T(8,128)(2,1)} %multiply_convert_fusion), calls=%async_computation.1 | async-start | bytes 2097152 | tf_op jit(solution)/shard_map/all_to_all | solution.py:283
  166.3 26.4 %collective-permute-start.18 = (bf16[2,1024,128]{2,1,0:T(8,128)(2,1)}, bf16[2,1024,128]{2,1,0:T(8,128)(2,1)}, u32[]{:S(2)}, u32[]{:S(2)}) collective-permute-start(bf16[2,1024,128]{2,1,0:T(8,128)(2,1)} %get-tuple-element.48), channel_id=1, source_target_pairs={{0,96},{4,28},{8,104},{12,4},{16,112},{20,12},{24,120},{28,20},{32... | collective-permute-start | bytes 1572872 | tf_op jit(solution)/shard_map/ppermute | solution.py:44
  180.1 12.6 %collective-permute-start.20 = (bf16[2,1024,128]{2,1,0:T(8,128)(2,1)}, bf16[2,1024,128]{2,1,0:T(8,128)(2,1)}, u32[]{:S(2)}, u32[]{:S(2)}) collective-permute-start(bf16[2,1024,128]{2,1,0:T(8,128)(2,1)} %get-tuple-element.49), channel_id=1, source_target_pairs={{0,64},{4,20},{8,72},{12,28},{16,80},{20,4},{24,88},{28,12},{32,96... | collective-permute-start | bytes 1572872 | tf_op jit(solution)/shard_map/ppermute | solution.py:44
  180.1 16.3 %collective-permute-start.19 = (bf16[2,1024,128]{2,1,0:T(8,128)(2,1)}, bf16[2,1024,128]{2,1,0:T(8,128)(2,1)}, u32[]{:S(2)}, u32[]{:S(2)}) collective-permute-start(bf16[2,1024,128]{2,1,0:T(8,128)(2,1)} %get-tuple-element.50), channel_id=1, source_target_pairs={{0,32},{4,12},{8,40},{12,20},{16,48},{20,28},{24,56},{28,4},{32,64... | collective-permute-start | bytes 1572872 | tf_op jit(solution)/shard_map/ppermute | solution.py:44
  182.8 16.0 %copy-start.11 = (f32[1024,128]{1,0:T(8,128)S(1)}, f32[1024,128]{1,0:T(8,128)}, u32[]{:S(2)}) copy-start(f32[1024,128]{1,0:T(8,128)} %get-tuple-element.27) | copy-start | bytes 1572868
  182.8 16.0 %copy-start.12 = (f32[1024,128]{1,0:T(8,128)S(1)}, f32[1024,128]{1,0:T(8,128)}, u32[]{:S(2)}) copy-start(f32[1024,128]{1,0:T(8,128)} %get-tuple-element.28) | copy-start | bytes 1572868

commit v4 on v3

--- a/solution.py
+++ b/solution.py
@@ -324,25 +324,26 @@
     back_behind = shift(part_behind, 1, -1)
     back_ahead = shift(part_ahead, 1, 1)
     second0, second1, part_across = remote([line_across], (2 * SIDE,))
-    back_across = shift(part_across, 1, 2)
     own_q, own_k, own_v = own_grads(own, own_stats, keys, values, scale2)
 
     def summed(*parts):
         return sum(part.astype(jnp.float32) for part in parts)
 
-    total = [
-        summed(part_line[i], back_behind[i], back_ahead[i], back_across[i])
-        for i in range(SIDE)
-    ]
-    low = [part.astype(jnp.bfloat16) for part in total[1:]]
-    near_sum = (
-        total[0]
-        + shift(low[0], 0, -1).astype(jnp.float32)
-        + shift(low[1], 0, 1).astype(jnp.float32)
-        + shift(low[2], 0, 2).astype(jnp.float32)
-    )
-    grad_k = ((near_sum[0] + own_k) * scale).astype(jnp.bfloat16)
-    grad_v = (near_sum[1] + own_v).astype(jnp.bfloat16)
+    def spread(parts):
+        return (shift(parts[0], 0, -1), shift(parts[1], 0, 1), shift(parts[2], 0, 2))
+
+    side = spread(part_across[1:])
+    far_sum = summed(part_across[0], *side).astype(jnp.bfloat16)
+    total = [summed(part_line[i], back_behind[i], back_ahead[i]) for i in range(SIDE)]
+    received = spread([part.astype(jnp.bfloat16) for part in total[1:]])
+    received += (shift(far_sum, 1, 2),)
+
+    def final(i, own_part, factor):
+        return ((total[0][i] + summed(*(part[i] for part in received)) + own_part) * factor).astype(
+            jnp.bfloat16
+        )
+
+    grad_k, grad_v = final(0, own_k, scale), final(1, own_v, 1.0)
 
     dq_low = summed(level1, first1, second1).astype(jnp.bfloat16)
     returned = other_core(dq_low)

time: 200 us -> 210 us (1.050)
  starting transfers between devices: 57.1 us -> 62.2 us
  local copies, waits for them, and re-layouts: 9.21 us -> 12.1 us
    ppermute x18 -> x21, starting transfers between devices: 40.7 us -> 52.3 us  [shift(): return lax.ppermute(value, 'ctx', pairs(place))]
    all_to_all x2, waiting for transfers between devices: 18.8 us -> 29.6 us  [turn(): lax.all_to_all(value, 'head', split_axis=0, concat_axis=0, tiled=True)]
    ppermute x18 -> x21, waiting for transfers between devices: 49.6 us -> 40 us  [shift(): return lax.ppermute(value, 'ctx', pairs(place))]
    convert_element_type x0 -> x2, other arithmetic: none -> 7.1 us  [the longest x1 4.53 us: grads(): received = spread([part.astype(jnp.bfloat16) for part in total[1:]])]
    ppermute x3, starting transfers between devices: 6.47 us -> 0.01 us  [other_core(): lax.ppermute(value, 'ctx', pairs(lambda x, z, core: (x, z, 1 - core)))]
    add x2 -> x0, other arithmetic: 6.45 us -> none  [the longest x1 4.17 us: summed(): return sum((part.astype(jnp.float32) for part in parts))]
    squeeze x0 -> x1, local copies, waits for them, and re-layouts: none -> 2.52 us  [spread(): parts[0]]
  transfers between devices with their start and end apart: 23 -> 26, of which waited for: 8 -> 9; matrix products, arithmetic and copies ran while one was open for 10% -> 12% of each run, Pallas kernels for 21% -> 20%
where the time goes in v4:
time: 210 us; the launch traced here: 209 us
  waiting for transfers between devices  69.6 us (33%)
  starting transfers between devices  62.2 us (30%)
  Pallas kernels  42.1 us (20%)
  other arithmetic  22.4 us (11%)
  local copies, waits for them, and re-layouts  12.1 us (6%)
    ppermute x21, starting transfers between devices, shift(): return lax.ppermute(value, 'ctx', pairs(place))  52.3 us
    ppermute x21, waiting for transfers between devices, shift(): return lax.ppermute(value, 'ctx', pairs(place))  40 us
    all_to_all x2, waiting for transfers between devices, turn(): lax.all_to_all(value, 'head', split_axis=0, concat_axis=0, tiled=True)  29.6 us
    pallas_call x3, Pallas kernels, remote_grads(): pl.pallas_call(functools.partial(remote_kernel, scale2, bases, offsets),...  26.8 us
    pallas_call x1, Pallas kernels, own_grads(): pl.pallas_call(functools.partial(own_kernel, scale2), grid=(blocks,), in_...  15.2 us
    all_to_all x2, starting transfers between devices, turn(): lax.all_to_all(value, 'head', split_axis=0, concat_axis=0, tiled=True)  9.98 us
    convert_element_type x1, other arithmetic, grads(): received = spread([part.astype(jnp.bfloat16) for part in total[1:]])  4.53 us
  transfers between devices with their start and end apart: 26, of which 9 were waited for; matrix products, arithmetic and copies ran while one was open for 12% of the time, Pallas kernels for 20%

profile of v4, /device:TPU:8, one launch (start us, length us, event | category | flops | bytes accessed | tf_op | source)
XLA Modules:
  0.0 209.3 jit_solution(4748632417203847334)
XLA Ops:
  0.7 0.9 fusion.19
  1.5 2.7 %multiply_reduce_fusion = f32[1024,4]{1,0:T(8,128)S(1)} fusion(bf16[1024,4,1,128]{3,1,2,0:T(4,128)(2,1)} %param.11, bf16[1024,4,1,128]{3,1,2,0:T(4,128)(2,1)} %param.10), kind=kLoop, calls=%fused_computation.3 | loop fusion | flops 2093056 | bytes 2113536 | tf_op jit(solution)/shard_map/reduce_sum | solution.py:285
  4.3 0.2 copy.62
  4.6 0.3 copy_bitcast_fusion
  4.9 1.5 pad_maximum_fusion
  6.4 5.0 %all-to-all-start = ((bf16[4,2096,128]{2,1,0:T(8,128)(2,1)}), bf16[4,2096,128]{2,1,0:T(8,128)(2,1)S(1)}, u32[]{:S(2)}, u32[]{:S(2)}) async-start(bf16[4,2096,128]{2,1,0:T(8,128)(2,1)} %pad_maximum_fusion), calls=%async_computation | async-start | bytes 4292608 | tf_op jit(solution)/shard_map/all_to_all | solution.py:283
  11.5 25.4 %all-to-all-done.q_ref.g_ref.refs_0_.refs_1_ = bf16[4,2096,128]{2,1,0:T(8,128)(2,1)S(1)} async-done(((bf16[4,2096,128]{2,1,0:T(8,128)(2,1)}), bf16[4,2096,128]{2,1,0:T(8,128)(2,1)S(1)}, u32[]{:S(2)}, u32[]{:S(2)}) %all-to-all-start) | async-done | bytes 2146336 | tf_op jit(solution)/shard_map/all_to_all | solution.py:283
  36.9 3.1 %constant_dynamic-slice_fusion = (bf16[1024,1,128]{2,1,0:T(2,128)(2,1)S(1)}, bf16[1024,1,128]{2,1,0:T(2,128)(2,1)S(1)}) fusion(bf16[1024,4,128]{2,1,0:T(4,128)(2,1)S(1)} %copy-done.17, s32[]{:T(128)S(6)} %select_n.140, bf16[1024,4,128]{2,1,0:T(4,128)(2,1)} %param.8), kind=kLoop, calls=%fused_computation.80 | loop fusion | bytes 1048580 | tf_op jit(solution)/shard_map/jit(dynamic_index_in_dim)/dynamic_slice | solution.py:269
  40.1 1.1 pad_maximum_fusion.2
  41.2 2.8 %collective-permute-start.3 = (bf16[2,1024,128]{2,1,0:T(8,128)(2,1)}, bf16[2,1024,128]{2,1,0:T(8,128)(2,1)S(1)}, u32[]{:S(2)}, u32[]{:S(2)}) collective-permute-start(bf16[2,1024,128]{2,1,0:T(8,128)(2,1)} %get-tuple-element.57), channel_id=1, source_target_pairs={{0,96},{4,28},{8,104},{12,4},{16,112},{20,12},{24,120},{28,20},{32... | collective-permute-start | bytes 1572872 | tf_op jit(solution)/shard_map/ppermute | solution.py:44
  43.9 2.3 %collective-permute-start.4 = (bf16[2,1024,128]{2,1,0:T(8,128)(2,1)}, bf16[2,1024,128]{2,1,0:T(8,128)(2,1)}, u32[]{:S(2)}, u32[]{:S(2)}) collective-permute-start(bf16[2,1024,128]{2,1,0:T(8,128)(2,1)} %get-tuple-element.57), channel_id=1, source_target_pairs={{0,64},{4,20},{8,72},{12,28},{16,80},{20,4},{24,88},{28,12},{32,96... | collective-permute-start | bytes 1572872 | tf_op jit(solution)/shard_map/ppermute | solution.py:44
  46.2 10.4 %collective-permute-done.3 = bf16[2,1024,128]{2,1,0:T(8,128)(2,1)S(1)} collective-permute-done((bf16[2,1024,128]{2,1,0:T(8,128)(2,1)}, bf16[2,1024,128]{2,1,0:T(8,128)(2,1)S(1)}, u32[]{:S(2)}, u32[]{:S(2)}) %collective-permute-start.3) | collective-permute-done | bytes 524320 | tf_op jit(solution)/shard_map/ppermute | solution.py:44
  56.6 4.0 %collective-permute-start.8 = (bf16[1,2,1024,128]{3,2,1,0:T(8,128)(2,1)}, bf16[1,2,1024,128]{3,2,1,0:T(8,128)(2,1)}, u32[]{:S(2)}, u32[]{:S(2)}) collective-permute-start(bf16[1,2,1024,128]{3,2,1,0:T(8,128)(2,1)} %get-tuple-element.58.refs_6_), channel_id=1, source_target_pairs={{0,24},{4,100},{8,0},{12,108},{16,8},{20,116},{24,16},{28,124},{32... | collective-permute-start | bytes 1572872 | tf_op jit(solution)/shard_map/ppermute | solution.py:44
  60.6 0.1 pad_maximum_fusion.1.refs_7_
  60.8 3.6 %collective-permute-start.9 = (bf16[2,2,1024,128]{3,2,1,0:T(8,128)(2,1)S(1)}, bf16[2,2,1024,128]{3,2,1,0:T(8,128)(2,1)}, u32[]{:S(2)}, u32[]{:S(2)}) collective-permute-start(bf16[2,2,1024,128]{3,2,1,0:T(8,128)(2,1)S(1)} %pad_maximum_fusion.1.refs_7_), channel_id=1, source_target_pairs={{0,24},{4,100},{8,0},{12,108},{16,8},{20,116},{24,16},{28,124},{32... | collective-permute-start | bytes 3145736 | tf_op jit(solution)/shard_map/ppermute | solution.py:44
  64.6 0.7 pad_add_fusion.tbl
  65.4 2.3 %collective-permute-done.8.refs_9_ = bf16[1,2,1024,128]{3,2,1,0:T(8,128)(2,1)} collective-permute-done((bf16[1,2,1024,128]{3,2,1,0:T(8,128)(2,1)}, bf16[1,2,1024,128]{3,2,1,0:T(8,128)(2,1)}, u32[]{:S(2)}, u32[]{:S(2)}) %collective-permute-start.8) | collective-permute-done | bytes 524320 | tf_op jit(solution)/shard_map/ppermute | solution.py:44
  67.7 11.1 %collective-permute-done.9.refs_10_ = bf16[2,2,1024,128]{3,2,1,0:T(8,128)(2,1)} collective-permute-done((bf16[2,2,1024,128]{3,2,1,0:T(8,128)(2,1)S(1)}, bf16[2,2,1024,128]{3,2,1,0:T(8,128)(2,1)}, u32[]{:S(2)}, u32[]{:S(2)}) %collective-permute-start.9) | collective-permute-done | bytes 1048608 | tf_op jit(solution)/shard_map/ppermute | solution.py:44
  78.8 3.8 %collective-permute-start.10 = (bf16[1,2,1024,128]{3,2,1,0:T(8,128)(2,1)}, bf16[1,2,1024,128]{3,2,1,0:T(8,128)(2,1)}, u32[]{:S(2)}, u32[]{:S(2)}) collective-permute-start(bf16[1,2,1024,128]{3,2,1,0:T(8,128)(2,1)} %bitcast.24.refs_8_), channel_id=1, source_target_pairs={{0,24},{4,100},{8,0},{12,108},{16,8},{20,116},{24,16},{28,124},{32... | collective-permute-start | bytes 1572872 | tf_op jit(solution)/shard_map/ppermute | solution.py:44
  82.6 0.6 reshape.240.st_ref.refs_4_
  83.3 0.8 slice.162
  84.1 2.2 %collective-permute-done.5.refs_6_ = bf16[1,2,1024,128]{3,2,1,0:T(8,128)(2,1)} collective-permute-done((bf16[1,2,1024,128]{3,2,1,0:T(8,128)(2,1)}, bf16[1,2,1024,128]{3,2,1,0:T(8,128)(2,1)}, u32[]{:S(2)}, u32[]{:S(2)}) %collective-permute-start.5) | collective-permute-done | bytes 524320 | tf_op jit(solution)/shard_map/ppermute | solution.py:44
  86.2 5.6 %collective-permute-done.7.refs_8_ = bf16[1,2,1024,128]{3,2,1,0:T(8,128)(2,1)} collective-permute-done((bf16[1,2,1024,128]{3,2,1,0:T(8,128)(2,1)}, bf16[1,2,1024,128]{3,2,1,0:T(8,128)(2,1)}, u32[]{:S(2)}, u32[]{:S(2)}) %collective-permute-start.7) | collective-permute-done | bytes 524320 | tf_op jit(solution)/shard_map/ppermute | solution.py:44
  91.9 0.6 reshape.241.refs_5_
  92.5 10.5 %remote.4 = (bf16[4,1024,128]{2,1,0:T(8,128)(2,1)}, bf16[4,1024,128]{2,1,0:T(8,128)(2,1)}, bf16[4,2,1024,128]{3,2,1,0:T(8,128)(2,1)}, bf16[4,2,1024,128]{3,2,1,0:T(8,128)(2,1)}) custom-call(s32[32]{0:T(128)} %pad_add_fusion.tbl, bf16[4,2096,128]{2,1,0:T(8,128)(2,1)} %copy-done, bf16[4,2096,128]{2,1,0:T(8,128)(2,1)} %copy-done, ...), custom_call_target="tpu_custom_call" | custom-call | flops 5368709120 | bytes 16777216 | tf_op jit(solution)/shard_map/remote/pallas_call | solution.py:224
  103.0 9.2 %collective-permute-start.15 = (bf16[4,2,1024,128]{3,2,1,0:T(8,128)(2,1)}, bf16[4,2,1024,128]{3,2,1,0:T(8,128)(2,1)}, u32[]{:S(2)}, u32[]{:S(2)}) collective-permute-start(bf16[4,2,1024,128]{3,2,1,0:T(8,128)(2,1)} %get-tuple-element.24), channel_id=1, source_target_pairs={{0,24},{4,100},{8,0},{12,108},{16,8},{20,116},{24,16},{28,124},{32... | collective-permute-start | bytes 6291464 | tf_op jit(solution)/shard_map/ppermute | solution.py:44
  112.3 0.8 copy-done.15
  113.0 0.2 copy-done.16
  113.2 1.0 copy-done.12
  114.2 7.4 %remote.5 = (bf16[4,1024,128]{2,1,0:T(8,128)(2,1)}, bf16[4,1024,128]{2,1,0:T(8,128)(2,1)}, bf16[4,2,1024,128]{3,2,1,0:T(8,128)(2,1)}) custom-call(s32[32]{0:T(128)} %pad_add_fusion.tbl, bf16[4,2096,128]{2,1,0:T(8,128)(2,1)} %copy-done, bf16[4,2096,128]{2,1,0:T(8,128)(2,1)} %copy-done, bf16[4,2096,128]{2,1,0:T(8,128)(2,1)} %collective-permute-done.1.refs_2_.refs_3_, ...), custom_call_target="tpu_custom_call" | custom-call | flops 2684354560 | bytes 12582912 | tf_op jit(solution)/shard_map/remote/pallas_call | solution.py:224
  121.6 2.5 %slice_bitcast_fusion.4 = (bf16[2,1024,128]{2,1,0:T(8,128)(2,1)S(1)}, bf16[2,1024,128]{2,1,0:T(8,128)(2,1)}, bf16[2,1024,128]{2,1,0:T(8,128)(2,1)}) fusion(bf16[4,2,1024,128]{3,2,1,0:T(8,128)(2,1)} %get-tuple-element.26), kind=kLoop, calls=%fused_computation.30 | loop fusion | bytes 3145728 | tf_op jit(solution)/shard_map/squeeze | solution.py:333
  124.2 16.3 %collective-permute-start.20 = (bf16[2,1024,128]{2,1,0:T(8,128)(2,1)S(1)}, bf16[2,1024,128]{2,1,0:T(8,128)(2,1)S(1)}, u32[]{:S(2)}, u32[]{:S(2)}) collective-permute-start(bf16[2,1024,128]{2,1,0:T(8,128)(2,1)S(1)} %get-tuple-element.54), channel_id=1, source_target_pairs={{0,96},{4,28},{8,104},{12,4},{16,112},{20,12},{24,120},{28,20},{32... | collective-permute-start | bytes 1572872 | tf_op jit(solution)/shard_map/ppermute | solution.py:44
  140.4 8.9 %remote.3 = (bf16[4,1024,128]{2,1,0:T(8,128)(2,1)}, bf16[4,1024,128]{2,1,0:T(8,128)(2,1)}, bf16[4,2,1024,128]{3,2,1,0:T(8,128)(2,1)}) custom-call(s32[32]{0:T(128)} %pad_add_fusion.tbl, bf16[4,2096,128]{2,1,0:T(8,128)(2,1)} %copy-done, bf16[4,2096,128]{2,1,0:T(8,128)(2,1)} %copy-done, bf16[4,2096,128]{2,1,0:T(8,128)(2,1)} %collective-permute-done.1.refs_2_.refs_3_, ...), custom_call_target="tpu_custom_call" | custom-call | flops 2684354560 | bytes 12582912 | tf_op jit(solution)/shard_map/remote/pallas_call | solution.py:224
  149.4 2.6 %add_convert_fusion = bf16[4,1024,128]{2,1,0:T(8,128)(2,1)} fusion(bf16[4,1024,128]{2,1,0:T(8,128)(2,1)S(1)} %copy-done.11, bf16[4,1024,128]{2,1,0:T(8,128)(2,1)S(1)} %copy-done.10, bf16[4,1024,128]{2,1,0:T(8,128)(2,1)} %get-tuple-element.20), kind=kLoop, calls=%fused_computation.2 | loop fusion | flops 3145728 | bytes 4194304 | tf_op jit(solution)/shard_map/convert_element_type | solution.py:348
  152.0 4.4 %collective-permute-start.21 = (bf16[2,1024,128]{2,1,0:T(8,128)(2,1)}, bf16[2,1024,128]{2,1,0:T(8,128)(2,1)}, u32[]{:S(2)}, u32[]{:S(2)}) collective-permute-start(bf16[2,1024,128]{2,1,0:T(8,128)(2,1)} %get-tuple-element.56), channel_id=1, source_target_pairs={{0,32},{4,12},{8,40},{12,20},{16,48},{20,28},{24,56},{28,4},{32,64... | collective-permute-start | bytes 1572872 | tf_op jit(solution)/shard_map/ppermute | solution.py:44
  156.3 15.2 %own.1 = (f32[4,1024,128]{2,1,0:T(8,128)}, f32[1024,128]{1,0:T(8,128)}, f32[1024,128]{1,0:T(8,128)}) custom-call(bf16[4,2096,128]{2,1,0:T(8,128)(2,1)} %copy-done, bf16[4,2096,128]{2,1,0:T(8,128)(2,1)} %copy-done, f32[8,2,512]{2,1,0:T(2,128)} %reshape.240.st_ref.refs_4_, bf16[1024,128]{1,0:T(8,128)(2,1)} %bitcast.105, bf16[1024,128]{1,0:T(8,128)(2,1)} %bitcast.103), custom_call_target="tpu_custom_call" | custom-call | flops 3221225472 | bytes 8388608 | tf_op jit(solution)/shard_map/own/pallas_call | solution.py:107
  171.6 2.6 %fusion.2 = bf16[2,1024,128]{2,1,0:T(8,128)(2,1)} fusion(bf16[2,1024,128]{2,1,0:T(8,128)(2,1)} %collective-permute-done.22, bf16[2,1024,128]{2,1,0:T(8,128)(2,1)} %collective-permute-done.21, bf16[2,1024,128]{2,1,0:T(8,128)(2,1)S(1)} %collective-permute-done.20, bf16[4,2,1024,128]{3,2,1,0:T(8,128)(2,1)} %get-tuple-element.26), kind=kLoop, calls=%fused_computation.8 | loop fusion | flops 2097152 | bytes 2621440 | tf_op jit(solution)/shard_map/convert_element_type | solution.py:336
  174.1 1.2 collective-permute-start.23
  175.4 2.9 %multiply_convert_fusion = bf16[4,1024,128]{2,1,0:T(8,128)(2,1)} fusion(f32[4,1024,128]{2,1,0:T(8,128)S(1)} %copy-done.3, bf16[4,1024,128]{2,1,0:T(8,128)(2,1)} %collective-permute-done.14, bf16[4,1024,128]{2,1,0:T(8,128)(2,1)S(1)} %copy-done.5, bf16[4,1024,128]{2,1,0:T(8,128)(2,1)S(1)} %copy-done.4, bf16[4,1024,128]{2,1,0:T(8,128)(2,1)S(1)} %copy-done.6), kind=kLoop, calls=%fused_computation.1 | loop fusion | flops 5242880 | bytes 7340032 | tf_op jit(solution)/shard_map/convert_element_type | solution.py:350
  178.3 4.9 %all-to-all-start.1 = ((bf16[4,1024,128]{2,1,0:T(8,128)(2,1)}), bf16[4,1024,128]{2,1,0:T(8,128)(2,1)S(1)}, u32[]{:S(2)}, u32[]{:S(2)}) async-start(bf16[4,1024,128]{2,1,0:T(8,128)(2,1)} %multiply_convert_fusion), calls=%async_computation.1 | async-start | bytes 2097152 | tf_op jit(solution)/shard_map/all_to_all | solution.py:283
  183.2 4.5 %fusion.3 = (bf16[2,1024,128]{2,1,0:T(8,128)(2,1)}, bf16[2,1024,128]{2,1,0:T(8,128)(2,1)}, bf16[2,1024,128]{2,1,0:T(8,128)(2,1)}, f32[1,2,1024,128]{3,2,1,0:T(8,128)S(1)}) fusion(bf16[4,2,1024,128]{3,2,1,0:T(8,128)(2,1)} %collective-permute-done.16, bf16[4,2,1024,128]{3,2,1,0:T(8,128)(2,1)} %collective-permute-done.15, ...), kind=kLoop, calls=%fused_computation.15 | loop fusion | flops 6029312 | bytes 8912896 | tf_op jit(solution)/shard_map/convert_element_type | solution.py:338
  187.8 2.3 %collective-permute-start.17 = (bf16[2,1024,128]{2,1,0:T(8,128)(2,1)}, bf16[2,1024,128]{2,1,0:T(8,128)(2,1)}, u32[]{:S(2)}, u32[]{:S(2)}) collective-permute-start(bf16[2,1024,128]{2,1,0:T(8,128)(2,1)} %get-tuple-element.48), channel_id=1, source_target_pairs={{0,96},{4,28},{8,104},{12,4},{16,112},{20,12},{24,120},{28,20},{32... | collective-permute-start | bytes 1572872 | tf_op jit(solution)/shard_map/ppermute | solution.py:44
  190.0 2.2 %collective-permute-start.19 = (bf16[2,1024,128]{2,1,0:T(8,128)(2,1)}, bf16[2,1024,128]{2,1,0:T(8,128)(2,1)}, u32[]{:S(2)}, u32[]{:S(2)}) collective-permute-start(bf16[2,1024,128]{2,1,0:T(8,128)(2,1)} %get-tuple-element.49), channel_id=1, source_target_pairs={{0,64},{4,20},{8,72},{12,28},{16,80},{20,4},{24,88},{28,12},{32,96... | collective-permute-start | bytes 1572872 | tf_op jit(solution)/shard_map/ppermute | solution.py:44
  192.3 4.2 %all-to-all-done.1 = bf16[4,1024,128]{2,1,0:T(8,128)(2,1)S(1)} async-done(((bf16[4,1024,128]{2,1,0:T(8,128)(2,1)}), bf16[4,1024,128]{2,1,0:T(8,128)(2,1)S(1)}, u32[]{:S(2)}, u32[]{:S(2)}) %all-to-all-start.1) | async-done | bytes 1048608 | tf_op jit(solution)/shard_map/all_to_all | solution.py:283
  196.5 1.8 copy.72
  198.3 4.5 %collective-permute-done.17 = bf16[2,1024,128]{2,1,0:T(8,128)(2,1)} collective-permute-done((bf16[2,1024,128]{2,1,0:T(8,128)(2,1)}, bf16[2,1024,128]{2,1,0:T(8,128)(2,1)}, u32[]{:S(2)}, u32[]{:S(2)}) %collective-permute-start.17) | collective-permute-done | bytes 524320 | tf_op jit(solution)/shard_map/ppermute | solution.py:44
  202.7 3.9 %collective-permute-done.18 = bf16[2,1024,128]{2,1,0:T(8,128)(2,1)} collective-permute-done((bf16[2,1024,128]{2,1,0:T(8,128)(2,1)}, bf16[2,1024,128]{2,1,0:T(8,128)(2,1)}, u32[]{:S(2)}, u32[]{:S(2)}) %collective-permute-start.18) | collective-permute-done | bytes 524320 | tf_op jit(solution)/shard_map/ppermute | solution.py:44
  206.7 2.7 %fusion.14 = (bf16[1024,1,128]{2,0,1:T(8,128)(2,1)}, bf16[1024,1,128]{2,0,1:T(8,128)(2,1)}) fusion(f32[1024,128]{1,0:T(8,128)S(1)} %copy-done.14, f32[1,2,1024,128]{3,2,1,0:T(8,128)S(1)} %get-tuple-element.51, bf16[2,1024,128]{2,1,0:T(8,128)(2,1)} %collective-permute-done.23, bf16[2,1024,128]{2,1,0:T(8,128)(2,1)} %collective-permute-done.19, ...), kind=kLoop, calls=%fused_computation.32 | loop fusion | flops 2752512 | bytes 4718592 | tf_op jit(solution)/shard_map/broadcast_in_dim | solution.py:352
  (81 shorter events, 0.8 us)
Async XLA Ops:
  0.6 4.0 %copy-start.1 = (bf16[1024,4,1,128]{3,1,2,0:T(4,128)(2,1)S(1)}, bf16[1024,4,1,128]{3,1,2,0:T(4,128)(2,1)}, u32[]{:S(2)}) copy-start(bf16[1024,4,1,128]{3,1,2,0:T(4,128)(2,1)} %param.10) | copy-start | bytes 3145732
  0.6 4.0 %copy-start.9 = (bf16[1024,4,1,128]{3,1,2,0:T(4,128)(2,1)S(1)}, bf16[1024,4,1,128]{3,1,2,0:T(4,128)(2,1)}, u32[]{:S(2)}) copy-start(bf16[1024,4,1,128]{3,1,2,0:T(4,128)(2,1)} %param.7) | copy-start | bytes 3145732
  6.4 30.5 %copy-start.17 = (bf16[1024,4,128]{2,1,0:T(4,128)(2,1)S(1)}, bf16[1024,4,128]{2,1,0:T(4,128)(2,1)}, u32[]{:S(2)}) copy-start(bf16[1024,4,128]{2,1,0:T(4,128)(2,1)} %param.9) | copy-start | bytes 3145732
  6.4 30.4 %all-to-all-start = ((bf16[4,2096,128]{2,1,0:T(8,128)(2,1)}), bf16[4,2096,128]{2,1,0:T(8,128)(2,1)S(1)}, u32[]{:S(2)}, u32[]{:S(2)}) async-start(bf16[4,2096,128]{2,1,0:T(8,128)(2,1)} %pad_maximum_fusion), calls=%async_computation | async-start | bytes 4292608 | tf_op jit(solution)/shard_map/all_to_all | solution.py:283
  36.9 28.4 %copy-start = (bf16[4,2096,128]{2,1,0:T(8,128)(2,1)}, bf16[4,2096,128]{2,1,0:T(8,128)(2,1)S(1)}, u32[]{:S(2)}) copy-start(bf16[4,2096,128]{2,1,0:T(8,128)(2,1)S(1)} %all-to-all-done.q_ref.g_ref.refs_0_.refs_1_) | copy-start | bytes 6438916
  36.9 45.7 %collective-permute-start.1 = (bf16[4,2096,128]{2,1,0:T(8,128)(2,1)S(1)}, bf16[4,2096,128]{2,1,0:T(8,128)(2,1)}, u32[]{:S(2)}, u32[]{:S(2)}) collective-permute-start(bf16[4,2096,128]{2,1,0:T(8,128)(2,1)S(1)} %all-to-all-done.q_ref.g_ref.refs_0_.refs_1_), channel_id=1, source_target_pairs={{0,4},{4,0},{8,12},{12,8},{16,20},{20,16},{24,28},{28,24},{32,36},... | collective-permute-start | bytes 6438920 | tf_op jit(solution)/shard_map/ppermute | solution.py:48
  40.0 6.3 %copy-start.18 = (s32[8,3]{0,1:T(4,128)S(1)}, s32[8,3]{0,1:T(4,128)}, u32[]{:S(2)}) copy-start(s32[8,3]{0,1:T(4,128)} %param.13) | copy-start | bytes 292
  40.0 20.7 %copy-start.7 = (bf16[1024,1,128]{2,0,1:T(8,128)(2,1)}, bf16[1024,1,128]{2,0,1:T(8,128)(2,1)S(1)}, u32[]{:S(2)}) copy-start(bf16[1024,1,128]{2,0,1:T(8,128)(2,1)S(1)} %copy.104) | copy-start | bytes 786436
  40.1 20.6 %copy-start.8 = (bf16[1024,1,128]{2,0,1:T(8,128)(2,1)}, bf16[1024,1,128]{2,0,1:T(8,128)(2,1)S(1)}, u32[]{:S(2)}) copy-start(bf16[1024,1,128]{2,0,1:T(8,128)(2,1)S(1)} %copy.105) | copy-start | bytes 786436
  41.2 15.4 %collective-permute-start.3 = (bf16[2,1024,128]{2,1,0:T(8,128)(2,1)}, bf16[2,1024,128]{2,1,0:T(8,128)(2,1)S(1)}, u32[]{:S(2)}, u32[]{:S(2)}) collective-permute-start(bf16[2,1024,128]{2,1,0:T(8,128)(2,1)} %get-tuple-element.57), channel_id=1, source_target_pairs={{0,96},{4,28},{8,104},{12,4},{16,112},{20,12},{24,120},{28,20},{32... | collective-permute-start | bytes 1572872 | tf_op jit(solution)/shard_map/ppermute | solution.py:44
  43.9 16.7 %collective-permute-start.2 = (bf16[2,1024,128]{2,1,0:T(8,128)(2,1)}, bf16[2,1024,128]{2,1,0:T(8,128)(2,1)S(1)}, u32[]{:S(2)}, u32[]{:S(2)}) collective-permute-start(bf16[2,1024,128]{2,1,0:T(8,128)(2,1)} %get-tuple-element.57), channel_id=1, source_target_pairs={{0,32},{4,12},{8,40},{12,20},{16,48},{20,28},{24,56},{28,4},{32,64... | collective-permute-start | bytes 1572872 | tf_op jit(solution)/shard_map/ppermute | solution.py:44
  43.9 21.4 %collective-permute-start.4 = (bf16[2,1024,128]{2,1,0:T(8,128)(2,1)}, bf16[2,1024,128]{2,1,0:T(8,128)(2,1)}, u32[]{:S(2)}, u32[]{:S(2)}) collective-permute-start(bf16[2,1024,128]{2,1,0:T(8,128)(2,1)} %get-tuple-element.57), channel_id=1, source_target_pairs={{0,64},{4,20},{8,72},{12,28},{16,80},{20,4},{24,88},{28,12},{32,96... | collective-permute-start | bytes 1572872 | tf_op jit(solution)/shard_map/ppermute | solution.py:44
  46.2 18.2 %collective-permute-start = (s32[8,3]{0,1:T(4,128)S(1)}, s32[8,3]{0,1:T(4,128)S(1)}, u32[]{:S(2)}, u32[]{:S(2)}) collective-permute-start(s32[8,3]{0,1:T(4,128)S(1)} %copy-done.18), channel_id=1, source_target_pairs={{0,4},{4,0},{8,12},{12,8},{16,20},{20,16},{24,28},{28,24},{32,36},... | collective-permute-start | bytes 296 | tf_op jit(solution)/shard_map/ppermute | solution.py:48
  56.6 11.1 %collective-permute-start.8 = (bf16[1,2,1024,128]{3,2,1,0:T(8,128)(2,1)}, bf16[1,2,1024,128]{3,2,1,0:T(8,128)(2,1)}, u32[]{:S(2)}, u32[]{:S(2)}) collective-permute-start(bf16[1,2,1024,128]{3,2,1,0:T(8,128)(2,1)} %get-tuple-element.58.refs_6_), channel_id=1, source_target_pairs={{0,24},{4,100},{8,0},{12,108},{16,8},{20,116},{24,16},{28,124},{32... | collective-permute-start | bytes 1572872 | tf_op jit(solution)/shard_map/ppermute | solution.py:44
  60.8 42.3 %copy-start.2 = (bf16[2,2,1024,128]{3,2,1,0:T(8,128)(2,1)}, bf16[2,2,1024,128]{3,2,1,0:T(8,128)(2,1)S(1)}, u32[]{:S(2)}) copy-start(bf16[2,2,1024,128]{3,2,1,0:T(8,128)(2,1)S(1)} %pad_maximum_fusion.1.refs_7_) | copy-start | bytes 3145732
  60.8 18.0 %collective-permute-start.9 = (bf16[2,2,1024,128]{3,2,1,0:T(8,128)(2,1)S(1)}, bf16[2,2,1024,128]{3,2,1,0:T(8,128)(2,1)}, u32[]{:S(2)}, u32[]{:S(2)}) collective-permute-start(bf16[2,2,1024,128]{3,2,1,0:T(8,128)(2,1)S(1)} %pad_maximum_fusion.1.refs_7_), channel_id=1, source_target_pairs={{0,24},{4,100},{8,0},{12,108},{16,8},{20,116},{24,16},{28,124},{32... | collective-permute-start | bytes 3145736 | tf_op jit(solution)/shard_map/ppermute | solution.py:44
  64.4 28.1 %collective-permute-start.6 = (bf16[2,2,1024,128]{3,2,1,0:T(8,128)(2,1)S(1)}, bf16[2,2,1024,128]{3,2,1,0:T(8,128)(2,1)}, u32[]{:S(2)}, u32[]{:S(2)}) collective-permute-start(bf16[2,2,1024,128]{3,2,1,0:T(8,128)(2,1)S(1)} %pad_maximum_fusion.1.refs_7_), channel_id=1, source_target_pairs={{0,8},{4,36},{8,16},{12,44},{16,24},{20,52},{24,0},{28,60},{32,40}... | collective-permute-start | bytes 3145736 | tf_op jit(solution)/shard_map/ppermute | solution.py:44
  65.3 20.9 %collective-permute-start.5 = (bf16[1,2,1024,128]{3,2,1,0:T(8,128)(2,1)}, bf16[1,2,1024,128]{3,2,1,0:T(8,128)(2,1)}, u32[]{:S(2)}, u32[]{:S(2)}) collective-permute-start(bf16[1,2,1024,128]{3,2,1,0:T(8,128)(2,1)} %get-tuple-element.58.refs_6_), channel_id=1, source_target_pairs={{0,8},{4,36},{8,16},{12,44},{16,24},{20,52},{24,0},{28,60},{32,40}... | collective-permute-start | bytes 1572872 | tf_op jit(solution)/shard_map/ppermute | solution.py:44
  67.7 24.2 %collective-permute-start.7 = (bf16[1,2,1024,128]{3,2,1,0:T(8,128)(2,1)}, bf16[1,2,1024,128]{3,2,1,0:T(8,128)(2,1)}, u32[]{:S(2)}, u32[]{:S(2)}) collective-permute-start(bf16[1,2,1024,128]{3,2,1,0:T(8,128)(2,1)} %bitcast.24.refs_8_), channel_id=1, source_target_pairs={{0,8},{4,36},{8,16},{12,44},{16,24},{20,52},{24,0},{28,60},{32,40}... | collective-permute-start | bytes 1572872 | tf_op jit(solution)/shard_map/ppermute | solution.py:44
  78.8 13.7 %collective-permute-start.10 = (bf16[1,2,1024,128]{3,2,1,0:T(8,128)(2,1)}, bf16[1,2,1024,128]{3,2,1,0:T(8,128)(2,1)}, u32[]{:S(2)}, u32[]{:S(2)}) collective-permute-start(bf16[1,2,1024,128]{3,2,1,0:T(8,128)(2,1)} %bitcast.24.refs_8_), channel_id=1, source_target_pairs={{0,24},{4,100},{8,0},{12,108},{16,8},{20,116},{24,16},{28,124},{32... | collective-permute-start | bytes 1572872 | tf_op jit(solution)/shard_map/ppermute | solution.py:44
  82.6 29.7 %collective-permute-start.12 = (bf16[2,2,1024,128]{3,2,1,0:T(8,128)(2,1)}, bf16[2,2,1024,128]{3,2,1,0:T(8,128)(2,1)S(1)}, u32[]{:S(2)}, u32[]{:S(2)}) collective-permute-start(bf16[2,2,1024,128]{3,2,1,0:T(8,128)(2,1)} %collective-permute-done.9.refs_10_), channel_id=1, source_target_pairs={{0,24},{4,100},{8,0},{12,108},{16,8},{20,116},{24,16},{28,124},{32... | collective-permute-start | bytes 3145736 | tf_op jit(solution)/shard_map/ppermute | solution.py:44
  86.2 26.0 %collective-permute-start.11 = (bf16[1,2,1024,128]{3,2,1,0:T(8,128)(2,1)}, bf16[1,2,1024,128]{3,2,1,0:T(8,128)(2,1)S(1)}, u32[]{:S(2)}, u32[]{:S(2)}) collective-permute-start(bf16[1,2,1024,128]{3,2,1,0:T(8,128)(2,1)} %collective-permute-done.5.refs_6_), channel_id=1, source_target_pairs={{0,8},{4,36},{8,16},{12,44},{16,24},{20,52},{24,0},{28,60},{32,40}... | collective-permute-start | bytes 1572872 | tf_op jit(solution)/shard_map/ppermute | solution.py:44
  91.9 20.4 %collective-permute-start.13 = (bf16[1,2,1024,128]{3,2,1,0:T(8,128)(2,1)}, bf16[1,2,1024,128]{3,2,1,0:T(8,128)(2,1)S(1)}, u32[]{:S(2)}, u32[]{:S(2)}) collective-permute-start(bf16[1,2,1024,128]{3,2,1,0:T(8,128)(2,1)} %collective-permute-done.7.refs_8_), channel_id=1, source_target_pairs={{0,8},{4,36},{8,16},{12,44},{16,24},{20,52},{24,0},{28,60},{32,40}... | collective-permute-start | bytes 1572872 | tf_op jit(solution)/shard_map/ppermute | solution.py:44
  103.0 80.2 %collective-permute-start.15 = (bf16[4,2,1024,128]{3,2,1,0:T(8,128)(2,1)}, bf16[4,2,1024,128]{3,2,1,0:T(8,128)(2,1)}, u32[]{:S(2)}, u32[]{:S(2)}) collective-permute-start(bf16[4,2,1024,128]{3,2,1,0:T(8,128)(2,1)} %get-tuple-element.24), channel_id=1, source_target_pairs={{0,24},{4,100},{8,0},{12,108},{16,8},{20,116},{24,16},{28,124},{32... | collective-permute-start | bytes 6291464 | tf_op jit(solution)/shard_map/ppermute | solution.py:44
  112.2 71.0 %collective-permute-start.16 = (bf16[4,2,1024,128]{3,2,1,0:T(8,128)(2,1)}, bf16[4,2,1024,128]{3,2,1,0:T(8,128)(2,1)}, u32[]{:S(2)}, u32[]{:S(2)}) collective-permute-start(bf16[4,2,1024,128]{3,2,1,0:T(8,128)(2,1)} %get-tuple-element.25), channel_id=1, source_target_pairs={{0,8},{4,36},{8,16},{12,44},{16,24},{20,52},{24,0},{28,60},{32,40}... | collective-permute-start | bytes 6291464 | tf_op jit(solution)/shard_map/ppermute | solution.py:44
  112.2 0.8 copy-start.15
  112.2 1.0 copy-start.16
  113.2 1.0 copy-start.12
  124.2 25.2 %copy-start.10 = (bf16[4,1024,128]{2,1,0:T(8,128)(2,1)S(1)}, bf16[4,1024,128]{2,1,0:T(8,128)(2,1)}, u32[]{:S(2)}) copy-start(bf16[4,1024,128]{2,1,0:T(8,128)(2,1)} %get-tuple-element.21) | copy-start | bytes 3145732
  124.2 25.2 %copy-start.11 = (bf16[4,1024,128]{2,1,0:T(8,128)(2,1)S(1)}, bf16[4,1024,128]{2,1,0:T(8,128)(2,1)}, u32[]{:S(2)}) copy-start(bf16[4,1024,128]{2,1,0:T(8,128)(2,1)} %get-tuple-element.22) | copy-start | bytes 3145732
  124.2 27.8 %collective-permute-start.20 = (bf16[2,1024,128]{2,1,0:T(8,128)(2,1)S(1)}, bf16[2,1024,128]{2,1,0:T(8,128)(2,1)S(1)}, u32[]{:S(2)}, u32[]{:S(2)}) collective-permute-start(bf16[2,1024,128]{2,1,0:T(8,128)(2,1)S(1)} %get-tuple-element.54), channel_id=1, source_target_pairs={{0,96},{4,28},{8,104},{12,4},{16,112},{20,12},{24,120},{28,20},{32... | collective-permute-start | bytes 1572872 | tf_op jit(solution)/shard_map/ppermute | solution.py:44
  152.0 23.4 %collective-permute-start.14 = (bf16[4,1024,128]{2,1,0:T(8,128)(2,1)}, bf16[4,1024,128]{2,1,0:T(8,128)(2,1)}, u32[]{:S(2)}, u32[]{:S(2)}) collective-permute-start(bf16[4,1024,128]{2,1,0:T(8,128)(2,1)} %add_convert_fusion), channel_id=1, source_target_pairs={{0,4},{4,0},{8,12},{12,8},{16,20},{20,16},{24,28},{28,24},{32,36},... | collective-permute-start | bytes 3145736 | tf_op jit(solution)/shard_map/ppermute | solution.py:48
  152.0 19.6 %collective-permute-start.22 = (bf16[2,1024,128]{2,1,0:T(8,128)(2,1)}, bf16[2,1024,128]{2,1,0:T(8,128)(2,1)}, u32[]{:S(2)}, u32[]{:S(2)}) collective-permute-start(bf16[2,1024,128]{2,1,0:T(8,128)(2,1)} %get-tuple-element.55), channel_id=1, source_target_pairs={{0,64},{4,20},{8,72},{12,28},{16,80},{20,4},{24,88},{28,12},{32,96... | collective-permute-start | bytes 1572872 | tf_op jit(solution)/shard_map/ppermute | solution.py:44
  152.0 19.6 %collective-permute-start.21 = (bf16[2,1024,128]{2,1,0:T(8,128)(2,1)}, bf16[2,1024,128]{2,1,0:T(8,128)(2,1)}, u32[]{:S(2)}, u32[]{:S(2)}) collective-permute-start(bf16[2,1024,128]{2,1,0:T(8,128)(2,1)} %get-tuple-element.56), channel_id=1, source_target_pairs={{0,32},{4,12},{8,40},{12,20},{16,48},{20,28},{24,56},{28,4},{32,64... | collective-permute-start | bytes 1572872 | tf_op jit(solution)/shard_map/ppermute | solution.py:44
  156.3 19.1 %copy-start.4 = (bf16[4,1024,128]{2,1,0:T(8,128)(2,1)S(1)}, bf16[4,1024,128]{2,1,0:T(8,128)(2,1)}, u32[]{:S(2)}) copy-start(bf16[4,1024,128]{2,1,0:T(8,128)(2,1)} %get-tuple-element.18) | copy-start | bytes 3145732
  156.3 19.1 %copy-start.5 = (bf16[4,1024,128]{2,1,0:T(8,128)(2,1)S(1)}, bf16[4,1024,128]{2,1,0:T(8,128)(2,1)}, u32[]{:S(2)}) copy-start(bf16[4,1024,128]{2,1,0:T(8,128)(2,1)} %get-tuple-element.19) | copy-start | bytes 3145732
  156.3 19.1 %copy-start.6 = (bf16[4,1024,128]{2,1,0:T(8,128)(2,1)S(1)}, bf16[4,1024,128]{2,1,0:T(8,128)(2,1)}, u32[]{:S(2)}) copy-start(bf16[4,1024,128]{2,1,0:T(8,128)(2,1)} %get-tuple-element.17) | copy-start | bytes 3145732
  171.5 3.9 %copy-start.3 = (f32[4,1024,128]{2,1,0:T(8,128)S(1)}, f32[4,1024,128]{2,1,0:T(8,128)}, u32[]{:S(2)}) copy-start(f32[4,1024,128]{2,1,0:T(8,128)} %get-tuple-element.16) | copy-start | bytes 6291460
  174.1 24.1 %collective-permute-start.23 = (bf16[2,1024,128]{2,1,0:T(8,128)(2,1)}, bf16[2,1024,128]{2,1,0:T(8,128)(2,1)}, u32[]{:S(2)}, u32[]{:S(2)}) collective-permute-start(bf16[2,1024,128]{2,1,0:T(8,128)(2,1)} %fusion.2), channel_id=1, source_target_pairs={{0,16},{4,68},{8,24},{12,76},{16,0},{20,84},{24,8},{28,92},{32,48}... | collective-permute-start | bytes 1572872 | tf_op jit(solution)/shard_map/ppermute | solution.py:44
  178.3 18.2 %all-to-all-start.1 = ((bf16[4,1024,128]{2,1,0:T(8,128)(2,1)}), bf16[4,1024,128]{2,1,0:T(8,128)(2,1)S(1)}, u32[]{:S(2)}, u32[]{:S(2)}) async-start(bf16[4,1024,128]{2,1,0:T(8,128)(2,1)} %multiply_convert_fusion), calls=%async_computation.1 | async-start | bytes 2097152 | tf_op jit(solution)/shard_map/all_to_all | solution.py:283
  187.8 18.9 %copy-start.13 = (f32[1024,128]{1,0:T(8,128)S(1)}, f32[1024,128]{1,0:T(8,128)}, u32[]{:S(2)}) copy-start(f32[1024,128]{1,0:T(8,128)} %get-tuple-element.27) | copy-start | bytes 1572868
  187.8 18.9 %copy-start.14 = (f32[1024,128]{1,0:T(8,128)S(1)}, f32[1024,128]{1,0:T(8,128)}, u32[]{:S(2)}) copy-start(f32[1024,128]{1,0:T(8,128)} %get-tuple-element.28) | copy-start | bytes 1572868
  187.8 14.9 %collective-permute-start.17 = (bf16[2,1024,128]{2,1,0:T(8,128)(2,1)}, bf16[2,1024,128]{2,1,0:T(8,128)(2,1)}, u32[]{:S(2)}, u32[]{:S(2)}) collective-permute-start(bf16[2,1024,128]{2,1,0:T(8,128)(2,1)} %get-tuple-element.48), channel_id=1, source_target_pairs={{0,96},{4,28},{8,104},{12,4},{16,112},{20,12},{24,120},{28,20},{32... | collective-permute-start | bytes 1572872 | tf_op jit(solution)/shard_map/ppermute | solution.py:44
  190.0 12.7 %collective-permute-start.19 = (bf16[2,1024,128]{2,1,0:T(8,128)(2,1)}, bf16[2,1024,128]{2,1,0:T(8,128)(2,1)}, u32[]{:S(2)}, u32[]{:S(2)}) collective-permute-start(bf16[2,1024,128]{2,1,0:T(8,128)(2,1)} %get-tuple-element.49), channel_id=1, source_target_pairs={{0,64},{4,20},{8,72},{12,28},{16,80},{20,4},{24,88},{28,12},{32,96... | collective-permute-start | bytes 1572872 | tf_op jit(solution)/shard_map/ppermute | solution.py:44
  192.3 14.4 %collective-permute-start.18 = (bf16[2,1024,128]{2,1,0:T(8,128)(2,1)}, bf16[2,1024,128]{2,1,0:T(8,128)(2,1)}, u32[]{:S(2)}, u32[]{:S(2)}) collective-permute-start(bf16[2,1024,128]{2,1,0:T(8,128)(2,1)} %get-tuple-element.50), channel_id=1, source_target_pairs={{0,32},{4,12},{8,40},{12,20},{16,48},{20,28},{24,56},{28,4},{32,64... | collective-permute-start | bytes 1572872 | tf_op jit(solution)/shard_map/ppermute | solution.py:44

commit v5 on v4

--- a/solution.py
+++ b/solution.py
@@ -118,7 +118,7 @@
     )(packed, packed, stats, keys, values)
 
 
-def remote_kernel(scale2, bases, offsets, tbl, *refs):
+def remote_kernel(scale2, bases, offsets, out_offsets, tbl, *refs):
     sources = len(offsets) - 1
     q0, g0, q1, g1, st0, st1 = refs[:6]
     blocks = refs[6 : 6 + sources]
@@ -190,7 +190,7 @@
 
     for i, out_ref in enumerate(outs):
 
-        @pl.when(at // SIDE == i)
+        @pl.when((at >= out_offsets[i]) & (at < out_offsets[i + 1]))
         def _():
             out_ref[0] = buf[...]
 
@@ -200,7 +200,7 @@
         out1[...] = dq[1].astype(out1.dtype)
 
 
-def remote_grads(table, own, sib, stats, groups, bases, scale2):
+def remote_grads(table, own, sib, stats, groups, bases, out_sizes, scale2):
     heads, _, width = own.shape
     rows = stats[0].shape[0] * QB
     count = len(bases)
@@ -219,16 +219,19 @@
     offsets = [0]
     for array in operands:
         offsets.append(offsets[-1] + array.shape[0])
+    out_offsets = [0]
+    for size in out_sizes:
+        out_offsets.append(out_offsets[-1] + size)
     acc = jax.ShapeDtypeStruct((heads, rows, width), jnp.bfloat16)
-    part = jax.ShapeDtypeStruct((SIDE, 2, rows, width), jnp.bfloat16)
     return pl.pallas_call(
-        functools.partial(remote_kernel, scale2, bases, offsets),
+        functools.partial(remote_kernel, scale2, bases, offsets, out_offsets),
         grid_spec=pltpu.PrefetchScalarGridSpec(
             num_scalar_prefetch=1,
             grid=(SIDE * count,),
             in_specs=[q_spec, g_spec, q_spec, g_spec, stat, stat]
             + [piece(start, array.shape[0]) for start, array in zip(offsets, operands)],
-            out_specs=[acc_spec, acc_spec] + [piece(SIDE * i, SIDE) for i in range(count)],
+            out_specs=[acc_spec, acc_spec]
+            + [piece(start, size) for start, size in zip(out_offsets, out_sizes)],
             scratch_shapes=[
                 pltpu.VMEM((2, rows, width), jnp.bfloat16),
                 pltpu.VMEM((heads * QB, width), jnp.bfloat16),
@@ -236,7 +239,8 @@
                 pltpu.VMEM((2, heads, rows, width), jnp.float32),
             ],
         ),
-        out_shape=[acc, acc] + [part] * count,
+        out_shape=[acc, acc]
+        + [jax.ShapeDtypeStruct((size, 2, rows, width), jnp.bfloat16) for size in out_sizes],
         compiler_params=pltpu.CompilerParams(vmem_limit_bytes=VMEM_LIMIT),
         cost_estimate=pl.CostEstimate(
             flops=SIDE * count * 10 * heads * QB * rows * width,
@@ -316,14 +320,20 @@
 
     table = jnp.concatenate([listed(selections, me), listed(sib_selections, me + 1 - 2 * core)])
 
-    def remote(groups, bases):
-        return remote_grads(table, own, sib, (own_stats, sib_stats), groups, bases, scale2)
-
-    level0, level1, part_line = remote([line], (0,))
-    first0, first1, part_behind, part_ahead = remote([line_behind, line_ahead], (SIDE, 3 * SIDE))
+    def remote(groups, bases, out_sizes):
+        return remote_grads(
+            table, own, sib, (own_stats, sib_stats), groups, bases, out_sizes, scale2
+        )
+
+    first0, first1, part_behind, part_ahead = remote(
+        [line_behind, line_ahead], (SIDE, 3 * SIDE), (SIDE, SIDE)
+    )
     back_behind = shift(part_behind, 1, -1)
     back_ahead = shift(part_ahead, 1, 1)
-    second0, second1, part_across = remote([line_across], (2 * SIDE,))
+    second0, second1, *part_across, part_line = remote(
+        [line_across, line], (2 * SIDE, 0), (1,) * SIDE + (SIDE,)
+    )
+    part_across = [part[0] for part in part_across]
     own_q, own_k, own_v = own_grads(own, own_stats, keys, values, scale2)
 
     def summed(*parts):
@@ -345,9 +355,9 @@
 
     grad_k, grad_v = final(0, own_k, scale), final(1, own_v, 1.0)
 
-    dq_low = summed(level1, first1, second1).astype(jnp.bfloat16)
+    dq_low = summed(first1, second1).astype(jnp.bfloat16)
     returned = other_core(dq_low)
-    dq = ((own_q + summed(level0, first0, second0, returned)) * scale).astype(jnp.bfloat16)
+    dq = ((own_q + summed(first0, second0, returned)) * scale).astype(jnp.bfloat16)
     dq = jnp.transpose(turn(dq), (1, 0, 2))[:, :, None]
     return dq, grad_k[:, None], grad_v[:, None]
 

time: 210 us -> 202 us (0.962)
  starting transfers between devices: 62.2 us -> 71.2 us
  waiting for transfers between devices: 69.6 us -> 62.9 us
  Pallas kernels: 42.1 us -> 37.8 us
  local copies, waits for them, and re-layouts: 12.1 us -> 8.45 us
    ppermute x21, starting transfers between devices: 52.3 us -> 61.1 us  [shift(): return lax.ppermute(value, 'ctx', pairs(place))]
    ppermute x21, waiting for transfers between devices: 40 us -> 34.3 us  [shift(): return lax.ppermute(value, 'ctx', pairs(place))]
    pallas_call x3 -> x2, Pallas kernels: 26.8 us -> 22.6 us  [remote_grads(): pl.pallas_call(functools.partial(remote_kernel, scale2, bases, offsets, o...]
    squeeze x1 -> x0, local copies, waits for them, and re-layouts: 2.52 us -> none  [spread(): parts[0]]
  transfers between devices with their start and end apart: 26 -> 26, of which waited for: 9 -> 11; matrix products, arithmetic and copies ran while one was open for 12% -> 10% of each run, Pallas kernels for 20% -> 19%
where the time goes in v5:
time: 202 us
  starting transfers between devices  71.2 us (35%)
  waiting for transfers between devices  62.9 us (31%)
  Pallas kernels  37.8 us (19%)
  other arithmetic  20.5 us (10%)
  local copies, waits for them, and re-layouts  8.45 us (4%)
    ppermute x21, starting transfers between devices, shift(): return lax.ppermute(value, 'ctx', pairs(place))  61.1 us
    ppermute x21, waiting for transfers between devices, shift(): return lax.ppermute(value, 'ctx', pairs(place))  34.3 us
    all_to_all x2, waiting for transfers between devices, turn(): lax.all_to_all(value, 'head', split_axis=0, concat_axis=0, tiled=True)  28.6 us
    pallas_call x2, Pallas kernels, remote_grads(): pl.pallas_call(functools.partial(remote_kernel, scale2, bases, offsets, o...  22.6 us
    pallas_call x1, Pallas kernels, own_grads(): pl.pallas_call(functools.partial(own_kernel, scale2), grid=(blocks,), in_...  15.2 us
    all_to_all x2, starting transfers between devices, turn(): lax.all_to_all(value, 'head', split_axis=0, concat_axis=0, tiled=True)  9.98 us
    convert_element_type x1, other arithmetic, grads(): received = spread([part.astype(jnp.bfloat16) for part in total[1:]])  4.52 us
  transfers between devices with their start and end apart: 26, of which 11 were waited for; matrix products, arithmetic and copies ran while one was open for 10% of the time, Pallas kernels for 19%

profile of v5, /device:TPU:8, one launch (start us, length us, event | category | flops | bytes accessed | tf_op | source)
XLA Modules:
  0.0 201.8 jit_solution(1815398805596263105)
XLA Ops:
  0.7 2.9 %multiply_reduce_fusion = f32[1024,4]{1,0:T(8,128)S(1)} fusion(bf16[1024,4,1,128]{3,1,2,0:T(4,128)(2,1)} %param.11, bf16[1024,4,1,128]{3,1,2,0:T(4,128)(2,1)} %param.10), kind=kLoop, calls=%fused_computation.3 | loop fusion | flops 2093056 | bytes 2113536 | tf_op jit(solution)/shard_map/reduce_sum | solution.py:289
  3.5 0.2 copy.62
  3.9 0.3 copy_bitcast_fusion
  4.2 1.5 pad_maximum_fusion
  5.7 5.0 %all-to-all-start = ((bf16[4,2096,128]{2,1,0:T(8,128)(2,1)}), bf16[4,2096,128]{2,1,0:T(8,128)(2,1)S(1)}, u32[]{:S(2)}, u32[]{:S(2)}) async-start(bf16[4,2096,128]{2,1,0:T(8,128)(2,1)} %pad_maximum_fusion), calls=%async_computation | async-start | bytes 4292608 | tf_op jit(solution)/shard_map/all_to_all | solution.py:287
  10.8 25.4 %all-to-all-done.q_ref.g_ref.refs_0_.refs_1_ = bf16[4,2096,128]{2,1,0:T(8,128)(2,1)S(1)} async-done(((bf16[4,2096,128]{2,1,0:T(8,128)(2,1)}), bf16[4,2096,128]{2,1,0:T(8,128)(2,1)S(1)}, u32[]{:S(2)}, u32[]{:S(2)}) %all-to-all-start) | async-done | bytes 2146336 | tf_op jit(solution)/shard_map/all_to_all | solution.py:287
  36.2 3.1 %constant_dynamic-slice_fusion = (bf16[1024,1,128]{2,1,0:T(2,128)(2,1)S(1)}, bf16[1024,1,128]{2,1,0:T(2,128)(2,1)S(1)}) fusion(bf16[1024,4,128]{2,1,0:T(4,128)(2,1)S(1)} %copy-done.14, s32[]{:T(128)S(6)} %select_n.140, bf16[1024,4,128]{2,1,0:T(4,128)(2,1)} %param.8), kind=kLoop, calls=%fused_computation.77 | loop fusion | bytes 1048580 | tf_op jit(solution)/shard_map/jit(dynamic_index_in_dim)/dynamic_slice | solution.py:273
  39.4 1.1 pad_maximum_fusion.2
  40.4 1.5 collective-permute-start.3
  41.9 1.7 collective-permute-start.4
  43.7 1.8 collective-permute-start.6
  45.5 5.5 %collective-permute-done.3 = bf16[2,1024,128]{2,1,0:T(8,128)(2,1)S(1)} collective-permute-done((bf16[2,1024,128]{2,1,0:T(8,128)(2,1)}, bf16[2,1024,128]{2,1,0:T(8,128)(2,1)S(1)}, u32[]{:S(2)}, u32[]{:S(2)}) %collective-permute-start.3) | collective-permute-done | bytes 524320 | tf_op jit(solution)/shard_map/ppermute | solution.py:44
  51.0 1.9 collective-permute-start.2
  53.0 3.4 %collective-permute-done.4 = bf16[2,1024,128]{2,1,0:T(8,128)(2,1)S(1)} collective-permute-done((bf16[2,1024,128]{2,1,0:T(8,128)(2,1)}, bf16[2,1024,128]{2,1,0:T(8,128)(2,1)S(1)}, u32[]{:S(2)}, u32[]{:S(2)}) %collective-permute-start.4) | collective-permute-done | bytes 524320 | tf_op jit(solution)/shard_map/ppermute | solution.py:44
  56.5 4.1 %collective-permute-start.9 = (bf16[2,2,1024,128]{3,2,1,0:T(8,128)(2,1)S(1)}, bf16[2,2,1024,128]{3,2,1,0:T(8,128)(2,1)}, u32[]{:S(2)}, u32[]{:S(2)}) collective-permute-start(bf16[2,2,1024,128]{3,2,1,0:T(8,128)(2,1)S(1)} %pad_maximum_fusion.1.refs_10_), channel_id=1, source_target_pairs={{0,24},{4,100},{8,0},{12,108},{16,8},{20,116},{24,16},{28,124},{32... | collective-permute-start | bytes 3145736 | tf_op jit(solution)/shard_map/ppermute | solution.py:44
  60.8 0.7 pad_add_fusion.tbl
  61.5 4.2 %collective-permute-start.8 = (bf16[1,2,1024,128]{3,2,1,0:T(8,128)(2,1)}, bf16[1,2,1024,128]{3,2,1,0:T(8,128)(2,1)}, u32[]{:S(2)}, u32[]{:S(2)}) collective-permute-start(bf16[1,2,1024,128]{3,2,1,0:T(8,128)(2,1)} %get-tuple-element.57.refs_9_), channel_id=1, source_target_pairs={{0,24},{4,100},{8,0},{12,108},{16,8},{20,116},{24,16},{28,124},{32... | collective-permute-start | bytes 1572872 | tf_op jit(solution)/shard_map/ppermute | solution.py:44
  65.8 7.1 %collective-permute-done.9.refs_10_ = bf16[2,2,1024,128]{3,2,1,0:T(8,128)(2,1)} collective-permute-done((bf16[2,2,1024,128]{3,2,1,0:T(8,128)(2,1)S(1)}, bf16[2,2,1024,128]{3,2,1,0:T(8,128)(2,1)}, u32[]{:S(2)}, u32[]{:S(2)}) %collective-permute-start.9) | collective-permute-done | bytes 1048608 | tf_op jit(solution)/shard_map/ppermute | solution.py:44
  72.9 3.8 %collective-permute-start.10 = (bf16[1,2,1024,128]{3,2,1,0:T(8,128)(2,1)}, bf16[1,2,1024,128]{3,2,1,0:T(8,128)(2,1)}, u32[]{:S(2)}, u32[]{:S(2)}) collective-permute-start(bf16[1,2,1024,128]{3,2,1,0:T(8,128)(2,1)} %bitcast.24.refs_11_), channel_id=1, source_target_pairs={{0,24},{4,100},{8,0},{12,108},{16,8},{20,116},{24,16},{28,124},{32... | collective-permute-start | bytes 1572872 | tf_op jit(solution)/shard_map/ppermute | solution.py:44
  76.8 0.6 reshape.240.st_ref.refs_4_
  77.4 0.8 slice.142
  78.2 0.4 collective-permute-done.8.refs_9_
  78.6 1.7 collective-permute-start.11
  80.3 2.1 %collective-permute-done.7.refs_8_ = bf16[1,2,1024,128]{3,2,1,0:T(8,128)(2,1)} collective-permute-done((bf16[1,2,1024,128]{3,2,1,0:T(8,128)(2,1)}, bf16[1,2,1024,128]{3,2,1,0:T(8,128)(2,1)}, u32[]{:S(2)}, u32[]{:S(2)}) %collective-permute-start.7) | collective-permute-done | bytes 524320 | tf_op jit(solution)/shard_map/ppermute | solution.py:44
  82.5 0.6 reshape.241.refs_5_
  83.1 1.1 collective-permute-done.10.refs_11_
  84.2 10.5 %remote.2 = (bf16[4,1024,128]{2,1,0:T(8,128)(2,1)}, bf16[4,1024,128]{2,1,0:T(8,128)(2,1)}, bf16[4,2,1024,128]{3,2,1,0:T(8,128)(2,1)}, bf16[4,2,1024,128]{3,2,1,0:T(8,128)(2,1)}) custom-call(s32[32]{0:T(128)} %pad_add_fusion.tbl, bf16[4,2096,128]{2,1,0:T(8,128)(2,1)} %copy-done.1, bf16[4,2096,128]{2,1,0:T(8,128)(2,1)} %copy-done.1, ...), custom_call_target="tpu_custom_call" | custom-call | flops 5368709120 | bytes 16777216 | tf_op jit(solution)/shard_map/remote/pallas_call | solution.py:226
  94.8 9.6 %collective-permute-start.15 = (bf16[4,2,1024,128]{3,2,1,0:T(8,128)(2,1)}, bf16[4,2,1024,128]{3,2,1,0:T(8,128)(2,1)}, u32[]{:S(2)}, u32[]{:S(2)}) collective-permute-start(bf16[4,2,1024,128]{3,2,1,0:T(8,128)(2,1)} %get-tuple-element.23), channel_id=1, source_target_pairs={{0,24},{4,100},{8,0},{12,108},{16,8},{20,116},{24,16},{28,124},{32... | collective-permute-start | bytes 6291464 | tf_op jit(solution)/shard_map/ppermute | solution.py:44
  104.4 0.8 copy-done.17
  105.2 12.1 %remote.3 = (bf16[4,1024,128]{2,1,0:T(8,128)(2,1)}, bf16[4,1024,128]{2,1,0:T(8,128)(2,1)}, bf16[1,2,1024,128]{3,2,1,0:T(8,128)(2,1)}, bf16[1,2,1024,128]{3,2,1,0...) custom-call(s32[32]{0:T(128)} %pad_add_fusion.tbl, ...), custom_call_target="tpu_custom_call" | custom-call | flops 5368709120 | bytes 16777216 | tf_op jit(solution)/shard_map/remote/pallas_call | solution.py:226
  117.3 23.2 %collective-permute-start.20 = (bf16[2,1024,128]{2,1,0:T(8,128)(2,1)}, bf16[2,1024,128]{2,1,0:T(8,128)(2,1)S(1)}, u32[]{:S(2)}, u32[]{:S(2)}) collective-permute-start(bf16[2,1024,128]{2,1,0:T(8,128)(2,1)} %bitcast.107), channel_id=1, source_target_pairs={{0,96},{4,28},{8,104},{12,4},{16,112},{20,12},{24,120},{28,20},{32... | collective-permute-start | bytes 1572872 | tf_op jit(solution)/shard_map/ppermute | solution.py:44
  140.4 1.5 add_convert_fusion
  142.1 5.3 %collective-permute-done.20 = bf16[2,1024,128]{2,1,0:T(8,128)(2,1)S(1)} collective-permute-done((bf16[2,1024,128]{2,1,0:T(8,128)(2,1)}, bf16[2,1024,128]{2,1,0:T(8,128)(2,1)S(1)}, u32[]{:S(2)}, u32[]{:S(2)}) %collective-permute-start.20) | collective-permute-done | bytes 524320 | tf_op jit(solution)/shard_map/ppermute | solution.py:44
  147.5 1.8 collective-permute-start.22
  149.3 15.2 %own.1 = (f32[4,1024,128]{2,1,0:T(8,128)}, f32[1024,128]{1,0:T(8,128)}, f32[1024,128]{1,0:T(8,128)}) custom-call(bf16[4,2096,128]{2,1,0:T(8,128)(2,1)} %copy-done.1, bf16[4,2096,128]{2,1,0:T(8,128)(2,1)} %copy-done.1, f32[8,2,512]{2,1,0:T(2,128)} %reshape.240.st_ref.refs_4_, bf16[1024,128]{1,0:T(8,128)(2,1)} %bitcast.102, bf16[1024,128]{1,0:T(8,128)(2,1)} %bitcast.100), custom_call_target="tpu_custom_call" | custom-call | flops 3221225472 | bytes 8388608 | tf_op jit(solution)/shard_map/own/pallas_call | solution.py:107
  164.5 2.6 %fusion.2 = bf16[2,1024,128]{2,1,0:T(8,128)(2,1)} fusion(bf16[2,1024,128]{2,1,0:T(8,128)(2,1)} %collective-permute-done.22, bf16[2,1024,128]{2,1,0:T(8,128)(2,1)} %collective-permute-done.21, bf16[2,1024,128]{2,1,0:T(8,128)(2,1)} %copy-done.13, bf16[1,2,1024,128]{3,2,1,0:T(8,128)(2,1)S(1)} %copy-done.12), kind=kLoop, calls=%fused_computation.8 | loop fusion | flops 2097152 | bytes 2621440 | tf_op jit(solution)/shard_map/convert_element_type | solution.py:346
  167.1 0.8 collective-permute-start.23
  167.9 2.8 %multiply_convert_fusion = bf16[4,1024,128]{2,1,0:T(8,128)(2,1)} fusion(f32[4,1024,128]{2,1,0:T(8,128)S(1)} %copy-done.2, bf16[4,1024,128]{2,1,0:T(8,128)(2,1)} %collective-permute-done.14, bf16[4,1024,128]{2,1,0:T(8,128)(2,1)S(1)} %copy-done.9, bf16[4,1024,128]{2,1,0:T(8,128)(2,1)S(1)} %copy-done.8), kind=kLoop, calls=%fused_computation.1 | loop fusion | flops 4194304 | bytes 6291456 | tf_op jit(solution)/shard_map/convert_element_type | solution.py:360
  170.7 4.9 %all-to-all-start.1 = ((bf16[4,1024,128]{2,1,0:T(8,128)(2,1)}), bf16[4,1024,128]{2,1,0:T(8,128)(2,1)S(1)}, u32[]{:S(2)}, u32[]{:S(2)}) async-start(bf16[4,1024,128]{2,1,0:T(8,128)(2,1)} %multiply_convert_fusion), calls=%async_computation.1 | async-start | bytes 2097152 | tf_op jit(solution)/shard_map/all_to_all | solution.py:287
  175.6 4.5 %fusion.3 = (bf16[2,1024,128]{2,1,0:T(8,128)(2,1)}, bf16[2,1024,128]{2,1,0:T(8,128)(2,1)}, bf16[2,1024,128]{2,1,0:T(8,128)(2,1)}, f32[1,2,1024,128]{3,2,1,0:T(8,128)S(1)}) fusion(bf16[4,2,1024,128]{3,2,1,0:T(8,128)(2,1)} %collective-permute-done.16, bf16[4,2,1024,128]{3,2,1,0:T(8,128)(2,1)} %collective-permute-done.15, ...), kind=kLoop, calls=%fused_computation.15 | loop fusion | flops 6029312 | bytes 8912896 | tf_op jit(solution)/shard_map/convert_element_type | solution.py:348
  180.2 2.6 %collective-permute-start.17 = (bf16[2,1024,128]{2,1,0:T(8,128)(2,1)}, bf16[2,1024,128]{2,1,0:T(8,128)(2,1)}, u32[]{:S(2)}, u32[]{:S(2)}) collective-permute-start(bf16[2,1024,128]{2,1,0:T(8,128)(2,1)} %get-tuple-element.50), channel_id=1, source_target_pairs={{0,96},{4,28},{8,104},{12,4},{16,112},{20,12},{24,120},{28,20},{32... | collective-permute-start | bytes 1572872 | tf_op jit(solution)/shard_map/ppermute | solution.py:44
  182.8 0.2 collective-permute-start.18
  183.0 2.0 collective-permute-start.19
  184.9 3.2 %all-to-all-done.1 = bf16[4,1024,128]{2,1,0:T(8,128)(2,1)S(1)} async-done(((bf16[4,1024,128]{2,1,0:T(8,128)(2,1)}), bf16[4,1024,128]{2,1,0:T(8,128)(2,1)S(1)}, u32[]{:S(2)}, u32[]{:S(2)}) %all-to-all-start.1) | async-done | bytes 1048608 | tf_op jit(solution)/shard_map/all_to_all | solution.py:287
  188.1 1.8 copy.72
  189.9 5.5 %collective-permute-done.17 = bf16[2,1024,128]{2,1,0:T(8,128)(2,1)} collective-permute-done((bf16[2,1024,128]{2,1,0:T(8,128)(2,1)}, bf16[2,1024,128]{2,1,0:T(8,128)(2,1)}, u32[]{:S(2)}, u32[]{:S(2)}) %collective-permute-start.17) | collective-permute-done | bytes 524320 | tf_op jit(solution)/shard_map/ppermute | solution.py:44
  195.5 3.7 %collective-permute-done.18 = bf16[2,1024,128]{2,1,0:T(8,128)(2,1)} collective-permute-done((bf16[2,1024,128]{2,1,0:T(8,128)(2,1)}, bf16[2,1024,128]{2,1,0:T(8,128)(2,1)}, u32[]{:S(2)}, u32[]{:S(2)}) %collective-permute-start.18) | collective-permute-done | bytes 524320 | tf_op jit(solution)/shard_map/ppermute | solution.py:44
  199.1 2.7 %fusion.14 = (bf16[1024,1,128]{2,0,1:T(8,128)(2,1)}, bf16[1024,1,128]{2,0,1:T(8,128)(2,1)}) fusion(f32[1024,128]{1,0:T(8,128)S(1)} %copy-done.11, f32[1,2,1024,128]{3,2,1,0:T(8,128)S(1)} %get-tuple-element.53, bf16[2,1024,128]{2,1,0:T(8,128)(2,1)} %collective-permute-done.23, bf16[2,1024,128]{2,1,0:T(8,128)(2,1)} %collective-permute-done.19, ...), kind=kLoop, calls=%fused_computation.29 | loop fusion | flops 2752512 | bytes 4718592 | tf_op jit(solution)/shard_map/broadcast_in_dim | solution.py:362
  (77 shorter events, 0.9 us)
Async XLA Ops:
  0.6 3.3 %copy-start = (bf16[1024,4,1,128]{3,1,2,0:T(4,128)(2,1)S(1)}, bf16[1024,4,1,128]{3,1,2,0:T(4,128)(2,1)}, u32[]{:S(2)}) copy-start(bf16[1024,4,1,128]{3,1,2,0:T(4,128)(2,1)} %param.10) | copy-start | bytes 3145732
  0.6 3.1 %copy-start.15 = (f32[4,1,1024]{2,1,0:T(1,128)S(1)}, f32[4,1,1024]{2,1,0:T(1,128)}, u32[]{:S(2)}) copy-start(f32[4,1,1024]{2,1,0:T(1,128)} %param.12) | copy-start | bytes 49156
  0.7 3.3 %copy-start.7 = (bf16[1024,4,1,128]{3,1,2,0:T(4,128)(2,1)S(1)}, bf16[1024,4,1,128]{3,1,2,0:T(4,128)(2,1)}, u32[]{:S(2)}) copy-start(bf16[1024,4,1,128]{3,1,2,0:T(4,128)(2,1)} %param.7) | copy-start | bytes 3145732
  5.7 30.5 %copy-start.14 = (bf16[1024,4,128]{2,1,0:T(4,128)(2,1)S(1)}, bf16[1024,4,128]{2,1,0:T(4,128)(2,1)}, u32[]{:S(2)}) copy-start(bf16[1024,4,128]{2,1,0:T(4,128)(2,1)} %param.9) | copy-start | bytes 3145732
  5.7 30.4 %all-to-all-start = ((bf16[4,2096,128]{2,1,0:T(8,128)(2,1)}), bf16[4,2096,128]{2,1,0:T(8,128)(2,1)S(1)}, u32[]{:S(2)}, u32[]{:S(2)}) async-start(bf16[4,2096,128]{2,1,0:T(8,128)(2,1)} %pad_maximum_fusion), calls=%async_computation | async-start | bytes 4292608 | tf_op jit(solution)/shard_map/all_to_all | solution.py:287
  36.2 25.3 %copy-start.1 = (bf16[4,2096,128]{2,1,0:T(8,128)(2,1)}, bf16[4,2096,128]{2,1,0:T(8,128)(2,1)S(1)}, u32[]{:S(2)}) copy-start(bf16[4,2096,128]{2,1,0:T(8,128)(2,1)S(1)} %all-to-all-done.q_ref.g_ref.refs_0_.refs_1_) | copy-start | bytes 6438916
  36.2 40.5 %collective-permute-start.1 = (bf16[4,2096,128]{2,1,0:T(8,128)(2,1)S(1)}, bf16[4,2096,128]{2,1,0:T(8,128)(2,1)}, u32[]{:S(2)}, u32[]{:S(2)}) collective-permute-start(bf16[4,2096,128]{2,1,0:T(8,128)(2,1)S(1)} %all-to-all-done.q_ref.g_ref.refs_0_.refs_1_), channel_id=1, source_target_pairs={{0,4},{4,0},{8,12},{12,8},{16,20},{20,16},{24,28},{28,24},{32,36},... | collective-permute-start | bytes 6438920 | tf_op jit(solution)/shard_map/ppermute | solution.py:48
  39.3 6.2 %copy-start.16 = (s32[8,3]{0,1:T(4,128)S(1)}, s32[8,3]{0,1:T(4,128)}, u32[]{:S(2)}) copy-start(s32[8,3]{0,1:T(4,128)} %param.13) | copy-start | bytes 292
  39.3 17.1 %copy-start.5 = (bf16[1024,1,128]{2,0,1:T(8,128)(2,1)}, bf16[1024,1,128]{2,0,1:T(8,128)(2,1)S(1)}, u32[]{:S(2)}) copy-start(bf16[1024,1,128]{2,0,1:T(8,128)(2,1)S(1)} %copy.104) | copy-start | bytes 786436
  39.4 17.0 %copy-start.6 = (bf16[1024,1,128]{2,0,1:T(8,128)(2,1)}, bf16[1024,1,128]{2,0,1:T(8,128)(2,1)S(1)}, u32[]{:S(2)}) copy-start(bf16[1024,1,128]{2,0,1:T(8,128)(2,1)S(1)} %copy.105) | copy-start | bytes 786436
  40.4 10.6 %collective-permute-start.3 = (bf16[2,1024,128]{2,1,0:T(8,128)(2,1)}, bf16[2,1024,128]{2,1,0:T(8,128)(2,1)S(1)}, u32[]{:S(2)}, u32[]{:S(2)}) collective-permute-start(bf16[2,1024,128]{2,1,0:T(8,128)(2,1)} %get-tuple-element.56), channel_id=1, source_target_pairs={{0,32},{4,12},{8,40},{12,20},{16,48},{20,28},{24,56},{28,4},{32,64... | collective-permute-start | bytes 1572872 | tf_op jit(solution)/shard_map/ppermute | solution.py:44
  41.9 14.4 %collective-permute-start.4 = (bf16[2,1024,128]{2,1,0:T(8,128)(2,1)}, bf16[2,1024,128]{2,1,0:T(8,128)(2,1)S(1)}, u32[]{:S(2)}, u32[]{:S(2)}) collective-permute-start(bf16[2,1024,128]{2,1,0:T(8,128)(2,1)} %get-tuple-element.56), channel_id=1, source_target_pairs={{0,96},{4,28},{8,104},{12,4},{16,112},{20,12},{24,120},{28,20},{32... | collective-permute-start | bytes 1572872 | tf_op jit(solution)/shard_map/ppermute | solution.py:44
  43.7 17.8 %collective-permute-start.6 = (bf16[2,1024,128]{2,1,0:T(8,128)(2,1)}, bf16[2,1024,128]{2,1,0:T(8,128)(2,1)}, u32[]{:S(2)}, u32[]{:S(2)}) collective-permute-start(bf16[2,1024,128]{2,1,0:T(8,128)(2,1)} %get-tuple-element.56), channel_id=1, source_target_pairs={{0,64},{4,20},{8,72},{12,28},{16,80},{20,4},{24,88},{28,12},{32,96... | collective-permute-start | bytes 1572872 | tf_op jit(solution)/shard_map/ppermute | solution.py:44
  45.5 15.1 %collective-permute-start = (s32[8,3]{0,1:T(4,128)S(1)}, s32[8,3]{0,1:T(4,128)S(1)}, u32[]{:S(2)}, u32[]{:S(2)}) collective-permute-start(s32[8,3]{0,1:T(4,128)S(1)} %copy-done.16), channel_id=1, source_target_pairs={{0,4},{4,0},{8,12},{12,8},{16,20},{20,16},{24,28},{28,24},{32,36},... | collective-permute-start | bytes 296 | tf_op jit(solution)/shard_map/ppermute | solution.py:48
  51.0 14.7 %collective-permute-start.2 = (bf16[1,2,1024,128]{3,2,1,0:T(8,128)(2,1)}, bf16[1,2,1024,128]{3,2,1,0:T(8,128)(2,1)}, u32[]{:S(2)}, u32[]{:S(2)}) collective-permute-start(bf16[1,2,1024,128]{3,2,1,0:T(8,128)(2,1)} %get-tuple-element.57.refs_9_), channel_id=1, source_target_pairs={{0,8},{4,36},{8,16},{12,44},{16,24},{20,52},{24,0},{28,60},{32,40}... | collective-permute-start | bytes 1572872 | tf_op jit(solution)/shard_map/ppermute | solution.py:44
  56.5 38.3 %copy-start.4 = (bf16[2,2,1024,128]{3,2,1,0:T(8,128)(2,1)}, bf16[2,2,1024,128]{3,2,1,0:T(8,128)(2,1)S(1)}, u32[]{:S(2)}) copy-start(bf16[2,2,1024,128]{3,2,1,0:T(8,128)(2,1)S(1)} %pad_maximum_fusion.1.refs_10_) | copy-start | bytes 3145732
  56.5 16.4 %collective-permute-start.9 = (bf16[2,2,1024,128]{3,2,1,0:T(8,128)(2,1)S(1)}, bf16[2,2,1024,128]{3,2,1,0:T(8,128)(2,1)}, u32[]{:S(2)}, u32[]{:S(2)}) collective-permute-start(bf16[2,2,1024,128]{3,2,1,0:T(8,128)(2,1)S(1)} %pad_maximum_fusion.1.refs_10_), channel_id=1, source_target_pairs={{0,24},{4,100},{8,0},{12,108},{16,8},{20,116},{24,16},{28,124},{32... | collective-permute-start | bytes 3145736 | tf_op jit(solution)/shard_map/ppermute | solution.py:44
  60.6 23.6 %collective-permute-start.5 = (bf16[2,2,1024,128]{3,2,1,0:T(8,128)(2,1)S(1)}, bf16[2,2,1024,128]{3,2,1,0:T(8,128)(2,1)}, u32[]{:S(2)}, u32[]{:S(2)}) collective-permute-start(bf16[2,2,1024,128]{3,2,1,0:T(8,128)(2,1)S(1)} %pad_maximum_fusion.1.refs_10_), channel_id=1, source_target_pairs={{0,8},{4,36},{8,16},{12,44},{16,24},{20,52},{24,0},{28,60},{32,40}... | collective-permute-start | bytes 3145736 | tf_op jit(solution)/shard_map/ppermute | solution.py:44
  61.5 17.1 %collective-permute-start.8 = (bf16[1,2,1024,128]{3,2,1,0:T(8,128)(2,1)}, bf16[1,2,1024,128]{3,2,1,0:T(8,128)(2,1)}, u32[]{:S(2)}, u32[]{:S(2)}) collective-permute-start(bf16[1,2,1024,128]{3,2,1,0:T(8,128)(2,1)} %get-tuple-element.57.refs_9_), channel_id=1, source_target_pairs={{0,24},{4,100},{8,0},{12,108},{16,8},{20,116},{24,16},{28,124},{32... | collective-permute-start | bytes 1572872 | tf_op jit(solution)/shard_map/ppermute | solution.py:44
  65.7 16.7 %collective-permute-start.7 = (bf16[1,2,1024,128]{3,2,1,0:T(8,128)(2,1)}, bf16[1,2,1024,128]{3,2,1,0:T(8,128)(2,1)}, u32[]{:S(2)}, u32[]{:S(2)}) collective-permute-start(bf16[1,2,1024,128]{3,2,1,0:T(8,128)(2,1)} %bitcast.24.refs_11_), channel_id=1, source_target_pairs={{0,8},{4,36},{8,16},{12,44},{16,24},{20,52},{24,0},{28,60},{32,40}... | collective-permute-start | bytes 1572872 | tf_op jit(solution)/shard_map/ppermute | solution.py:44
  72.9 11.3 %collective-permute-start.10 = (bf16[1,2,1024,128]{3,2,1,0:T(8,128)(2,1)}, bf16[1,2,1024,128]{3,2,1,0:T(8,128)(2,1)}, u32[]{:S(2)}, u32[]{:S(2)}) collective-permute-start(bf16[1,2,1024,128]{3,2,1,0:T(8,128)(2,1)} %bitcast.24.refs_11_), channel_id=1, source_target_pairs={{0,24},{4,100},{8,0},{12,108},{16,8},{20,116},{24,16},{28,124},{32... | collective-permute-start | bytes 1572872 | tf_op jit(solution)/shard_map/ppermute | solution.py:44
  76.7 27.7 %collective-permute-start.12 = (bf16[2,2,1024,128]{3,2,1,0:T(8,128)(2,1)}, bf16[2,2,1024,128]{3,2,1,0:T(8,128)(2,1)}, u32[]{:S(2)}, u32[]{:S(2)}) collective-permute-start(bf16[2,2,1024,128]{3,2,1,0:T(8,128)(2,1)} %collective-permute-done.9.refs_10_), channel_id=1, source_target_pairs={{0,24},{4,100},{8,0},{12,108},{16,8},{20,116},{24,16},{28,124},{32... | collective-permute-start | bytes 3145736 | tf_op jit(solution)/shard_map/ppermute | solution.py:44
  78.6 25.8 %collective-permute-start.11 = (bf16[1,2,1024,128]{3,2,1,0:T(8,128)(2,1)}, bf16[1,2,1024,128]{3,2,1,0:T(8,128)(2,1)S(1)}, u32[]{:S(2)}, u32[]{:S(2)}) collective-permute-start(bf16[1,2,1024,128]{3,2,1,0:T(8,128)(2,1)} %collective-permute-done.2.refs_6_), channel_id=1, source_target_pairs={{0,8},{4,36},{8,16},{12,44},{16,24},{20,52},{24,0},{28,60},{32,40}... | collective-permute-start | bytes 1572872 | tf_op jit(solution)/shard_map/ppermute | solution.py:44
  82.4 22.0 %collective-permute-start.13 = (bf16[1,2,1024,128]{3,2,1,0:T(8,128)(2,1)}, bf16[1,2,1024,128]{3,2,1,0:T(8,128)(2,1)}, u32[]{:S(2)}, u32[]{:S(2)}) collective-permute-start(bf16[1,2,1024,128]{3,2,1,0:T(8,128)(2,1)} %collective-permute-done.7.refs_8_), channel_id=1, source_target_pairs={{0,8},{4,36},{8,16},{12,44},{16,24},{20,52},{24,0},{28,60},{32,40}... | collective-permute-start | bytes 1572872 | tf_op jit(solution)/shard_map/ppermute | solution.py:44
  94.8 80.9 %collective-permute-start.15 = (bf16[4,2,1024,128]{3,2,1,0:T(8,128)(2,1)}, bf16[4,2,1024,128]{3,2,1,0:T(8,128)(2,1)}, u32[]{:S(2)}, u32[]{:S(2)}) collective-permute-start(bf16[4,2,1024,128]{3,2,1,0:T(8,128)(2,1)} %get-tuple-element.23), channel_id=1, source_target_pairs={{0,24},{4,100},{8,0},{12,108},{16,8},{20,116},{24,16},{28,124},{32... | collective-permute-start | bytes 6291464 | tf_op jit(solution)/shard_map/ppermute | solution.py:44
  104.4 36.0 %copy-start.3 = (bf16[4,1024,128]{2,1,0:T(8,128)(2,1)S(1)}, bf16[4,1024,128]{2,1,0:T(8,128)(2,1)}, u32[]{:S(2)}) copy-start(bf16[4,1024,128]{2,1,0:T(8,128)(2,1)} %get-tuple-element.20) | copy-start | bytes 3145732
  104.4 71.2 %collective-permute-start.16 = (bf16[4,2,1024,128]{3,2,1,0:T(8,128)(2,1)}, bf16[4,2,1024,128]{3,2,1,0:T(8,128)(2,1)}, u32[]{:S(2)}, u32[]{:S(2)}) collective-permute-start(bf16[4,2,1024,128]{3,2,1,0:T(8,128)(2,1)} %get-tuple-element.24), channel_id=1, source_target_pairs={{0,8},{4,36},{8,16},{12,44},{16,24},{20,52},{24,0},{28,60},{32,40}... | collective-permute-start | bytes 6291464 | tf_op jit(solution)/shard_map/ppermute | solution.py:44
  104.4 0.8 copy-start.17
  117.3 30.2 %collective-permute-start.20 = (bf16[2,1024,128]{2,1,0:T(8,128)(2,1)}, bf16[2,1024,128]{2,1,0:T(8,128)(2,1)S(1)}, u32[]{:S(2)}, u32[]{:S(2)}) collective-permute-start(bf16[2,1024,128]{2,1,0:T(8,128)(2,1)} %bitcast.107), channel_id=1, source_target_pairs={{0,96},{4,28},{8,104},{12,4},{16,112},{20,12},{24,120},{28,20},{32... | collective-permute-start | bytes 1572872 | tf_op jit(solution)/shard_map/ppermute | solution.py:44
  141.9 25.9 %collective-permute-start.14 = (bf16[4,1024,128]{2,1,0:T(8,128)(2,1)S(1)}, bf16[4,1024,128]{2,1,0:T(8,128)(2,1)}, u32[]{:S(2)}, u32[]{:S(2)}) collective-permute-start(bf16[4,1024,128]{2,1,0:T(8,128)(2,1)S(1)} %add_convert_fusion), channel_id=1, source_target_pairs={{0,4},{4,0},{8,12},{12,8},{16,20},{20,16},{24,28},{28,24},{32,36},... | collective-permute-start | bytes 3145736 | tf_op jit(solution)/shard_map/ppermute | solution.py:48
  142.0 22.5 %collective-permute-start.21 = (bf16[2,1024,128]{2,1,0:T(8,128)(2,1)}, bf16[2,1024,128]{2,1,0:T(8,128)(2,1)}, u32[]{:S(2)}, u32[]{:S(2)}) collective-permute-start(bf16[2,1024,128]{2,1,0:T(8,128)(2,1)} %bitcast.33), channel_id=1, source_target_pairs={{0,32},{4,12},{8,40},{12,20},{16,48},{20,28},{24,56},{28,4},{32,64... | collective-permute-start | bytes 1572872 | tf_op jit(solution)/shard_map/ppermute | solution.py:44
  147.5 1.8 copy-start.13
  147.5 17.0 %collective-permute-start.22 = (bf16[2,1024,128]{2,1,0:T(8,128)(2,1)}, bf16[2,1024,128]{2,1,0:T(8,128)(2,1)}, u32[]{:S(2)}, u32[]{:S(2)}) collective-permute-start(bf16[2,1024,128]{2,1,0:T(8,128)(2,1)} %bitcast.34), channel_id=1, source_target_pairs={{0,64},{4,20},{8,72},{12,28},{16,80},{20,4},{24,88},{28,12},{32,96... | collective-permute-start | bytes 1572872 | tf_op jit(solution)/shard_map/ppermute | solution.py:44
  149.3 15.2 %copy-start.12 = (bf16[1,2,1024,128]{3,2,1,0:T(8,128)(2,1)S(1)}, bf16[1,2,1024,128]{3,2,1,0:T(8,128)(2,1)}, u32[]{:S(2)}) copy-start(bf16[1,2,1024,128]{3,2,1,0:T(8,128)(2,1)} %get-tuple-element.25) | copy-start | bytes 1572868
  149.3 18.6 %copy-start.8 = (bf16[4,1024,128]{2,1,0:T(8,128)(2,1)S(1)}, bf16[4,1024,128]{2,1,0:T(8,128)(2,1)}, u32[]{:S(2)}) copy-start(bf16[4,1024,128]{2,1,0:T(8,128)(2,1)} %get-tuple-element.18) | copy-start | bytes 3145732
  149.3 18.6 %copy-start.9 = (bf16[4,1024,128]{2,1,0:T(8,128)(2,1)S(1)}, bf16[4,1024,128]{2,1,0:T(8,128)(2,1)}, u32[]{:S(2)}) copy-start(bf16[4,1024,128]{2,1,0:T(8,128)(2,1)} %get-tuple-element.19) | copy-start | bytes 3145732
  164.5 3.4 %copy-start.2 = (f32[4,1024,128]{2,1,0:T(8,128)S(1)}, f32[4,1024,128]{2,1,0:T(8,128)}, u32[]{:S(2)}) copy-start(f32[4,1024,128]{2,1,0:T(8,128)} %get-tuple-element.17) | copy-start | bytes 6291460
  167.1 22.8 %collective-permute-start.23 = (bf16[2,1024,128]{2,1,0:T(8,128)(2,1)}, bf16[2,1024,128]{2,1,0:T(8,128)(2,1)}, u32[]{:S(2)}, u32[]{:S(2)}) collective-permute-start(bf16[2,1024,128]{2,1,0:T(8,128)(2,1)} %fusion.2), channel_id=1, source_target_pairs={{0,16},{4,68},{8,24},{12,76},{16,0},{20,84},{24,8},{28,92},{32,48}... | collective-permute-start | bytes 1572872 | tf_op jit(solution)/shard_map/ppermute | solution.py:44
  170.7 17.5 %all-to-all-start.1 = ((bf16[4,1024,128]{2,1,0:T(8,128)(2,1)}), bf16[4,1024,128]{2,1,0:T(8,128)(2,1)S(1)}, u32[]{:S(2)}, u32[]{:S(2)}) async-start(bf16[4,1024,128]{2,1,0:T(8,128)(2,1)} %multiply_convert_fusion), calls=%async_computation.1 | async-start | bytes 2097152 | tf_op jit(solution)/shard_map/all_to_all | solution.py:287
  180.2 19.0 %copy-start.10 = (f32[1024,128]{1,0:T(8,128)S(1)}, f32[1024,128]{1,0:T(8,128)}, u32[]{:S(2)}) copy-start(f32[1024,128]{1,0:T(8,128)} %get-tuple-element.29) | copy-start | bytes 1572868
  180.2 19.0 %copy-start.11 = (f32[1024,128]{1,0:T(8,128)S(1)}, f32[1024,128]{1,0:T(8,128)}, u32[]{:S(2)}) copy-start(f32[1024,128]{1,0:T(8,128)} %get-tuple-element.30) | copy-start | bytes 1572868
  180.2 15.3 %collective-permute-start.17 = (bf16[2,1024,128]{2,1,0:T(8,128)(2,1)}, bf16[2,1024,128]{2,1,0:T(8,128)(2,1)}, u32[]{:S(2)}, u32[]{:S(2)}) collective-permute-start(bf16[2,1024,128]{2,1,0:T(8,128)(2,1)} %get-tuple-element.50), channel_id=1, source_target_pairs={{0,96},{4,28},{8,104},{12,4},{16,112},{20,12},{24,120},{28,20},{32... | collective-permute-start | bytes 1572872 | tf_op jit(solution)/shard_map/ppermute | solution.py:44
  182.8 16.3 %collective-permute-start.18 = (bf16[2,1024,128]{2,1,0:T(8,128)(2,1)}, bf16[2,1024,128]{2,1,0:T(8,128)(2,1)}, u32[]{:S(2)}, u32[]{:S(2)}) collective-permute-start(bf16[2,1024,128]{2,1,0:T(8,128)(2,1)} %get-tuple-element.52), channel_id=1, source_target_pairs={{0,32},{4,12},{8,40},{12,20},{16,48},{20,28},{24,56},{28,4},{32,64... | collective-permute-start | bytes 1572872 | tf_op jit(solution)/shard_map/ppermute | solution.py:44
  183.0 16.2 %collective-permute-start.19 = (bf16[2,1024,128]{2,1,0:T(8,128)(2,1)}, bf16[2,1024,128]{2,1,0:T(8,128)(2,1)}, u32[]{:S(2)}, u32[]{:S(2)}) collective-permute-start(bf16[2,1024,128]{2,1,0:T(8,128)(2,1)} %get-tuple-element.51), channel_id=1, source_target_pairs={{0,64},{4,20},{8,72},{12,28},{16,80},{20,4},{24,88},{28,12},{32,96... | collective-permute-start | bytes 1572872 | tf_op jit(solution)/shard_map/ppermute | solution.py:44

commit v6 on v5

--- a/solution.py
+++ b/solution.py
@@ -11,7 +11,7 @@
 
 QB = 128
 SIDE = 4
-OWN_TILE = 512
+OWN_TILE = 256
 VMEM_LIMIT = 60 * 1024 * 1024
 LOG2E = math.log2(math.e)
 
@@ -118,12 +118,14 @@
     )(packed, packed, stats, keys, values)
 
 
-def remote_kernel(scale2, bases, offsets, out_offsets, tbl, *refs):
+def remote_kernel(scale2, bases, offsets, out_offsets, fresh, tbl, *refs):
     sources = len(offsets) - 1
     q0, g0, q1, g1, st0, st1 = refs[:6]
     blocks = refs[6 : 6 + sources]
-    out0, out1 = refs[6 + sources : 8 + sources]
-    outs = refs[8 + sources : -4]
+    rest = refs[6 + sources : -4]
+    if not fresh:
+        in0, in1, rest = rest[0], rest[1], rest[2:]
+    out0, out1, outs = rest[0], rest[1], rest[2:]
     buf, q_buf, g_buf, dq = refs[-4:]
     at = pl.program_id(0)
     heads = q0.shape[0]
@@ -131,7 +133,11 @@
 
     @pl.when(at == 0)
     def _():
-        dq[...] = jnp.zeros_like(dq)
+        if fresh:
+            dq[...] = jnp.zeros_like(dq)
+        else:
+            dq[0] = in0[...].astype(jnp.float32)
+            dq[1] = in1[...].astype(jnp.float32)
 
     for i, block_ref in enumerate(blocks):
 
@@ -200,7 +206,7 @@
         out1[...] = dq[1].astype(out1.dtype)
 
 
-def remote_grads(table, own, sib, stats, groups, bases, out_sizes, scale2):
+def remote_grads(table, own, sib, stats, groups, bases, out_sizes, carried, scale2):
     heads, _, width = own.shape
     rows = stats[0].shape[0] * QB
     count = len(bases)
@@ -224,12 +230,13 @@
         out_offsets.append(out_offsets[-1] + size)
     acc = jax.ShapeDtypeStruct((heads, rows, width), jnp.bfloat16)
     return pl.pallas_call(
-        functools.partial(remote_kernel, scale2, bases, offsets, out_offsets),
+        functools.partial(remote_kernel, scale2, bases, offsets, out_offsets, not carried),
         grid_spec=pltpu.PrefetchScalarGridSpec(
             num_scalar_prefetch=1,
             grid=(SIDE * count,),
             in_specs=[q_spec, g_spec, q_spec, g_spec, stat, stat]
-            + [piece(start, array.shape[0]) for start, array in zip(offsets, operands)],
+            + [piece(start, array.shape[0]) for start, array in zip(offsets, operands)]
+            + [q_spec] * len(carried),
             out_specs=[acc_spec, acc_spec]
             + [piece(start, size) for start, size in zip(out_offsets, out_sizes)],
             scratch_shapes=[
@@ -248,7 +255,7 @@
             transcendentals=0,
         ),
         name="remote",
-    )(table, own, own, sib, sib, *stats, *operands)
+    )(table, own, own, sib, sib, *stats, *operands, *carried)
 
 
 def split3(value):
@@ -318,11 +325,13 @@
         hit = ((picks[:, 1:2] == source) | (picks[:, 2:3] == source)) & (source != device)
         return jnp.max(jnp.where(hit, jnp.arange(blocks, dtype=jnp.int32)[:, None], -1), axis=0)
 
-    table = jnp.concatenate([listed(selections, me), listed(sib_selections, me + 1 - 2 * core)])
-
-    def remote(groups, bases, out_sizes):
+    table = jnp.concatenate(
+        [listed(selections, me), listed(sib_selections, me + 1 - 2 * core)]
+    )
+
+    def remote(groups, bases, out_sizes, carried=()):
         return remote_grads(
-            table, own, sib, (own_stats, sib_stats), groups, bases, out_sizes, scale2
+            table, own, sib, (own_stats, sib_stats), groups, bases, out_sizes, carried, scale2
         )
 
     first0, first1, part_behind, part_ahead = remote(
@@ -331,7 +340,7 @@
     back_behind = shift(part_behind, 1, -1)
     back_ahead = shift(part_ahead, 1, 1)
     second0, second1, *part_across, part_line = remote(
-        [line_across, line], (2 * SIDE, 0), (1,) * SIDE + (SIDE,)
+        [line_across, line], (2 * SIDE, 0), (1,) * SIDE + (SIDE,), (first0, first1)
     )
     part_across = [part[0] for part in part_across]
     own_q, own_k, own_v = own_grads(own, own_stats, keys, values, scale2)
@@ -345,7 +354,8 @@
     side = spread(part_across[1:])
     far_sum = summed(part_across[0], *side).astype(jnp.bfloat16)
     total = [summed(part_line[i], back_behind[i], back_ahead[i]) for i in range(SIDE)]
-    received = spread([part.astype(jnp.bfloat16) for part in total[1:]])
+    low = [part.astype(jnp.bfloat16) for part in total[1:]]
+    received = spread(low)
     received += (shift(far_sum, 1, 2),)
 
     def final(i, own_part, factor):
@@ -355,9 +365,8 @@
 
     grad_k, grad_v = final(0, own_k, scale), final(1, own_v, 1.0)
 
-    dq_low = summed(first1, second1).astype(jnp.bfloat16)
-    returned = other_core(dq_low)
-    dq = ((own_q + summed(first0, second0, returned)) * scale).astype(jnp.bfloat16)
+    returned = other_core(second1)
+    dq = ((own_q + summed(second0, returned)) * scale).astype(jnp.bfloat16)
     dq = jnp.transpose(turn(dq), (1, 0, 2))[:, :, None]
     return dq, grad_k[:, None], grad_v[:, None]
 

time: 202 us -> 205 us (1.015)
  waiting for transfers between devices: 62.9 us -> 75.9 us
  starting transfers between devices: 71.2 us -> 63.7 us
  other arithmetic: 20.5 us -> 18 us
    ppermute x21, waiting for transfers between devices: 34.3 us -> 47.5 us  [shift(): return lax.ppermute(value, 'ctx', pairs(place))]
    ppermute x21, starting transfers between devices: 61.1 us -> 53.7 us  [shift(): return lax.ppermute(value, 'ctx', pairs(place))]
    convert_element_type x3 -> x2, other arithmetic: 8.81 us -> 5.96 us  [the longest x1 4.53 us: grads(): low = [part.astype(jnp.bfloat16) for part in total[1:]]]
  transfers between devices with their start and end apart: 26 -> 26, of which waited for: 11 -> 11; matrix products, arithmetic and copies ran while one was open for 10% -> 8% of each run, Pallas kernels for 19% -> 18%
where the time goes in v6:
time: 205 us; the launch traced here: 204 us
  waiting for transfers between devices  75.9 us (37%)
  starting transfers between devices  63.7 us (31%)
  Pallas kernels  36.8 us (18%)
  other arithmetic  18 us (9%)
  local copies, waits for them, and re-layouts  8.75 us (4%)
    ppermute x21, starting transfers between devices, shift(): return lax.ppermute(value, 'ctx', pairs(place))  53.7 us
    ppermute x21, waiting for transfers between devices, shift(): return lax.ppermute(value, 'ctx', pairs(place))  47.5 us
    all_to_all x2, waiting for transfers between devices, turn(): lax.all_to_all(value, 'head', split_axis=0, concat_axis=0, tiled=True)  28.5 us
    pallas_call x2, Pallas kernels, remote_grads(): pl.pallas_call(functools.partial(remote_kernel, scale2, bases, offsets, o...  23.1 us
    pallas_call x1, Pallas kernels, own_grads(): pl.pallas_call(functools.partial(own_kernel, scale2), grid=(blocks,), in_...  13.7 us
    all_to_all x2, starting transfers between devices, turn(): lax.all_to_all(value, 'head', split_axis=0, concat_axis=0, tiled=True)  9.98 us
    convert_element_type x1, other arithmetic, grads(): low = [part.astype(jnp.bfloat16) for part in total[1:]]  4.53 us
  transfers between devices with their start and end apart: 26, of which 11 were waited for; matrix products, arithmetic and copies ran while one was open for 8% of the time, Pallas kernels for 18%

profile of v6, /device:TPU:8, one launch (start us, length us, event | category | flops | bytes accessed | tf_op | source)
XLA Modules:
  0.0 204.1 jit_solution(16467672057305452372)
XLA Ops:
  0.7 0.9 fusion.19
  1.5 2.7 %multiply_reduce_fusion = f32[1024,4]{1,0:T(8,128)S(1)} fusion(bf16[1024,4,1,128]{3,1,2,0:T(4,128)(2,1)} %param.11, bf16[1024,4,1,128]{3,1,2,0:T(4,128)(2,1)} %param.10), kind=kLoop, calls=%fused_computation.2 | loop fusion | flops 2093056 | bytes 2113536 | tf_op jit(solution)/shard_map/reduce_sum | solution.py:296
  4.3 0.2 copy.62
  4.6 0.3 copy_bitcast_fusion
  4.9 1.5 pad_maximum_fusion
  6.4 5.0 %all-to-all-start = ((bf16[4,2096,128]{2,1,0:T(8,128)(2,1)}), bf16[4,2096,128]{2,1,0:T(8,128)(2,1)S(1)}, u32[]{:S(2)}, u32[]{:S(2)}) async-start(bf16[4,2096,128]{2,1,0:T(8,128)(2,1)} %pad_maximum_fusion), calls=%async_computation | async-start | bytes 4292608 | tf_op jit(solution)/shard_map/all_to_all | solution.py:294
  11.5 25.4 %all-to-all-done.q_ref.g_ref.refs_0_.refs_1_ = bf16[4,2096,128]{2,1,0:T(8,128)(2,1)S(1)} async-done(((bf16[4,2096,128]{2,1,0:T(8,128)(2,1)}), bf16[4,2096,128]{2,1,0:T(8,128)(2,1)S(1)}, u32[]{:S(2)}, u32[]{:S(2)}) %all-to-all-start) | async-done | bytes 2146336 | tf_op jit(solution)/shard_map/all_to_all | solution.py:294
  36.9 3.1 %constant_dynamic-slice_fusion = (bf16[1024,1,128]{2,1,0:T(2,128)(2,1)S(1)}, bf16[1024,1,128]{2,1,0:T(2,128)(2,1)S(1)}) fusion(bf16[1024,4,128]{2,1,0:T(4,128)(2,1)S(1)} %copy-done.11, s32[]{:T(128)S(6)} %select_n.140, bf16[1024,4,128]{2,1,0:T(4,128)(2,1)} %param.8), kind=kLoop, calls=%fused_computation.76 | loop fusion | bytes 1048580 | tf_op jit(solution)/shard_map/jit(dynamic_index_in_dim)/dynamic_slice | solution.py:280
  40.1 1.1 pad_maximum_fusion.2
  41.2 2.8 %collective-permute-start.5 = (bf16[2,1024,128]{2,1,0:T(8,128)(2,1)}, bf16[2,1024,128]{2,1,0:T(8,128)(2,1)S(1)}, u32[]{:S(2)}, u32[]{:S(2)}) collective-permute-start(bf16[2,1024,128]{2,1,0:T(8,128)(2,1)} %get-tuple-element.56), channel_id=1, source_target_pairs={{0,96},{4,28},{8,104},{12,4},{16,112},{20,12},{24,120},{28,20},{32... | collective-permute-start | bytes 1572872 | tf_op jit(solution)/shard_map/ppermute | solution.py:44
  43.9 2.3 %collective-permute-start.8 = (bf16[2,1024,128]{2,1,0:T(8,128)(2,1)}, bf16[2,1024,128]{2,1,0:T(8,128)(2,1)}, u32[]{:S(2)}, u32[]{:S(2)}) collective-permute-start(bf16[2,1024,128]{2,1,0:T(8,128)(2,1)} %get-tuple-element.56), channel_id=1, source_target_pairs={{0,64},{4,20},{8,72},{12,28},{16,80},{20,4},{24,88},{28,12},{32,96... | collective-permute-start | bytes 1572872 | tf_op jit(solution)/shard_map/ppermute | solution.py:44
  46.2 10.4 %collective-permute-done.5 = bf16[2,1024,128]{2,1,0:T(8,128)(2,1)S(1)} collective-permute-done((bf16[2,1024,128]{2,1,0:T(8,128)(2,1)}, bf16[2,1024,128]{2,1,0:T(8,128)(2,1)S(1)}, u32[]{:S(2)}, u32[]{:S(2)}) %collective-permute-start.5) | collective-permute-done | bytes 524320 | tf_op jit(solution)/shard_map/ppermute | solution.py:44
  56.6 4.0 %collective-permute-start.12 = (bf16[1,2,1024,128]{3,2,1,0:T(8,128)(2,1)}, bf16[1,2,1024,128]{3,2,1,0:T(8,128)(2,1)}, u32[]{:S(2)}, u32[]{:S(2)}) collective-permute-start(bf16[1,2,1024,128]{3,2,1,0:T(8,128)(2,1)} %get-tuple-element.57.refs_9_), channel_id=1, source_target_pairs={{0,24},{4,100},{8,0},{12,108},{16,8},{20,116},{24,16},{28,124},{32... | collective-permute-start | bytes 1572872 | tf_op jit(solution)/shard_map/ppermute | solution.py:44
  60.6 0.1 pad_maximum_fusion.1.refs_10_
  60.7 3.6 %collective-permute-start.6 = (bf16[2,2,1024,128]{3,2,1,0:T(8,128)(2,1)S(1)}, bf16[2,2,1024,128]{3,2,1,0:T(8,128)(2,1)}, u32[]{:S(2)}, u32[]{:S(2)}) collective-permute-start(bf16[2,2,1024,128]{3,2,1,0:T(8,128)(2,1)S(1)} %pad_maximum_fusion.1.refs_10_), channel_id=1, source_target_pairs={{0,24},{4,100},{8,0},{12,108},{16,8},{20,116},{24,16},{28,124},{32... | collective-permute-start | bytes 3145736 | tf_op jit(solution)/shard_map/ppermute | solution.py:44
  64.4 0.1 collective-permute-start.11
  64.5 0.1 select_reduce_fusion.1
  64.6 0.6 pad_add_fusion.tbl
  65.3 2.3 %collective-permute-done.12.refs_9_ = bf16[1,2,1024,128]{3,2,1,0:T(8,128)(2,1)} collective-permute-done((bf16[1,2,1024,128]{3,2,1,0:T(8,128)(2,1)}, bf16[1,2,1024,128]{3,2,1,0:T(8,128)(2,1)}, u32[]{:S(2)}, u32[]{:S(2)}) %collective-permute-start.12) | collective-permute-done | bytes 524320 | tf_op jit(solution)/shard_map/ppermute | solution.py:44
  67.7 11.1 %collective-permute-done.6.refs_10_ = bf16[2,2,1024,128]{3,2,1,0:T(8,128)(2,1)} collective-permute-done((bf16[2,2,1024,128]{3,2,1,0:T(8,128)(2,1)S(1)}, bf16[2,2,1024,128]{3,2,1,0:T(8,128)(2,1)}, u32[]{:S(2)}, u32[]{:S(2)}) %collective-permute-start.6) | collective-permute-done | bytes 1048608 | tf_op jit(solution)/shard_map/ppermute | solution.py:44
  78.8 3.8 %collective-permute-start.13 = (bf16[1,2,1024,128]{3,2,1,0:T(8,128)(2,1)}, bf16[1,2,1024,128]{3,2,1,0:T(8,128)(2,1)}, u32[]{:S(2)}, u32[]{:S(2)}) collective-permute-start(bf16[1,2,1024,128]{3,2,1,0:T(8,128)(2,1)} %bitcast.24.refs_11_), channel_id=1, source_target_pairs={{0,24},{4,100},{8,0},{12,108},{16,8},{20,116},{24,16},{28,124},{32... | collective-permute-start | bytes 1572872 | tf_op jit(solution)/shard_map/ppermute | solution.py:44
  82.6 0.6 reshape.240.st_ref.refs_4_
  83.3 0.8 slice.142
  84.1 2.2 %collective-permute-done.2.refs_6_ = bf16[1,2,1024,128]{3,2,1,0:T(8,128)(2,1)} collective-permute-done((bf16[1,2,1024,128]{3,2,1,0:T(8,128)(2,1)}, bf16[1,2,1024,128]{3,2,1,0:T(8,128)(2,1)}, u32[]{:S(2)}, u32[]{:S(2)}) %collective-permute-start.2) | collective-permute-done | bytes 524320 | tf_op jit(solution)/shard_map/ppermute | solution.py:44
  86.2 5.6 %collective-permute-done.9.refs_8_ = bf16[1,2,1024,128]{3,2,1,0:T(8,128)(2,1)} collective-permute-done((bf16[1,2,1024,128]{3,2,1,0:T(8,128)(2,1)}, bf16[1,2,1024,128]{3,2,1,0:T(8,128)(2,1)}, u32[]{:S(2)}, u32[]{:S(2)}) %collective-permute-start.9) | collective-permute-done | bytes 524320 | tf_op jit(solution)/shard_map/ppermute | solution.py:44
  91.9 0.6 reshape.241.refs_5_
  92.5 10.4 %remote.2 = (bf16[4,1024,128]{2,1,0:T(8,128)(2,1)}, bf16[4,1024,128]{2,1,0:T(8,128)(2,1)}, bf16[4,2,1024,128]{3,2,1,0:T(8,128)(2,1)}, bf16[4,2,1024,128]{3,2,1,0:T(8,128)(2,1)}) custom-call(s32[32]{0:T(128)} %pad_add_fusion.tbl, bf16[4,2096,128]{2,1,0:T(8,128)(2,1)} %copy-done.1, bf16[4,2096,128]{2,1,0:T(8,128)(2,1)} %copy-done.1, ...), custom_call_target="tpu_custom_call" | custom-call | flops 5368709120 | bytes 16777216 | tf_op jit(solution)/shard_map/remote/pallas_call | solution.py:232
  102.9 9.2 %collective-permute-start.15 = (bf16[4,2,1024,128]{3,2,1,0:T(8,128)(2,1)}, bf16[4,2,1024,128]{3,2,1,0:T(8,128)(2,1)}, u32[]{:S(2)}, u32[]{:S(2)}) collective-permute-start(bf16[4,2,1024,128]{3,2,1,0:T(8,128)(2,1)} %get-tuple-element.23), channel_id=1, source_target_pairs={{0,24},{4,100},{8,0},{12,108},{16,8},{20,116},{24,16},{28,124},{32... | collective-permute-start | bytes 6291464 | tf_op jit(solution)/shard_map/ppermute | solution.py:44
  112.2 0.8 copy-done.14
  112.9 0.3 copy-done.13
  113.3 12.6 %remote.3 = (bf16[4,1024,128]{2,1,0:T(8,128)(2,1)}, bf16[4,1024,128]{2,1,0:T(8,128)(2,1)}, bf16[1,2,1024,128]{3,2,1,0:T(8,128)(2,1)}, bf16[1,2,1024,128]{3,2,1,0...) custom-call(s32[32]{0:T(128)} %pad_add_fusion.tbl, ...), custom_call_target="tpu_custom_call" | custom-call | flops 5368709120 | bytes 16777216 | tf_op jit(solution)/shard_map/remote/pallas_call | solution.py:232
  125.9 20.5 %collective-permute-start.20 = (bf16[2,1024,128]{2,1,0:T(8,128)(2,1)}, bf16[2,1024,128]{2,1,0:T(8,128)(2,1)S(1)}, u32[]{:S(2)}, u32[]{:S(2)}) collective-permute-start(bf16[2,1024,128]{2,1,0:T(8,128)(2,1)} %bitcast.109), channel_id=1, source_target_pairs={{0,96},{4,28},{8,104},{12,4},{16,112},{20,12},{24,120},{28,20},{32... | collective-permute-start | bytes 1572872 | tf_op jit(solution)/shard_map/ppermute | solution.py:44
  146.4 7.0 %collective-permute-done.20 = bf16[2,1024,128]{2,1,0:T(8,128)(2,1)S(1)} collective-permute-done((bf16[2,1024,128]{2,1,0:T(8,128)(2,1)}, bf16[2,1024,128]{2,1,0:T(8,128)(2,1)S(1)}, u32[]{:S(2)}, u32[]{:S(2)}) %collective-permute-start.20) | collective-permute-done | bytes 524320 | tf_op jit(solution)/shard_map/ppermute | solution.py:44
  153.4 1.8 collective-permute-start.22
  155.3 13.7 %own.1 = (f32[4,1024,128]{2,1,0:T(8,128)}, f32[1024,128]{1,0:T(8,128)}, f32[1024,128]{1,0:T(8,128)}) custom-call(bf16[4,2096,128]{2,1,0:T(8,128)(2,1)} %copy-done.1, bf16[4,2096,128]{2,1,0:T(8,128)(2,1)} %copy-done.1, f32[8,2,512]{2,1,0:T(2,128)} %reshape.240.st_ref.refs_4_, bf16[1024,128]{1,0:T(8,128)(2,1)} %bitcast.102, bf16[1024,128]{1,0:T(8,128)(2,1)} %bitcast.100), custom_call_target="tpu_custom_call" | custom-call | flops 3221225472 | bytes 8388608 | tf_op jit(solution)/shard_map/own/pallas_call | solution.py:107
  169.0 2.3 %fusion.2 = bf16[2,1024,128]{2,1,0:T(8,128)(2,1)} fusion(bf16[2,1024,128]{2,1,0:T(8,128)(2,1)} %collective-permute-done.22, bf16[2,1024,128]{2,1,0:T(8,128)(2,1)S(1)} %collective-permute-done.21, bf16[2,1024,128]{2,1,0:T(8,128)(2,1)S(1)} %collective-permute-done.20, bf16[1,2,1024,128]{3,2,1,0:T(8,128)(2,1)S(1)} %copy-done.10), kind=kLoop, calls=%fused_computation.7 | loop fusion | flops 2097152 | bytes 2621440 | tf_op jit(solution)/shard_map/convert_element_type | solution.py:355
  171.2 0.8 collective-permute-start.23
  172.0 1.4 multiply_convert_fusion
  173.5 4.9 %all-to-all-start.1 = ((bf16[4,1024,128]{2,1,0:T(8,128)(2,1)}), bf16[4,1024,128]{2,1,0:T(8,128)(2,1)S(1)}, u32[]{:S(2)}, u32[]{:S(2)}) async-start(bf16[4,1024,128]{2,1,0:T(8,128)(2,1)} %multiply_convert_fusion), calls=%async_computation.1 | async-start | bytes 2097152 | tf_op jit(solution)/shard_map/all_to_all | solution.py:294
  178.4 4.5 %fusion.3 = (bf16[2,1024,128]{2,1,0:T(8,128)(2,1)}, bf16[2,1024,128]{2,1,0:T(8,128)(2,1)}, bf16[2,1024,128]{2,1,0:T(8,128)(2,1)}, f32[1,2,1024,128]{3,2,1,0:T(8,128)S(1)}) fusion(bf16[4,2,1024,128]{3,2,1,0:T(8,128)(2,1)} %collective-permute-done.16, bf16[4,2,1024,128]{3,2,1,0:T(8,128)(2,1)} %collective-permute-done.15, ...), kind=kLoop, calls=%fused_computation.14 | loop fusion | flops 6029312 | bytes 8912896 | tf_op jit(solution)/shard_map/convert_element_type | solution.py:357
  182.9 1.9 collective-permute-start.17
  184.8 2.9 %collective-permute-start.19 = (bf16[2,1024,128]{2,1,0:T(8,128)(2,1)}, bf16[2,1024,128]{2,1,0:T(8,128)(2,1)}, u32[]{:S(2)}, u32[]{:S(2)}) collective-permute-start(bf16[2,1024,128]{2,1,0:T(8,128)(2,1)} %get-tuple-element.51), channel_id=1, source_target_pairs={{0,64},{4,20},{8,72},{12,28},{16,80},{20,4},{24,88},{28,12},{32,96... | collective-permute-start | bytes 1572872 | tf_op jit(solution)/shard_map/ppermute | solution.py:44
  187.7 3.1 %all-to-all-done.1 = bf16[4,1024,128]{2,1,0:T(8,128)(2,1)S(1)} async-done(((bf16[4,1024,128]{2,1,0:T(8,128)(2,1)}), bf16[4,1024,128]{2,1,0:T(8,128)(2,1)S(1)}, u32[]{:S(2)}, u32[]{:S(2)}) %all-to-all-start.1) | async-done | bytes 1048608 | tf_op jit(solution)/shard_map/all_to_all | solution.py:294
  190.8 1.8 copy.72
  192.6 0.6 collective-permute-done.17
  193.1 2.8 %collective-permute-done.19 = bf16[2,1024,128]{2,1,0:T(8,128)(2,1)} collective-permute-done((bf16[2,1024,128]{2,1,0:T(8,128)(2,1)}, bf16[2,1024,128]{2,1,0:T(8,128)(2,1)}, u32[]{:S(2)}, u32[]{:S(2)}) %collective-permute-start.19) | collective-permute-done | bytes 524320 | tf_op jit(solution)/shard_map/ppermute | solution.py:44
  195.9 5.5 %collective-permute-done.18 = bf16[2,1024,128]{2,1,0:T(8,128)(2,1)} collective-permute-done((bf16[2,1024,128]{2,1,0:T(8,128)(2,1)}, bf16[2,1024,128]{2,1,0:T(8,128)(2,1)}, u32[]{:S(2)}, u32[]{:S(2)}) %collective-permute-start.18) | collective-permute-done | bytes 524320 | tf_op jit(solution)/shard_map/ppermute | solution.py:44
  201.4 2.7 %fusion.14 = (bf16[1024,1,128]{2,0,1:T(8,128)(2,1)}, bf16[1024,1,128]{2,0,1:T(8,128)(2,1)}) fusion(f32[1024,128]{1,0:T(8,128)S(1)} %copy-done.9, f32[1,2,1024,128]{3,2,1,0:T(8,128)S(1)} %get-tuple-element.53, bf16[2,1024,128]{2,1,0:T(8,128)(2,1)} %collective-permute-done.23, bf16[2,1024,128]{2,1,0:T(8,128)(2,1)} %collective-permute-done.19, ...), kind=kLoop, calls=%fused_computation.28 | loop fusion | flops 2752512 | bytes 4718592 | tf_op jit(solution)/shard_map/broadcast_in_dim | solution.py:371
  (70 shorter events, 0.6 us)
Async XLA Ops:
  0.6 4.0 %copy-start = (bf16[1024,4,1,128]{3,1,2,0:T(4,128)(2,1)S(1)}, bf16[1024,4,1,128]{3,1,2,0:T(4,128)(2,1)}, u32[]{:S(2)}) copy-start(bf16[1024,4,1,128]{3,1,2,0:T(4,128)(2,1)} %param.10) | copy-start | bytes 3145732
  0.6 4.0 %copy-start.7 = (bf16[1024,4,1,128]{3,1,2,0:T(4,128)(2,1)S(1)}, bf16[1024,4,1,128]{3,1,2,0:T(4,128)(2,1)}, u32[]{:S(2)}) copy-start(bf16[1024,4,1,128]{3,1,2,0:T(4,128)(2,1)} %param.7) | copy-start | bytes 3145732
  6.4 30.5 %copy-start.11 = (bf16[1024,4,128]{2,1,0:T(4,128)(2,1)S(1)}, bf16[1024,4,128]{2,1,0:T(4,128)(2,1)}, u32[]{:S(2)}) copy-start(bf16[1024,4,128]{2,1,0:T(4,128)(2,1)} %param.9) | copy-start | bytes 3145732
  6.4 30.4 %all-to-all-start = ((bf16[4,2096,128]{2,1,0:T(8,128)(2,1)}), bf16[4,2096,128]{2,1,0:T(8,128)(2,1)S(1)}, u32[]{:S(2)}, u32[]{:S(2)}) async-start(bf16[4,2096,128]{2,1,0:T(8,128)(2,1)} %pad_maximum_fusion), calls=%async_computation | async-start | bytes 4292608 | tf_op jit(solution)/shard_map/all_to_all | solution.py:294
  36.9 28.4 %copy-start.1 = (bf16[4,2096,128]{2,1,0:T(8,128)(2,1)}, bf16[4,2096,128]{2,1,0:T(8,128)(2,1)S(1)}, u32[]{:S(2)}) copy-start(bf16[4,2096,128]{2,1,0:T(8,128)(2,1)S(1)} %all-to-all-done.q_ref.g_ref.refs_0_.refs_1_) | copy-start | bytes 6438916
  36.9 45.7 %collective-permute-start.1 = (bf16[4,2096,128]{2,1,0:T(8,128)(2,1)S(1)}, bf16[4,2096,128]{2,1,0:T(8,128)(2,1)}, u32[]{:S(2)}, u32[]{:S(2)}) collective-permute-start(bf16[4,2096,128]{2,1,0:T(8,128)(2,1)S(1)} %all-to-all-done.q_ref.g_ref.refs_0_.refs_1_), channel_id=1, source_target_pairs={{0,4},{4,0},{8,12},{12,8},{16,20},{20,16},{24,28},{28,24},{32,36},... | collective-permute-start | bytes 6438920 | tf_op jit(solution)/shard_map/ppermute | solution.py:48
  40.0 6.2 %copy-start.12 = (s32[8,3]{0,1:T(4,128)S(1)}, s32[8,3]{0,1:T(4,128)}, u32[]{:S(2)}) copy-start(s32[8,3]{0,1:T(4,128)} %param.13) | copy-start | bytes 292
  40.0 20.7 %copy-start.5 = (bf16[1024,1,128]{2,0,1:T(8,128)(2,1)}, bf16[1024,1,128]{2,0,1:T(8,128)(2,1)S(1)}, u32[]{:S(2)}) copy-start(bf16[1024,1,128]{2,0,1:T(8,128)(2,1)S(1)} %copy.104) | copy-start | bytes 786436
  40.1 20.6 %copy-start.6 = (bf16[1024,1,128]{2,0,1:T(8,128)(2,1)}, bf16[1024,1,128]{2,0,1:T(8,128)(2,1)S(1)}, u32[]{:S(2)}) copy-start(bf16[1024,1,128]{2,0,1:T(8,128)(2,1)S(1)} %copy.105) | copy-start | bytes 786436
  41.2 15.4 %collective-permute-start.5 = (bf16[2,1024,128]{2,1,0:T(8,128)(2,1)}, bf16[2,1024,128]{2,1,0:T(8,128)(2,1)S(1)}, u32[]{:S(2)}, u32[]{:S(2)}) collective-permute-start(bf16[2,1024,128]{2,1,0:T(8,128)(2,1)} %get-tuple-element.56), channel_id=1, source_target_pairs={{0,96},{4,28},{8,104},{12,4},{16,112},{20,12},{24,120},{28,20},{32... | collective-permute-start | bytes 1572872 | tf_op jit(solution)/shard_map/ppermute | solution.py:44
  43.9 16.7 %collective-permute-start.4 = (bf16[2,1024,128]{2,1,0:T(8,128)(2,1)}, bf16[2,1024,128]{2,1,0:T(8,128)(2,1)S(1)}, u32[]{:S(2)}, u32[]{:S(2)}) collective-permute-start(bf16[2,1024,128]{2,1,0:T(8,128)(2,1)} %get-tuple-element.56), channel_id=1, source_target_pairs={{0,32},{4,12},{8,40},{12,20},{16,48},{20,28},{24,56},{28,4},{32,64... | collective-permute-start | bytes 1572872 | tf_op jit(solution)/shard_map/ppermute | solution.py:44
  43.9 21.3 %collective-permute-start.8 = (bf16[2,1024,128]{2,1,0:T(8,128)(2,1)}, bf16[2,1024,128]{2,1,0:T(8,128)(2,1)}, u32[]{:S(2)}, u32[]{:S(2)}) collective-permute-start(bf16[2,1024,128]{2,1,0:T(8,128)(2,1)} %get-tuple-element.56), channel_id=1, source_target_pairs={{0,64},{4,20},{8,72},{12,28},{16,80},{20,4},{24,88},{28,12},{32,96... | collective-permute-start | bytes 1572872 | tf_op jit(solution)/shard_map/ppermute | solution.py:44
  46.2 18.2 %collective-permute-start = (s32[8,3]{0,1:T(4,128)S(1)}, s32[8,3]{0,1:T(4,128)S(1)}, u32[]{:S(2)}, u32[]{:S(2)}) collective-permute-start(s32[8,3]{0,1:T(4,128)S(1)} %copy-done.12), channel_id=1, source_target_pairs={{0,4},{4,0},{8,12},{12,8},{16,20},{20,16},{24,28},{28,24},{32,36},... | collective-permute-start | bytes 296 | tf_op jit(solution)/shard_map/ppermute | solution.py:48
  56.6 11.1 %collective-permute-start.12 = (bf16[1,2,1024,128]{3,2,1,0:T(8,128)(2,1)}, bf16[1,2,1024,128]{3,2,1,0:T(8,128)(2,1)}, u32[]{:S(2)}, u32[]{:S(2)}) collective-permute-start(bf16[1,2,1024,128]{3,2,1,0:T(8,128)(2,1)} %get-tuple-element.57.refs_9_), channel_id=1, source_target_pairs={{0,24},{4,100},{8,0},{12,108},{16,8},{20,116},{24,16},{28,124},{32... | collective-permute-start | bytes 1572872 | tf_op jit(solution)/shard_map/ppermute | solution.py:44
  60.7 42.2 %copy-start.4 = (bf16[2,2,1024,128]{3,2,1,0:T(8,128)(2,1)}, bf16[2,2,1024,128]{3,2,1,0:T(8,128)(2,1)S(1)}, u32[]{:S(2)}) copy-start(bf16[2,2,1024,128]{3,2,1,0:T(8,128)(2,1)S(1)} %pad_maximum_fusion.1.refs_10_) | copy-start | bytes 3145732
  60.7 18.0 %collective-permute-start.6 = (bf16[2,2,1024,128]{3,2,1,0:T(8,128)(2,1)S(1)}, bf16[2,2,1024,128]{3,2,1,0:T(8,128)(2,1)}, u32[]{:S(2)}, u32[]{:S(2)}) collective-permute-start(bf16[2,2,1024,128]{3,2,1,0:T(8,128)(2,1)S(1)} %pad_maximum_fusion.1.refs_10_), channel_id=1, source_target_pairs={{0,24},{4,100},{8,0},{12,108},{16,8},{20,116},{24,16},{28,124},{32... | collective-permute-start | bytes 3145736 | tf_op jit(solution)/shard_map/ppermute | solution.py:44
  64.4 28.1 %collective-permute-start.11 = (bf16[2,2,1024,128]{3,2,1,0:T(8,128)(2,1)S(1)}, bf16[2,2,1024,128]{3,2,1,0:T(8,128)(2,1)}, u32[]{:S(2)}, u32[]{:S(2)}) collective-permute-start(bf16[2,2,1024,128]{3,2,1,0:T(8,128)(2,1)S(1)} %pad_maximum_fusion.1.refs_10_), channel_id=1, source_target_pairs={{0,8},{4,36},{8,16},{12,44},{16,24},{20,52},{24,0},{28,60},{32,40}... | collective-permute-start | bytes 3145736 | tf_op jit(solution)/shard_map/ppermute | solution.py:44
  65.2 21.0 %collective-permute-start.2 = (bf16[1,2,1024,128]{3,2,1,0:T(8,128)(2,1)}, bf16[1,2,1024,128]{3,2,1,0:T(8,128)(2,1)}, u32[]{:S(2)}, u32[]{:S(2)}) collective-permute-start(bf16[1,2,1024,128]{3,2,1,0:T(8,128)(2,1)} %get-tuple-element.57.refs_9_), channel_id=1, source_target_pairs={{0,8},{4,36},{8,16},{12,44},{16,24},{20,52},{24,0},{28,60},{32,40}... | collective-permute-start | bytes 1572872 | tf_op jit(solution)/shard_map/ppermute | solution.py:44
  67.6 24.2 %collective-permute-start.9 = (bf16[1,2,1024,128]{3,2,1,0:T(8,128)(2,1)}, bf16[1,2,1024,128]{3,2,1,0:T(8,128)(2,1)}, u32[]{:S(2)}, u32[]{:S(2)}) collective-permute-start(bf16[1,2,1024,128]{3,2,1,0:T(8,128)(2,1)} %bitcast.24.refs_11_), channel_id=1, source_target_pairs={{0,8},{4,36},{8,16},{12,44},{16,24},{20,52},{24,0},{28,60},{32,40}... | collective-permute-start | bytes 1572872 | tf_op jit(solution)/shard_map/ppermute | solution.py:44
  78.8 13.8 %collective-permute-start.13 = (bf16[1,2,1024,128]{3,2,1,0:T(8,128)(2,1)}, bf16[1,2,1024,128]{3,2,1,0:T(8,128)(2,1)}, u32[]{:S(2)}, u32[]{:S(2)}) collective-permute-start(bf16[1,2,1024,128]{3,2,1,0:T(8,128)(2,1)} %bitcast.24.refs_11_), channel_id=1, source_target_pairs={{0,24},{4,100},{8,0},{12,108},{16,8},{20,116},{24,16},{28,124},{32... | collective-permute-start | bytes 1572872 | tf_op jit(solution)/shard_map/ppermute | solution.py:44
  82.6 29.6 %collective-permute-start.7 = (bf16[2,2,1024,128]{3,2,1,0:T(8,128)(2,1)}, bf16[2,2,1024,128]{3,2,1,0:T(8,128)(2,1)S(1)}, u32[]{:S(2)}, u32[]{:S(2)}) collective-permute-start(bf16[2,2,1024,128]{3,2,1,0:T(8,128)(2,1)} %collective-permute-done.6.refs_10_), channel_id=1, source_target_pairs={{0,24},{4,100},{8,0},{12,108},{16,8},{20,116},{24,16},{28,124},{32... | collective-permute-start | bytes 3145736 | tf_op jit(solution)/shard_map/ppermute | solution.py:44
  86.2 25.9 %collective-permute-start.3 = (bf16[1,2,1024,128]{3,2,1,0:T(8,128)(2,1)}, bf16[1,2,1024,128]{3,2,1,0:T(8,128)(2,1)S(1)}, u32[]{:S(2)}, u32[]{:S(2)}) collective-permute-start(bf16[1,2,1024,128]{3,2,1,0:T(8,128)(2,1)} %collective-permute-done.2.refs_6_), channel_id=1, source_target_pairs={{0,8},{4,36},{8,16},{12,44},{16,24},{20,52},{24,0},{28,60},{32,40}... | collective-permute-start | bytes 1572872 | tf_op jit(solution)/shard_map/ppermute | solution.py:44
  91.8 20.3 %collective-permute-start.10 = (bf16[1,2,1024,128]{3,2,1,0:T(8,128)(2,1)}, bf16[1,2,1024,128]{3,2,1,0:T(8,128)(2,1)}, u32[]{:S(2)}, u32[]{:S(2)}) collective-permute-start(bf16[1,2,1024,128]{3,2,1,0:T(8,128)(2,1)} %collective-permute-done.9.refs_8_), channel_id=1, source_target_pairs={{0,8},{4,36},{8,16},{12,44},{16,24},{20,52},{24,0},{28,60},{32,40}... | collective-permute-start | bytes 1572872 | tf_op jit(solution)/shard_map/ppermute | solution.py:44
  102.9 75.5 %collective-permute-start.15 = (bf16[4,2,1024,128]{3,2,1,0:T(8,128)(2,1)}, bf16[4,2,1024,128]{3,2,1,0:T(8,128)(2,1)}, u32[]{:S(2)}, u32[]{:S(2)}) collective-permute-start(bf16[4,2,1024,128]{3,2,1,0:T(8,128)(2,1)} %get-tuple-element.23), channel_id=1, source_target_pairs={{0,24},{4,100},{8,0},{12,108},{16,8},{20,116},{24,16},{28,124},{32... | collective-permute-start | bytes 6291464 | tf_op jit(solution)/shard_map/ppermute | solution.py:44
  112.1 66.3 %collective-permute-start.16 = (bf16[4,2,1024,128]{3,2,1,0:T(8,128)(2,1)}, bf16[4,2,1024,128]{3,2,1,0:T(8,128)(2,1)}, u32[]{:S(2)}, u32[]{:S(2)}) collective-permute-start(bf16[4,2,1024,128]{3,2,1,0:T(8,128)(2,1)} %get-tuple-element.24), channel_id=1, source_target_pairs={{0,8},{4,36},{8,16},{12,44},{16,24},{20,52},{24,0},{28,60},{32,40}... | collective-permute-start | bytes 6291464 | tf_op jit(solution)/shard_map/ppermute | solution.py:44
  112.1 0.8 copy-start.14
  112.1 1.1 copy-start.13
  125.9 27.5 %collective-permute-start.20 = (bf16[2,1024,128]{2,1,0:T(8,128)(2,1)}, bf16[2,1024,128]{2,1,0:T(8,128)(2,1)S(1)}, u32[]{:S(2)}, u32[]{:S(2)}) collective-permute-start(bf16[2,1024,128]{2,1,0:T(8,128)(2,1)} %bitcast.109), channel_id=1, source_target_pairs={{0,96},{4,28},{8,104},{12,4},{16,112},{20,12},{24,120},{28,20},{32... | collective-permute-start | bytes 1572872 | tf_op jit(solution)/shard_map/ppermute | solution.py:44
  146.4 25.6 %collective-permute-start.14 = (bf16[4,1024,128]{2,1,0:T(8,128)(2,1)}, bf16[4,1024,128]{2,1,0:T(8,128)(2,1)S(1)}, u32[]{:S(2)}, u32[]{:S(2)}) collective-permute-start(bf16[4,1024,128]{2,1,0:T(8,128)(2,1)} %get-tuple-element.21), channel_id=1, source_target_pairs={{0,4},{4,0},{8,12},{12,8},{16,20},{20,16},{24,28},{28,24},{32,36},... | collective-permute-start | bytes 3145736 | tf_op jit(solution)/shard_map/ppermute | solution.py:48
  146.4 22.5 %collective-permute-start.21 = (bf16[2,1024,128]{2,1,0:T(8,128)(2,1)}, bf16[2,1024,128]{2,1,0:T(8,128)(2,1)S(1)}, u32[]{:S(2)}, u32[]{:S(2)}) collective-permute-start(bf16[2,1024,128]{2,1,0:T(8,128)(2,1)} %bitcast.108), channel_id=1, source_target_pairs={{0,32},{4,12},{8,40},{12,20},{16,48},{20,28},{24,56},{28,4},{32,64... | collective-permute-start | bytes 1572872 | tf_op jit(solution)/shard_map/ppermute | solution.py:44
  153.4 15.5 %collective-permute-start.22 = (bf16[2,1024,128]{2,1,0:T(8,128)(2,1)}, bf16[2,1024,128]{2,1,0:T(8,128)(2,1)}, u32[]{:S(2)}, u32[]{:S(2)}) collective-permute-start(bf16[2,1024,128]{2,1,0:T(8,128)(2,1)} %bitcast.107), channel_id=1, source_target_pairs={{0,64},{4,20},{8,72},{12,28},{16,80},{20,4},{24,88},{28,12},{32,96... | collective-permute-start | bytes 1572872 | tf_op jit(solution)/shard_map/ppermute | solution.py:44
  155.2 13.7 %copy-start.10 = (bf16[1,2,1024,128]{3,2,1,0:T(8,128)(2,1)S(1)}, bf16[1,2,1024,128]{3,2,1,0:T(8,128)(2,1)}, u32[]{:S(2)}) copy-start(bf16[1,2,1024,128]{3,2,1,0:T(8,128)(2,1)} %get-tuple-element.25) | copy-start | bytes 1572868
  155.2 16.8 %copy-start.3 = (bf16[4,1024,128]{2,1,0:T(8,128)(2,1)S(1)}, bf16[4,1024,128]{2,1,0:T(8,128)(2,1)}, u32[]{:S(2)}) copy-start(bf16[4,1024,128]{2,1,0:T(8,128)(2,1)} %get-tuple-element.20) | copy-start | bytes 3145732
  168.9 3.1 %copy-start.2 = (f32[4,1024,128]{2,1,0:T(8,128)S(1)}, f32[4,1024,128]{2,1,0:T(8,128)}, u32[]{:S(2)}) copy-start(f32[4,1024,128]{2,1,0:T(8,128)} %get-tuple-element.17) | copy-start | bytes 6291460
  171.2 21.3 %collective-permute-start.23 = (bf16[2,1024,128]{2,1,0:T(8,128)(2,1)}, bf16[2,1024,128]{2,1,0:T(8,128)(2,1)}, u32[]{:S(2)}, u32[]{:S(2)}) collective-permute-start(bf16[2,1024,128]{2,1,0:T(8,128)(2,1)} %fusion.2), channel_id=1, source_target_pairs={{0,16},{4,68},{8,24},{12,76},{16,0},{20,84},{24,8},{28,92},{32,48}... | collective-permute-start | bytes 1572872 | tf_op jit(solution)/shard_map/ppermute | solution.py:44
  173.5 17.3 %all-to-all-start.1 = ((bf16[4,1024,128]{2,1,0:T(8,128)(2,1)}), bf16[4,1024,128]{2,1,0:T(8,128)(2,1)S(1)}, u32[]{:S(2)}, u32[]{:S(2)}) async-start(bf16[4,1024,128]{2,1,0:T(8,128)(2,1)} %multiply_convert_fusion), calls=%async_computation.1 | async-start | bytes 2097152 | tf_op jit(solution)/shard_map/all_to_all | solution.py:294
  182.9 18.5 %copy-start.8 = (f32[1024,128]{1,0:T(8,128)S(1)}, f32[1024,128]{1,0:T(8,128)}, u32[]{:S(2)}) copy-start(f32[1024,128]{1,0:T(8,128)} %get-tuple-element.29) | copy-start | bytes 1572868
  182.9 18.5 %copy-start.9 = (f32[1024,128]{1,0:T(8,128)S(1)}, f32[1024,128]{1,0:T(8,128)}, u32[]{:S(2)}) copy-start(f32[1024,128]{1,0:T(8,128)} %get-tuple-element.30) | copy-start | bytes 1572868
  182.9 10.2 %collective-permute-start.17 = (bf16[2,1024,128]{2,1,0:T(8,128)(2,1)}, bf16[2,1024,128]{2,1,0:T(8,128)(2,1)}, u32[]{:S(2)}, u32[]{:S(2)}) collective-permute-start(bf16[2,1024,128]{2,1,0:T(8,128)(2,1)} %get-tuple-element.50), channel_id=1, source_target_pairs={{0,96},{4,28},{8,104},{12,4},{16,112},{20,12},{24,120},{28,20},{32... | collective-permute-start | bytes 1572872 | tf_op jit(solution)/shard_map/ppermute | solution.py:44
  184.8 11.1 %collective-permute-start.19 = (bf16[2,1024,128]{2,1,0:T(8,128)(2,1)}, bf16[2,1024,128]{2,1,0:T(8,128)(2,1)}, u32[]{:S(2)}, u32[]{:S(2)}) collective-permute-start(bf16[2,1024,128]{2,1,0:T(8,128)(2,1)} %get-tuple-element.51), channel_id=1, source_target_pairs={{0,64},{4,20},{8,72},{12,28},{16,80},{20,4},{24,88},{28,12},{32,96... | collective-permute-start | bytes 1572872 | tf_op jit(solution)/shard_map/ppermute | solution.py:44
  187.7 13.7 %collective-permute-start.18 = (bf16[2,1024,128]{2,1,0:T(8,128)(2,1)}, bf16[2,1024,128]{2,1,0:T(8,128)(2,1)}, u32[]{:S(2)}, u32[]{:S(2)}) collective-permute-start(bf16[2,1024,128]{2,1,0:T(8,128)(2,1)} %get-tuple-element.52), channel_id=1, source_target_pairs={{0,32},{4,12},{8,40},{12,20},{16,48},{20,28},{24,56},{28,4},{32,64... | collective-permute-start | bytes 1572872 | tf_op jit(solution)/shard_map/ppermute | solution.py:44
